TPU v7x, 768 devices: a whole 4x8x12 slice. The times are simulated.
768 devices in a mesh: row: 24 (over z_lo, y), col: 32 (over z_hi, x, core).
Axes of the slice: x: 4, y: 8, z: 12 (z_hi: 4, z_lo: 3; z = z_hi * 3 + z_lo), core: 2. Of those that a mesh axis runs over, the one named last changes fastest.
Arguments:
- qkv: bfloat16 [9216, 3, 4096], P('row', None, 'col'), may hold values from -22 to 22
- out_weight: bfloat16 [4096, 8192], P(None, 'col'), may hold values from -0.09375 to 0.09375
- cotangent: bfloat16 [9216, 8192], P('row', 'col'), may hold values from -6 to 6
- scene_lengths: int32 [192], P('row'), may hold values from 8 to 328, as said below
- bucket_ids: int32 [192], P('row'), may hold values from 0 to 7
- sensor_ids: int32 [192], P('row'), may hold values from 0 to 7
- gsd_ids: int32 [192], P('row'), may hold values from 0 to 15
- step_ids: int32 [192], P('row'), may hold values from 0 to 999
- step_table: bfloat16 [1000, 8192], P(None, 'col'), may hold values from -3 to 3
- gsd_table: bfloat16 [16, 8192], P(None, 'col'), may hold values from -3 to 3
- sensor_table: bfloat16 [8, 8192], P(None, 'col'), may hold values from -3 to 3
- bucket_table: bfloat16 [8, 8192], P(None, 'col'), may hold values from -3 to 3
Outputs:
- mixed: bfloat16 [9216, 8192], P('row', 'col')
- grad_qkv: bfloat16 [9216, 3, 4096], P('row', None, 'col')
- grad_weight: bfloat16 [4096, 8192], P(None, 'col')
Inputs may be any that keep to these rules, and one draw needn't show every extreme that they name: `scene_lengths`: each block of 384 tokens holds 8 scenes whose lengths are positive multiples of 8 and sum to 384.
All inputs are finite; a program needn't handle non-finite values.
Results may differ from a plain program's by a relative error of at most 0.03.
Values may be sent and summed in bfloat16 or wider, within the bound.
No kernel may reach another device: no remote copies, remote signals or barrier semaphores. Data moves between devices by JAX's collectives and lax.ppermute only.
A program may use at most 64 MiB of HBM per device.

v0:
```python
import jax
import jax.numpy as jnp
from jax import lax
from jax.sharding import PartitionSpec as P

HEAD = 128


def scene_of(lengths, count):
    ends = jnp.cumsum(lengths)
    places = jnp.arange(count)
    return jnp.sum((places[:, None] >= ends[None, :]).astype(jnp.int32), axis=1)


def lookup(ids, table):
    picks = (ids[:, None] == jnp.arange(table.shape[0])[None, :]).astype(table.dtype)
    return jnp.dot(picks, table, preferred_element_type=jnp.float32)


def attend(queries, keys, values, same):
    factor = HEAD ** (-0.5)
    scores = jnp.einsum("the,she->hts", queries, keys, preferred_element_type=jnp.float32) * factor
    scores = jnp.where(same[None], scores, -1e30)
    top = jnp.max(scores, axis=-1, keepdims=True)
    weights = jnp.exp(scores - top)
    probs = weights / jnp.sum(weights, axis=-1, keepdims=True)
    rounded = probs.astype(jnp.bfloat16)
    output = jnp.einsum("hts,she->the", rounded, values, preferred_element_type=jnp.float32).astype(
        jnp.bfloat16
    )
    return (probs, rounded, output)


def attend_back(queries, keys, values, probs, rounded, upstream):
    factor = HEAD ** (-0.5)
    grad_values = jnp.einsum(
        "hts,the->she", rounded, upstream, preferred_element_type=jnp.float32
    ).astype(jnp.bfloat16)
    grad_probs = jnp.einsum("the,she->hts", upstream, values, preferred_element_type=jnp.float32)
    inner = jnp.sum(probs * grad_probs, axis=-1, keepdims=True)
    grad_scores = (probs * (grad_probs - inner)).astype(jnp.bfloat16)
    grad_queries = (
        jnp.einsum("hts,she->the", grad_scores, keys, preferred_element_type=jnp.float32) * factor
    ).astype(jnp.bfloat16)
    grad_keys = (
        jnp.einsum("hts,the->she", grad_scores, queries, preferred_element_type=jnp.float32)
        * factor
    ).astype(jnp.bfloat16)
    stacked = jnp.stack([grad_queries, grad_keys, grad_values], axis=1)
    return stacked.reshape(stacked.shape[0], 3, stacked.shape[2] * stacked.shape[3])


def on_device(
    qkv,
    out_weight,
    cotangent,
    scene_lengths,
    bucket_ids,
    sensor_ids,
    gsd_ids,
    step_ids,
    step_table,
    gsd_table,
    sensor_table,
    bucket_table,
):
    tok_rows = qkv.shape[0]
    local_width = qkv.shape[2]
    heads_here = local_width // HEAD
    gate_scene = lookup(step_ids, step_table) + lookup(gsd_ids, gsd_table)
    gate_scene = gate_scene + lookup(sensor_ids, sensor_table) + lookup(bucket_ids, bucket_table)
    segments = scene_of(scene_lengths, tok_rows)
    member = (segments[:, None] == jnp.arange(scene_lengths.shape[0])[None, :]).astype(jnp.float32)
    gate = jnp.dot(
        member, gate_scene, precision=lax.Precision.HIGHEST, preferred_element_type=jnp.float32
    )
    same = segments[:, None] == segments[None, :]
    block = qkv.reshape(tok_rows, 3, heads_here, HEAD)
    queries = block[:, 0]
    keys = block[:, 1]
    values = block[:, 2]
    probs, rounded, attended = attend(queries, keys, values, same)
    attended = attended.reshape(tok_rows, local_width)
    rows = out_weight
    projected = jnp.dot(
        lax.all_gather(attended, "col", axis=1, tiled=True),
        rows,
        preferred_element_type=jnp.float32,
    )
    mixed = (gate * projected).astype(jnp.bfloat16)
    gated = (gate * cotangent.astype(jnp.float32)).astype(jnp.bfloat16)
    rows = out_weight
    summed = lax.psum_scatter(
        lax.dot_general(
            rows, gated, (((1,), (1,)), ((), ())), preferred_element_type=jnp.float32
        ).astype(jnp.bfloat16),
        "col",
        scatter_dimension=0,
        tiled=True,
    )
    upstream = summed.T.reshape(tok_rows, heads_here, HEAD)
    grad_qkv = attend_back(queries, keys, values, probs, rounded, upstream)
    partial_sum = lax.dot_general(
        lax.all_gather(attended, "col", axis=1, tiled=True),
        gated,
        (((0,), (0,)), ((), ())),
        preferred_element_type=jnp.float32,
    )
    total = lax.psum(partial_sum.astype(jnp.bfloat16), "row")
    return (mixed, grad_qkv, total)


def solution(mesh):
    return jax.shard_map(
        on_device,
        mesh=mesh,
        in_specs=(
            P("row", None, "col"),
            P(None, "col"),
            P("row", "col"),
            P("row"),
            P("row"),
            P("row"),
            P("row"),
            P("row"),
            P(None, "col"),
            P(None, "col"),
            P(None, "col"),
            P(None, "col"),
        ),
        out_specs=(P("row", "col"), P("row", None, "col"), P(None, "col")),
        check_vma=False,
    )
```

profile of v0, /device:TPU:192, one launch (start us, length us, event | category | flops | bytes accessed | tf_op | source)
XLA Modules:
  0.0 491.8 jit_solution(1445822269964608687)
XLA Ops:
  7.2 0.0 copy-start
  7.3 0.0 all-gather.2.cloned.1.call-start
  7.3 1.0 reduce-window.8
  8.3 0.1 convert_reduce_fusion
  8.4 1.2 fusion.22
  9.6 0.1 fusion.9
  9.7 1.8 convolution_convert_fusion.3
  11.6 0.0 all-gather.2.cloned.1.call-update
  11.6 0.0 reduce-scatter.4.cloned.1.call-start
  11.7 0.2 fusion.15
  11.9 0.0 copy-done.9
  11.9 0.2 convolution_add_fusion.2
  12.1 0.2 convolution_add_fusion.1
  12.3 0.2 convolution_add_fusion
  12.5 0.4 fusion.10
  12.9 2.7 fusion
  15.6 4.7 copy.19
  20.3 0.0 reduce-scatter.4.cloned.1.call-update
  20.3 0.0 all-reduce.2.cloned.1.call-start
  20.3 77.6 %all-gather.2.cloned.1.call-done = bf16[384,4096]{1,0:T(8,128)(2,1)} async-done(((bf16[384,128]{1,0:T(8,128)(2,1)}), bf16[384,4096]{1,0:T(8,128)(2,1)}) %all-gather.2.cloned.1.call-update) | async-done | bytes 3145744 | tf_op jit(solution)/shard_map/all_gather | solution.py:86
  97.9 4.5 convolution_convert_fusion.1
  102.4 0.0 all-reduce.2.cloned.1.call-update
  102.5 120.1 %reduce-scatter.4.cloned.1.call-done = bf16[128,384]{1,0:T(8,128)(2,1)} async-done(((bf16[4096,384]{1,0:T(8,128)(2,1)}), bf16[128,384]{1,0:T(8,128)(2,1)}) %reduce-scatter.4.cloned.1.call-update) | async-done | bytes 98320
  222.6 1.2 multiply_reduce_fusion
  223.8 0.2 multiply_convert_fusion
  224.0 1.3 fusion.6
  225.2 1.2 fusion.7
  226.4 0.3 fusion.5
  226.7 0.7 maximum_bitcast_fusion
  227.5 1.7 fusion.2
  229.1 253.1 %all-reduce.2.cloned.1.call-done = bf16[4096,256]{1,0:T(8,128)(2,1)} async-done(((bf16[4096,256]{1,0:T(8,128)(2,1)}), bf16[4096,256]{1,0:T(8,128)(2,1)}) %all-reduce.2.cloned.1.call-update) | async-done | bytes 2097168 | tf_op jit(solution)/shard_map/psum | solution.py:109
  482.2 3.0 copy.22
  (22 shorter events, 0.0 us)
Async XLA Ops:
  7.2 5.7 %copy-start = (bf16[4096,256]{1,0:T(8,128)(2,1)S(1)}, bf16[4096,256]{1,0:T(8,128)(2,1)}, u32[]{:S(2)}) copy-start(bf16[4096,256]{1,0:T(8,128)(2,1)} %param.13) | copy-start | bytes 6291460
  7.2 4.5 copy-start.3
  7.2 4.5 copy-start.1
  7.2 4.7 copy-start.9
  7.2 4.6 copy-start.6
  7.2 4.8 copy-start.10
  7.2 4.8 copy-start.7
  7.2 5.0 %copy-start.11 = (s32[8]{0:T(128)S(1)}, s32[8]{0:T(128)}, u32[]{:S(2)}) copy-start(s32[8]{0:T(128)} %param.16) | copy-start | bytes 100
  7.3 5.0 %copy-start.8 = (bf16[8,256]{1,0:T(8,128)(2,1)S(1)}, bf16[8,256]{1,0:T(8,128)(2,1)}, u32[]{:S(2)}) copy-start(bf16[8,256]{1,0:T(8,128)(2,1)} %param.23) | copy-start | bytes 12292
  7.3 5.6 %copy-start.2 = (bf16[384,256]{1,0:T(8,128)(2,1)S(1)}, bf16[384,256]{1,0:T(8,128)(2,1)}, u32[]{:S(2)}) copy-start(bf16[384,256]{1,0:T(8,128)(2,1)} %param.14) | copy-start | bytes 589828
  7.3 90.6 %all-gather.2.cloned.1.call-start = ((), (), s32[]{:S(2)}) async-start(), calls=%async_computation.1 | async-start | bytes 3244032 | tf_op jit(solution)/shard_map/all_gather | solution.py:86
  11.6 211.0 %reduce-scatter.4.cloned.1.call-start = ((), (), s32[]{:S(2)}) async-start(), calls=%async_computation.3 | async-start | bytes 3244032
  20.3 462.0 %all-reduce.2.cloned.1.call-start = ((), (), s32[]{:S(2)}) async-start(), calls=%async_computation.2 | async-start | bytes 4194304 | tf_op jit(solution)/shard_map/psum | solution.py:109
  222.6 3.9 copy-start.5
  223.8 3.7 copy-start.4
Sparse Core Ops, SparseCore 0:
  12.3 85.5 all-gather.1
  103.0 119.5 reduce-scatter.3
  226.7 255.4 all-reduce.1
where the time goes:
time: 492 us
  waiting for transfers between devices  451 us (92%)
  matrix products  17 us (3%)
  between operations  13.9 us (3%)
  local copies, waits for them, and re-layouts  7.77 us (2%)
    psum x1, waiting for transfers between devices, on_device(): total = lax.psum(partial_sum.astype(jnp.bfloat16), 'row')  253 us
    unnamed x4, waiting for transfers between devices  120 us
    all_gather x1, waiting for transfers between devices, on_device(): lax.all_gather(attended, 'col', axis=1, tiled=True)  77.6 us
  transfers between devices with their start and end apart: 3, of which 3 were waited for; matrix products, arithmetic and copies ran while one was open for 4% of the time, Pallas kernels for 0%

commit v1 on v0

v1 whole, which is shorter than its diff:
```python
import jax
import jax.numpy as jnp
from jax import lax
from jax.sharding import Mesh, PartitionSpec as P

HEAD = 128
ROW = ("zlo", "y")
COL = ("zhi", "x", "core")
F32 = jnp.float32
BF = jnp.bfloat16


def scene_of(lengths, count):
    ends = jnp.cumsum(lengths)
    places = jnp.arange(count)
    return jnp.sum((places[:, None] >= ends[None, :]).astype(jnp.int32), axis=1)


def lookup(ids, table):
    picks = (ids[:, None] == jnp.arange(table.shape[0])[None, :]).astype(table.dtype)
    return jnp.dot(picks, table, preferred_element_type=F32)


def dot(a, b, dims):
    return lax.dot_general(a, b, (dims, ((), ())), preferred_element_type=F32)


def shift(value, axis, size, step):
    return lax.ppermute(value, axis, [(i, (i + step) % size) for i in range(size)])


def on_device(
    qkv,
    out_weight,
    cotangent,
    scene_lengths,
    bucket_ids,
    sensor_ids,
    gsd_ids,
    step_ids,
    step_table,
    gsd_table,
    sensor_table,
    bucket_table,
):
    toks = qkv.shape[0]
    width = cotangent.shape[1]
    factor = HEAD ** (-0.5)
    n_core, n_x, n_zhi = lax.axis_size("core"), lax.axis_size("x"), lax.axis_size("zhi")
    n_y, n_zlo = lax.axis_size("y"), lax.axis_size("zlo")
    core, x = lax.axis_index("core"), lax.axis_index("x")

    segments = scene_of(scene_lengths, toks)
    same = segments[:, None] == segments[None, :]
    queries, keys, values = qkv[:, 0], qkv[:, 1], qkv[:, 2]

    scores = dot(queries, keys, ((1,), (1,))) * factor
    scores = jnp.where(same, scores, -1e30)
    top = jnp.max(scores, axis=-1, keepdims=True)
    weights = jnp.exp(scores - top)
    probs = weights / jnp.sum(weights, axis=-1, keepdims=True)
    rounded = probs.astype(BF)
    attended = dot(values, rounded, ((0,), (1,))).astype(BF)

    gathered = lax.all_gather(attended, "zhi", axis=0, tiled=True)

    gate_scene = lookup(step_ids, step_table) + lookup(gsd_ids, gsd_table)
    gate_scene = gate_scene + lookup(sensor_ids, sensor_table) + lookup(bucket_ids, bucket_table)
    member = (segments[:, None] == jnp.arange(scene_lengths.shape[0])[None, :]).astype(F32)
    gate = jnp.dot(member, gate_scene, precision=lax.Precision.HIGHEST, preferred_element_type=F32)
    gated = (gate * cotangent.astype(F32)).astype(BF)

    weight = out_weight.reshape(n_zhi, n_x, n_core, HEAD, width)
    weight = weight.transpose(2, 1, 0, 3, 4).reshape(n_core, n_x * n_zhi * HEAD, width)

    theirs = lax.dynamic_index_in_dim(weight, 1 - core, 0, keepdims=False)
    mine = lax.dynamic_index_in_dim(weight, core, 0, keepdims=False)
    sent = dot(theirs, gated, ((1,), (1,))).astype(BF)
    got = shift(sent, "core", n_core, 1)
    summed = (dot(mine, gated, ((1,), (1,))) + got.astype(F32)).astype(BF)
    summed = lax.psum_scatter(summed, "x", scatter_dimension=0, tiled=True)
    summed = lax.psum_scatter(summed, "zhi", scatter_dimension=0, tiled=True)

    pieces = [gathered] + [shift(gathered, "x", n_x, s) for s in range(1, n_x)]
    stacked = jnp.stack(pieces)
    order = jnp.mod(x - jnp.arange(n_x), n_x)
    del order
    ring = jnp.concatenate([stacked, stacked])
    ring = jnp.flip(ring, 0)
    ring = lax.dynamic_slice_in_dim(ring, n_x - 1 - x, n_x, 0)
    half = ring.reshape(n_x * n_zhi * HEAD, toks)
    other = shift(half, "core", n_core, 1)
    first = jnp.where(core == 0, half, other)
    second = jnp.where(core == 0, other, half)
    heads = jnp.concatenate([first, second])

    partial_sum = dot(heads, gated, ((1,), (0,))).astype(BF)
    spread = lax.all_to_all(partial_sum, "y", split_axis=0, concat_axis=0, tiled=True)
    spread = spread.reshape(n_y, -1, width).astype(F32).sum(0).astype(BF)
    total = spread.astype(F32)
    for s in range(1, n_zlo):
        total = total + shift(spread, "zlo", n_zlo, s).astype(F32)
    total = lax.all_gather(total.astype(BF), "y", axis=0, tiled=True)
    total = total.reshape(n_core, n_x, n_zhi, HEAD, width).transpose(2, 1, 0, 3, 4)
    total = total.reshape(-1, width)

    projected = dot(heads, weight.reshape(-1, width), ((0,), (0,)))
    mixed = (gate * projected).astype(BF)

    upstream = summed.T
    grad_values = dot(rounded, upstream, ((0,), (0,))).astype(BF)
    grad_probs = dot(upstream, values, ((1,), (1,)))
    inner = jnp.sum(probs * grad_probs, axis=-1, keepdims=True)
    grad_scores = (probs * (grad_probs - inner)).astype(BF)
    grad_queries = (dot(grad_scores, keys, ((1,), (0,))) * factor).astype(BF)
    grad_keys = (dot(grad_scores, queries, ((0,), (0,))) * factor).astype(BF)
    grad_qkv = jnp.stack([grad_queries, grad_keys, grad_values], axis=1)
    return (mixed, grad_qkv, total)


def solution(mesh):
    fine = Mesh(mesh.devices.reshape(3, 8, 4, 4, 2), ROW + COL)
    return jax.shard_map(
        on_device,
        mesh=fine,
        in_specs=(
            P(ROW, None, COL),
            P(None, COL),
            P(ROW, COL),
            P(ROW),
            P(ROW),
            P(ROW),
            P(ROW),
            P(ROW),
            P(None, COL),
            P(None, COL),
            P(None, COL),
            P(None, COL),
        ),
        out_specs=(P(ROW, COL), P(ROW, None, COL), P(None, COL)),
        check_vma=False,
    )
```

time: 492 us -> 241 us (0.49)
  the two profiles are of different devices: /device:TPU:192 before, /device:TPU:2 now
where the time goes in v1:
time: 241 us; the launch traced here: 240 us
  waiting for transfers between devices  112 us (46%)
  blocking collectives  34.1 us (14%)
  starting transfers between devices  28.8 us (12%)
  local copies, waits for them, and re-layouts  24.3 us (10%)
  matrix products  17.9 us (7%)
  between operations  15.8 us (7%)
  other arithmetic  6.94 us (3%)
    all_gather x1, waiting for transfers between devices, on_device(): total = lax.all_gather(total.astype(BF), 'y', axis=0, tiled=True)  37.1 us
    all_gather x1, blocking collectives, on_device(): gathered = lax.all_gather(attended, 'zhi', axis=0, tiled=True)  34.1 us
    reduce_scatter x1, waiting for transfers between devices, on_device(): summed = lax.psum_scatter(summed, 'x', scatter_dimension=0, tiled=True)  33.7 us
    ppermute x7, waiting for transfers between devices, shift(): lax.ppermute(value, axis, [(i, (i + step) % size) for i in range(size)])  27.1 us
    ppermute x7, starting transfers between devices, shift(): lax.ppermute(value, axis, [(i, (i + step) % size) for i in range(size)])  21.6 us
    dot_general x10, matrix products, dot(): return lax.dot_general(a, b, (dims, ((), ())), preferred_element_type=F32)  16 us
    all_to_all x1, waiting for transfers between devices, on_device(): lax.all_to_all(partial_sum, 'y', split_axis=0, concat_axis=0, tiled=True)  14.3 us
    unnamed x37, local copies, waits for them, and re-layouts  9.46 us
  transfers between devices with their start and end apart: 11, of which 6 were waited for; matrix products, arithmetic and copies ran while one was open for 11% of the time, Pallas kernels for 0%

profile of v1, /device:TPU:2, one launch (start us, length us, event | category | flops | bytes accessed | tf_op | source)
XLA Modules:
  0.0 240.1 jit_solution(11890260987262043309)
XLA Ops:
  9.0 1.2 fusion.47
  10.3 1.3 fusion.6
  11.7 34.1 %all_gather.6 = bf16[512,384]{0,1:T(8,128)(2,1)S(1)} all-gather(bf16[128,384]{0,1:T(8,128)(2,1)S(1)} %fusion.6), channel_id=1, replica_groups=mesh['zlo'=3,'y'=8,'zhi'=4,'x'=4,'core'=2] {'zhi'}, dimensions={0}, use_global_device_ids=true | all-gather | bytes 491520 | tf_op jit(solution)/shard_map/all_gather | solution.py:65
  45.8 2.4 collective-permute-start.2
  48.2 4.3 %collective-permute-start.1 = (bf16[512,384]{0,1:T(8,128)(2,1)S(1)}, bf16[512,384]{0,1:T(8,128)(2,1)}, u32[]{:S(2)}, u32[]{:S(2)}) collective-permute-start(bf16[512,384]{0,1:T(8,128)(2,1)S(1)} %all_gather.6), channel_id=1, source_target_pairs={{0,4},{2,6},{4,0},{6,2},{1,5},{3,7},{5,1},{7,3},{8,12},{10,14},{12... | collective-permute-start | bytes 1179656 | tf_op jit(solution)/shard_map/ppermute | solution.py:29
  52.5 3.7 %collective-permute-start = (bf16[512,384]{0,1:T(8,128)(2,1)S(1)}, bf16[512,384]{0,1:T(8,128)(2,1)}, u32[]{:S(2)}, u32[]{:S(2)}) collective-permute-start(bf16[512,384]{0,1:T(8,128)(2,1)S(1)} %all_gather.6), channel_id=1, source_target_pairs={{0,2},{2,4},{4,6},{6,0},{1,3},{3,5},{5,7},{7,1},{8,10},{10,12},{12... | collective-permute-start | bytes 1179656 | tf_op jit(solution)/shard_map/ppermute | solution.py:29
  57.0 1.8 copy.21
  59.2 10.5 %collective-permute-done = bf16[512,384]{0,1:T(8,128)(2,1)} collective-permute-done((bf16[512,384]{0,1:T(8,128)(2,1)S(1)}, bf16[512,384]{0,1:T(8,128)(2,1)}, u32[]{:S(2)}, u32[]{:S(2)}) %collective-permute-start) | collective-permute-done | bytes 393248 | tf_op jit(solution)/shard_map/ppermute | solution.py:29
  69.7 1.8 bitcast_dynamic-update-slice_fusion.4
  71.5 1.8 bitcast_dynamic-update-slice_fusion.2
  74.8 1.8 bitcast_dynamic-update-slice_fusion.5
  76.6 1.8 bitcast_dynamic-update-slice_fusion.3
  79.1 3.8 %rev.4 = bf16[8,512,384]{1,2,0:T(8,128)(2,1)} reverse(bf16[8,512,384]{1,2,0:T(8,128)(2,1)} %bitcast_dynamic-update-slice_fusion.1), dimensions={0} | reverse | bytes 6291456 | tf_op jit(solution)/shard_map/jit(_flip)/rev | solution.py:89
  82.9 2.7 %constant_dynamic-slice_fusion = bf16[4,512,384]{1,2,0:T(8,128)(2,1)} fusion(bf16[8,512,384]{1,2,0:T(8,128)(2,1)} %rev.4, s32[]{:T(128)S(6)} %select_n.28), kind=kLoop, calls=%fused_computation.76 | loop fusion | bytes 3145732 | tf_op jit(solution)/shard_map/dynamic_slice | solution.py:90
  85.6 2.6 %copy.20 = bf16[4,512,384]{2,1,0:T(8,128)(2,1)} copy(bf16[4,512,384]{1,2,0:T(8,128)(2,1)} %constant_dynamic-slice_fusion) | data formatting | bytes 3145728 | tf_op jit(solution)/shard_map/dynamic_slice | solution.py:90
  88.3 1.9 collective-permute-start.3
  91.7 1.9 convolution_convert_fusion.1
  93.6 2.4 collective-permute-start.4
  96.0 2.2 broadcast_select_fusion.1
  98.2 2.6 %convolution_convert_fusion = bf16[4096,256]{1,0:T(8,128)(2,1)} fusion(bf16[384,256]{1,0:T(8,128)(2,1)S(1)} %get-tuple-element.7, bf16[2048,384]{1,0:T(8,128)(2,1)S(1)} %get-tuple-element.4, bf16[2048,384]{1,0:T(8,128)(2,1)S(1)} %get-tuple-element.3), kind=kOutput, calls=%fused_computation | convolution fusion | flops 812646400 | bytes 5439488 | tf_op jit(solution)/shard_map/dot_general | solution.py:25
  100.8 7.0 %all-to-all-start = ((bf16[8,512,256]{2,1,0:T(8,128)(2,1)}), bf16[8,512,256]{2,1,0:T(8,128)(2,1)}, u32[]{:S(2)}, u32[]{:S(2)}) async-start(bf16[8,512,256]{2,1,0:T(8,128)(2,1)} %bitcast.82), calls=%async_computation.2 | async-start | bytes 4194304 | tf_op jit(solution)/shard_map/all_to_all | solution.py:98
  107.9 3.3 %add_convert_fusion = bf16[2048,384]{1,0:T(8,128)(2,1)} fusion(bf16[2048,384]{1,0:T(8,128)(2,1)} %collective-permute-done.4, bf16[384,256]{1,0:T(8,128)(2,1)S(1)} %get-tuple-element.7, bf16[2,2048,256]{2,1,0:T(8,128)(2,1)S(1)} %bitcast.78, s32[]{:T(128)S(6)} %select_n.31), kind=kOutput, calls=%fused_computation.2 | convolution fusion | flops 405012480 | bytes 4390916 | tf_op jit(solution)/shard_map/dot_general | solution.py:25
  111.3 33.7 %reduce-scatter.3.cloned.1.call-done = bf16[512,384]{1,0:T(8,128)(2,1)} async-done(((bf16[2048,384]{1,0:T(8,128)(2,1)}), bf16[512,384]{1,0:T(8,128)(2,1)}) %reduce-scatter.3.cloned.1.call-update) | async-done | bytes 393232 | tf_op jit(solution)/shard_map/reduce_scatter | solution.py:81
  145.1 14.3 %all-to-all-done = bf16[8,512,256]{2,1,0:T(8,128)(2,1)} async-done(((bf16[8,512,256]{2,1,0:T(8,128)(2,1)}), bf16[8,512,256]{2,1,0:T(8,128)(2,1)}, u32[]{:S(2)}, u32[]{:S(2)}) %all-to-all-start) | async-done | bytes 2097184 | tf_op jit(solution)/shard_map/all_to_all | solution.py:98
  159.4 2.0 reduce_sum.42
  161.3 3.0 %collective-permute-start.6 = (bf16[512,256]{1,0:T(8,128)(2,1)S(1)}, bf16[512,256]{1,0:T(8,128)(2,1)S(1)}, u32[]{:S(2)}, u32[]{:S(2)}) collective-permute-start(bf16[512,256]{1,0:T(8,128)(2,1)S(1)} %reduce_sum.42), channel_id=1, source_target_pairs={{0,512},{256,0},{512,256},{1,513},{257,1},{513,257},{2,514},{258,2... | collective-permute-start | bytes 786440 | tf_op jit(solution)/shard_map/ppermute | solution.py:29
  164.3 4.0 %collective-permute-start.5 = (bf16[512,256]{1,0:T(8,128)(2,1)S(1)}, bf16[512,256]{1,0:T(8,128)(2,1)S(1)}, u32[]{:S(2)}, u32[]{:S(2)}) collective-permute-start(bf16[512,256]{1,0:T(8,128)(2,1)S(1)} %reduce_sum.42), channel_id=1, source_target_pairs={{0,256},{256,512},{512,0},{1,257},{257,513},{513,1},{2,258},{258,5... | collective-permute-start | bytes 786440 | tf_op jit(solution)/shard_map/ppermute | solution.py:29
  168.3 10.3 %collective-permute-done.6 = bf16[512,256]{1,0:T(8,128)(2,1)S(1)} collective-permute-done((bf16[512,256]{1,0:T(8,128)(2,1)S(1)}, bf16[512,256]{1,0:T(8,128)(2,1)S(1)}, u32[]{:S(2)}, u32[]{:S(2)}) %collective-permute-start.6) | collective-permute-done | bytes 262176 | tf_op jit(solution)/shard_map/ppermute | solution.py:29
  178.6 6.3 %collective-permute-done.5 = bf16[512,256]{1,0:T(8,128)(2,1)S(1)} collective-permute-done((bf16[512,256]{1,0:T(8,128)(2,1)S(1)}, bf16[512,256]{1,0:T(8,128)(2,1)S(1)}, u32[]{:S(2)}, u32[]{:S(2)}) %collective-permute-start.5) | collective-permute-done | bytes 262176 | tf_op jit(solution)/shard_map/ppermute | solution.py:29
  185.7 3.8 %fusion.3 = bf16[384,256]{1,0:T(8,128)(2,1)} fusion(f32[384,256]{1,0:T(8,128)} %get-tuple-element.8, bf16[4096,256]{1,0:T(8,128)(2,1)S(1)} %bitcast.79, bf16[2048,384]{1,0:T(8,128)(2,1)} %copy-done.4, bf16[2048,384]{1,0:T(8,128)(2,1)} %copy-done.3), kind=kOutput, calls=%fused_computation.10 | convolution fusion | flops 811794432 | bytes 5832704 | tf_op jit(solution)/shard_map/dot_general | solution.py:25
  192.4 37.1 %all-gather.2.cloned.1.call-done = bf16[4096,256]{1,0:T(8,128)(2,1)} async-done(((bf16[512,256]{1,0:T(8,128)(2,1)}), bf16[4096,256]{1,0:T(8,128)(2,1)}) %all-gather.2.cloned.1.call-update) | async-done | bytes 2097168 | tf_op jit(solution)/shard_map/all_gather | solution.py:103
  229.5 3.1 %copy.23 = bf16[4,4,2,128,256]{4,3,2,1,0:T(8,128)(2,1)} copy(bf16[4,4,2,128,256]{4,3,0,1,2:T(8,128)(2,1)} %bitcast.83) | data formatting | bytes 4194304 | tf_op jit(solution)/shard_map/transpose | solution.py:104
  (60 shorter events, 10.1 us)
Async XLA Ops:
  8.0 50.8 %copy-start = (bf16[1000,256]{1,0:T(8,128)(2,1)S(1)}, bf16[1000,256]{1,0:T(8,128)(2,1)}, u32[]{:S(2)}) copy-start(bf16[1000,256]{1,0:T(8,128)(2,1)} %param.20) | copy-start | bytes 1536004
  10.2 46.8 %copy-start.1 = (f32[384,384]{0,1:T(8,128)}, f32[384,384]{0,1:T(8,128)S(1)}, u32[]{:S(2)}) copy-start(f32[384,384]{0,1:T(8,128)S(1)} %get-tuple-element.6) | copy-start | bytes 1769476
  11.6 47.2 %copy-start.7 = (s32[8]{0:T(128)S(1)}, s32[8]{0:T(128)}, u32[]{:S(2)}) copy-start(s32[8]{0:T(128)} %param.19) | copy-start | bytes 100
  11.6 47.4 %copy-start.9 = (bf16[16,256]{1,0:T(8,128)(2,1)S(1)}, bf16[16,256]{1,0:T(8,128)(2,1)}, u32[]{:S(2)}) copy-start(bf16[16,256]{1,0:T(8,128)(2,1)} %param.21) | copy-start | bytes 24580
  11.6 47.4 %copy-start.12 = (s32[8]{0:T(128)S(1)}, s32[8]{0:T(128)}, u32[]{:S(2)}) copy-start(s32[8]{0:T(128)} %param.18) | copy-start | bytes 100
  45.8 27.5 %collective-permute-start.2 = (bf16[512,384]{0,1:T(8,128)(2,1)S(1)}, bf16[512,384]{0,1:T(8,128)(2,1)S(1)}, u32[]{:S(2)}, u32[]{:S(2)}) collective-permute-start(bf16[512,384]{0,1:T(8,128)(2,1)S(1)} %all_gather.6), channel_id=1, source_target_pairs={{0,6},{2,0},{4,2},{6,4},{1,7},{3,1},{5,3},{7,5},{8,14},{10,8},{12,... | collective-permute-start | bytes 1179656 | tf_op jit(solution)/shard_map/ppermute | solution.py:29
  48.2 23.3 %collective-permute-start.1 = (bf16[512,384]{0,1:T(8,128)(2,1)S(1)}, bf16[512,384]{0,1:T(8,128)(2,1)}, u32[]{:S(2)}, u32[]{:S(2)}) collective-permute-start(bf16[512,384]{0,1:T(8,128)(2,1)S(1)} %all_gather.6), channel_id=1, source_target_pairs={{0,4},{2,6},{4,0},{6,2},{1,5},{3,7},{5,1},{7,3},{8,12},{10,14},{12... | collective-permute-start | bytes 1179656 | tf_op jit(solution)/shard_map/ppermute | solution.py:29
  52.5 17.2 %collective-permute-start = (bf16[512,384]{0,1:T(8,128)(2,1)S(1)}, bf16[512,384]{0,1:T(8,128)(2,1)}, u32[]{:S(2)}, u32[]{:S(2)}) collective-permute-start(bf16[512,384]{0,1:T(8,128)(2,1)S(1)} %all_gather.6), channel_id=1, source_target_pairs={{0,2},{2,4},{4,6},{6,0},{1,3},{3,5},{5,7},{7,1},{8,10},{10,12},{12... | collective-permute-start | bytes 1179656 | tf_op jit(solution)/shard_map/ppermute | solution.py:29
  82.9 7.3 %copy-start.10 = (bf16[8,256]{1,0:T(8,128)(2,1)S(1)}, bf16[8,256]{1,0:T(8,128)(2,1)}, u32[]{:S(2)}) copy-start(bf16[8,256]{1,0:T(8,128)(2,1)} %param.22) | copy-start | bytes 12292
  82.9 7.3 %copy-start.13 = (s32[8]{0:T(128)S(1)}, s32[8]{0:T(128)}, u32[]{:S(2)}) copy-start(s32[8]{0:T(128)} %param.17) | copy-start | bytes 100
  82.9 7.5 %copy-start.11 = (bf16[8,256]{1,0:T(8,128)(2,1)S(1)}, bf16[8,256]{1,0:T(8,128)(2,1)}, u32[]{:S(2)}) copy-start(bf16[8,256]{1,0:T(8,128)(2,1)} %param.23) | copy-start | bytes 12292
  82.9 7.5 %copy-start.14 = (s32[8]{0:T(128)S(1)}, s32[8]{0:T(128)}, u32[]{:S(2)}) copy-start(s32[8]{0:T(128)} %param.16) | copy-start | bytes 100
  82.9 7.7 %copy-start.5 = (bf16[384,256]{1,0:T(8,128)(2,1)S(1)}, bf16[384,256]{1,0:T(8,128)(2,1)}, u32[]{:S(2)}) copy-start(bf16[384,256]{1,0:T(8,128)(2,1)} %param.14) | copy-start | bytes 589828
  88.3 7.8 %collective-permute-start.3 = (bf16[2048,384]{1,0:T(8,128)(2,1)}, bf16[2048,384]{1,0:T(8,128)(2,1)}, u32[]{:S(2)}, u32[]{:S(2)}) collective-permute-start(bf16[2048,384]{1,0:T(8,128)(2,1)} %bitcast.80), channel_id=1, source_target_pairs={{0,1},{1,0},{2,3},{3,2},{4,5},{5,4},{6,7},{7,6},{8,9},{9,8},{10,11... | collective-permute-start | bytes 4718600 | tf_op jit(solution)/shard_map/ppermute | solution.py:29
  93.6 14.3 %collective-permute-start.4 = (bf16[2048,384]{1,0:T(8,128)(2,1)}, bf16[2048,384]{1,0:T(8,128)(2,1)}, u32[]{:S(2)}, u32[]{:S(2)}) collective-permute-start(bf16[2048,384]{1,0:T(8,128)(2,1)} %convolution_convert_fusion.1), channel_id=1, source_target_pairs={{0,1},{1,0},{2,3},{3,2},{4,5},{5,4},{6,7},{7,6},{8,9},{9,8},{10,11... | collective-permute-start | bytes 4718600 | tf_op jit(solution)/shard_map/ppermute | solution.py:29
  98.2 2.6 %copy-start.3 = (bf16[2048,384]{1,0:T(8,128)(2,1)}, bf16[2048,384]{1,0:T(8,128)(2,1)S(1)}, u32[]{:S(2)}) copy-start(bf16[2048,384]{1,0:T(8,128)(2,1)S(1)} %get-tuple-element.3) | copy-start | bytes 4718596
  98.2 2.6 %copy-start.4 = (bf16[2048,384]{1,0:T(8,128)(2,1)}, bf16[2048,384]{1,0:T(8,128)(2,1)S(1)}, u32[]{:S(2)}) copy-start(bf16[2048,384]{1,0:T(8,128)(2,1)S(1)} %get-tuple-element.4) | copy-start | bytes 4718596
  100.8 58.5 %all-to-all-start = ((bf16[8,512,256]{2,1,0:T(8,128)(2,1)}), bf16[8,512,256]{2,1,0:T(8,128)(2,1)}, u32[]{:S(2)}, u32[]{:S(2)}) async-start(bf16[8,512,256]{2,1,0:T(8,128)(2,1)} %bitcast.82), calls=%async_computation.2 | async-start | bytes 4194304 | tf_op jit(solution)/shard_map/all_to_all | solution.py:98
  107.9 37.1 %reduce-scatter.3.cloned.1.call-start = ((), (), s32[]{:S(2)}) async-start(), calls=%async_computation.3 | async-start | bytes 1966080 | tf_op jit(solution)/shard_map/reduce_scatter | solution.py:81
  111.3 78.2 %reduce-scatter.5.cloned.1.call-start = ((), (), s32[]{:S(2)}) async-start(), calls=%async_computation.4 | async-start | bytes 491520 | tf_op jit(solution)/shard_map/reduce_scatter | solution.py:82
  145.0 84.5 %all-gather.2.cloned.1.call-start = ((), (), s32[]{:S(2)}) async-start(), calls=%async_computation.5 | async-start | bytes 2359296 | tf_op jit(solution)/shard_map/all_gather | solution.py:103
  161.3 17.2 %collective-permute-start.6 = (bf16[512,256]{1,0:T(8,128)(2,1)S(1)}, bf16[512,256]{1,0:T(8,128)(2,1)S(1)}, u32[]{:S(2)}, u32[]{:S(2)}) collective-permute-start(bf16[512,256]{1,0:T(8,128)(2,1)S(1)} %reduce_sum.42), channel_id=1, source_target_pairs={{0,512},{256,0},{512,256},{1,513},{257,1},{513,257},{2,514},{258,2... | collective-permute-start | bytes 786440 | tf_op jit(solution)/shard_map/ppermute | solution.py:29
  164.3 20.6 %collective-permute-start.5 = (bf16[512,256]{1,0:T(8,128)(2,1)S(1)}, bf16[512,256]{1,0:T(8,128)(2,1)S(1)}, u32[]{:S(2)}, u32[]{:S(2)}) collective-permute-start(bf16[512,256]{1,0:T(8,128)(2,1)S(1)} %reduce_sum.42), channel_id=1, source_target_pairs={{0,256},{256,512},{512,0},{1,257},{257,513},{513,1},{2,258},{258,5... | collective-permute-start | bytes 786440 | tf_op jit(solution)/shard_map/ppermute | solution.py:29
  185.7 3.8 %copy-start.2 = (f32[384,384]{0,1:T(8,128)S(1)}, f32[384,384]{0,1:T(8,128)}, u32[]{:S(2)}) copy-start(f32[384,384]{0,1:T(8,128)} %copy-done.1) | copy-start | bytes 1769476
  185.7 3.8 %copy-start.6 = (bf16[384,3,128]{2,0,1:T(8,128)(2,1)S(1)}, bf16[384,3,128]{2,0,1:T(8,128)(2,1)}, u32[]{:S(2)}) copy-start(bf16[384,3,128]{2,0,1:T(8,128)(2,1)} %param.12) | copy-start | bytes 884740
  189.5 1.9 copy-start.8
Sparse Core Ops, SparseCore 0:
  111.8 33.1 reduce-scatter.2
  148.1 37.3 reduce-scatter.4
Sparse Core Ops, SparseCore 1:
  185.8 43.6 all-gather.1

commit v2 on v1

v2 whole, which is shorter than its diff:
```python
import jax
import jax.numpy as jnp
from jax import lax
from jax.experimental import pallas as pl
from jax.experimental.pallas import tpu as pltpu
from jax.sharding import Mesh, PartitionSpec as P

HEAD = 128
ROW = ("zlo", "y")
COL = ("zhi", "x", "core")
NZLO, NY, NZHI, NX, NCORE = 3, 8, 4, 4, 2
F32 = jnp.float32
BF = jnp.bfloat16
LIMIT = 32 * 1024 * 1024
SMEM = pl.BlockSpec(memory_space=pltpu.SMEM)
VMEM = pl.BlockSpec(memory_space=pltpu.VMEM)
ANY = pl.BlockSpec(memory_space=pl.ANY)


def scene_of(lengths, count):
    ends = jnp.cumsum(lengths)
    places = jnp.arange(count)
    return jnp.sum((places[:, None] >= ends[None, :]).astype(jnp.int32), axis=1)


def lookup(ids, table):
    picks = (ids[:, None] == jnp.arange(table.shape[0])[None, :]).astype(table.dtype)
    return jnp.dot(picks, table, preferred_element_type=F32)


def dot(a, b, dims):
    return lax.dot_general(a, b, (dims, ((), ())), preferred_element_type=F32)


def shift(value, axis, size, step):
    return lax.ppermute(value, axis, [(i, (i + step) % size) for i in range(size)])


def after(value, *others):
    return lax.optimization_barrier((value,) + others)[0]


def call(body, out_shape, in_specs, out_specs, flops, nbytes, scratch=()):
    return pl.pallas_call(
        body,
        out_shape=out_shape,
        in_specs=in_specs,
        out_specs=out_specs,
        scratch_shapes=list(scratch),
        compiler_params=pltpu.CompilerParams(vmem_limit_bytes=LIMIT),
        cost_estimate=pl.CostEstimate(flops=flops, bytes_accessed=nbytes, transcendentals=0),
    )


def up_body(place, weight, gated, *refs):
    out = refs[-1]
    core = place[1]
    pick = core if len(refs) == 2 else 1 - core
    for x in range(NX):
        for z in range(NZHI):
            rows = pl.ds((x * NZHI + z) * HEAD, HEAD)
            value = dot(weight[(z * NX + x) * NCORE + pick], gated[...], ((1,), (1,)))
            if len(refs) == 2:
                value = value + refs[0][rows, :].astype(F32)
            out[rows, :] = value.astype(BF)


def upstream_part(place, weight, gated, *got):
    toks = gated.shape[0]
    rows = NX * NZHI * HEAD
    return call(
        up_body,
        jax.ShapeDtypeStruct((rows, toks), BF),
        [SMEM] + [VMEM] * (2 + len(got)),
        VMEM,
        2 * rows * toks * gated.shape[1],
        4 * rows * toks,
    )(place, weight, gated, *got)


def part_body(*refs):
    *pieces, gated, out = refs
    rows = pieces[0].shape[0]
    for i, piece in enumerate(pieces):
        out[i * rows : (i + 1) * rows, :] = dot(piece[...], gated[...], ((1,), (0,))).astype(BF)


def weight_part(pieces, gated):
    rows = sum(p.shape[0] for p in pieces)
    toks, width = gated.shape
    return call(
        part_body,
        jax.ShapeDtypeStruct((rows, width), BF),
        [VMEM] * (len(pieces) + 1),
        VMEM,
        2 * rows * toks * width,
        2 * rows * (toks + width),
    )(*pieces, gated)


def mix_body(place, weight, gate, *refs):
    *pieces, out, acc = refs
    x, core = place[0], place[1]
    for i, piece in enumerate(pieces):
        s, c = i // 2, i % 2
        chip = lax.rem(x + NX - s, NX)
        pick = core if c == 0 else 1 - core
        rows = jnp.concatenate([weight[(z * NX + chip) * NCORE + pick] for z in range(NZHI)])
        value = dot(piece[...], rows, ((0,), (0,)))
        acc[...] = value if i == 0 else acc[...] + value
    out[...] = (gate[...] * acc[...]).astype(BF)


def mix(place, weight, gate, pieces):
    toks, width = gate.shape
    rows = sum(p.shape[0] for p in pieces)
    return call(
        mix_body,
        jax.ShapeDtypeStruct((toks, width), BF),
        [SMEM] + [VMEM] * (2 + len(pieces)),
        VMEM,
        2 * rows * toks * width,
        2 * rows * (toks + width),
        [pltpu.VMEM((toks, width), F32)],
    )(place, weight, gate, *pieces)


def place_body(place, src, dst, sems):
    x, core = place[0], place[1]
    copies = []
    for y in range(NY):
        for b in range(4):
            if b == 0:
                i, s = y, 0
            else:
                i = 3 * y + b - 1
                s, i = 1 + i // 8, i % 8
            c, z = i // NZHI, i % NZHI
            chip = lax.rem(x + NX - s, NX)
            head = (z * NX + chip) * NCORE + (core if c == 0 else 1 - core)
            copies.append(pltpu.make_async_copy(src.at[y * 4 + b], dst.at[head], sems.at[y * 4 + b]))
    for copy in copies:
        copy.start()
    for copy in copies:
        copy.wait()


def put_heads(place, total):
    heads = total.shape[0] // HEAD
    return call(
        place_body,
        jax.ShapeDtypeStruct((heads, HEAD, total.shape[1]), BF),
        [SMEM, ANY],
        ANY,
        0,
        4 * total.size,
        [pltpu.SemaphoreType.DMA((heads,))],
    )(place, total.reshape(heads, HEAD, -1)).reshape(total.shape)


def exchange(part):
    spread = lax.all_to_all(part, "y", split_axis=0, concat_axis=0, tiled=True)
    return spread


def fold(spread):
    return spread.reshape(NY, -1, spread.shape[1]).astype(F32).sum(0).astype(BF)


def fold_zlo(value):
    total = value.astype(F32)
    for s in range(1, NZLO):
        total = total + shift(value, "zlo", NZLO, s).astype(F32)
    return total.astype(BF)


def on_device(
    qkv,
    out_weight,
    cotangent,
    scene_lengths,
    bucket_ids,
    sensor_ids,
    gsd_ids,
    step_ids,
    step_table,
    gsd_table,
    sensor_table,
    bucket_table,
):
    toks = qkv.shape[0]
    width = cotangent.shape[1]
    factor = HEAD ** (-0.5)
    place = jnp.stack([lax.axis_index("x"), lax.axis_index("core")]).astype(jnp.int32)
    weight = out_weight.reshape(-1, HEAD, width)

    segments = scene_of(scene_lengths, toks)
    same = segments[:, None] == segments[None, :]
    queries, keys, values = qkv[:, 0], qkv[:, 1], qkv[:, 2]

    scores = dot(queries, keys, ((1,), (1,))) * factor
    scores = jnp.where(same, scores, -1e30)
    top = jnp.max(scores, axis=-1, keepdims=True)
    weights = jnp.exp(scores - top)
    probs = weights / jnp.sum(weights, axis=-1, keepdims=True)
    rounded = probs.astype(BF)
    attended = dot(values, rounded, ((0,), (1,))).astype(BF)

    gate_scene = lookup(step_ids, step_table) + lookup(gsd_ids, gsd_table)
    gate_scene = gate_scene + lookup(sensor_ids, sensor_table) + lookup(bucket_ids, bucket_table)
    member = (segments[:, None] == jnp.arange(scene_lengths.shape[0])[None, :]).astype(F32)
    gate = jnp.dot(member, gate_scene, precision=lax.Precision.HIGHEST, preferred_element_type=F32)
    gated = (gate * cotangent.astype(F32)).astype(BF)

    own = {0: lax.all_gather(attended, "zhi", axis=0, tiled=True)}
    for s in (1, 3, 2):
        own[s] = shift(own[0], "x", NX, s)

    sent = upstream_part(place, weight, gated)
    got = shift(sent, "core", NCORE, 1)
    summed = upstream_part(place, weight, gated, got)

    other = {0: shift(own[0], "core", NCORE, 1)}
    first = weight_part([own[0], other[0]], gated)
    first = exchange(first)

    held = lax.optimization_barrier((own[1], own[2], own[3], summed))
    own[1], own[2], own[3], summed = held
    summed = lax.psum_scatter(summed, "x", scatter_dimension=0, tiled=True)
    summed = lax.psum_scatter(summed, "zhi", scatter_dimension=0, tiled=True)

    for s in (1, 3, 2):
        other[s] = shift(own[s], "core", NCORE, 1)
    second = weight_part([p for s in (1, 2, 3) for p in (own[s], other[s])], gated)
    second = exchange(second)
    first = fold_zlo(fold(first))
    second = fold_zlo(fold(second))
    total = jnp.concatenate([first, second])
    total = lax.all_gather(total, "y", axis=0, tiled=True)
    total = put_heads(place, total)

    mixed = mix(place, weight, gate, [p for s in range(NX) for p in (own[s], other[s])])

    upstream = summed.T
    grad_values = dot(rounded, upstream, ((0,), (0,))).astype(BF)
    grad_probs = dot(upstream, values, ((1,), (1,)))
    inner = jnp.sum(probs * grad_probs, axis=-1, keepdims=True)
    grad_scores = (probs * (grad_probs - inner)).astype(BF)
    grad_queries = (dot(grad_scores, keys, ((1,), (0,))) * factor).astype(BF)
    grad_keys = (dot(grad_scores, queries, ((0,), (0,))) * factor).astype(BF)
    grad_qkv = jnp.stack([grad_queries, grad_keys, grad_values], axis=1)
    return (mixed, grad_qkv, total)


def solution(mesh):
    fine = Mesh(mesh.devices.reshape(NZLO, NY, NZHI, NX, NCORE), ROW + COL)
    return jax.shard_map(
        on_device,
        mesh=fine,
        in_specs=(
            P(ROW, None, COL),
            P(None, COL),
            P(ROW, COL),
            P(ROW),
            P(ROW),
            P(ROW),
            P(ROW),
            P(ROW),
            P(None, COL),
            P(None, COL),
            P(None, COL),
            P(None, COL),
        ),
        out_specs=(P(ROW, COL), P(ROW, None, COL), P(None, COL)),
        check_vma=False,
    )
```

time: 241 us -> 215 us (0.89)
  waiting for transfers between devices: 112 us -> 78.8 us
  starting transfers between devices: 28.8 us -> 48.9 us
  Pallas kernels: 0 us -> 12.8 us
  local copies, waits for them, and re-layouts: 24.3 us -> 13.7 us
  matrix products: 17.9 us -> 8.41 us
  blocking collectives: 34.1 us -> 27.4 us
    reduce_scatter x1, waiting for transfers between devices: 33.7 us -> 13.3 us  [on_device(): summed = lax.psum_scatter(summed, 'x', scatter_dimension=0, tiled=True)]
    ppermute x7 -> x12, waiting for transfers between devices: 27.1 us -> 13.8 us  [shift(): lax.ppermute(value, axis, [(i, (i + step) % size) for i in range(size)])]
    dot_general x10 -> x6, matrix products: 16 us -> 2.81 us  [dot(): return lax.dot_general(a, b, (dims, ((), ())), preferred_element_type=F32)]
    ppermute x7 -> x12, starting transfers between devices: 21.6 us -> 34.5 us  [shift(): lax.ppermute(value, axis, [(i, (i + step) % size) for i in range(size)])]
    pallas_call x0 -> x6, Pallas kernels: none -> 12.8 us  [the longest x2 5.08 us: upstream_part(): call(up_body, jax.ShapeDtypeStruct((rows, toks), BF), [SMEM] + [VMEM] * (...]
    all_to_all x1 -> x2, starting transfers between devices: 7.05 us -> 14.3 us  [exchange(): spread = lax.all_to_all(part, 'y', split_axis=0, concat_axis=0, tiled=True)]
    all_gather x1, blocking collectives: 34.1 us -> 27.4 us  [on_device(): own = {0: lax.all_gather(attended, 'zhi', axis=0, tiled=True)}]
    all_to_all x1 -> x2, waiting for transfers between devices: 14.3 us -> 19.6 us  [exchange(): spread = lax.all_to_all(part, 'y', split_axis=0, concat_axis=0, tiled=True)]
  transfers between devices with their start and end apart: 11 -> 17, of which waited for: 6 -> 7; matrix products, arithmetic and copies ran while one was open for 11% -> 5% of each run, Pallas kernels for 0% -> 4%
where the time goes in v2:
time: 215 us; the launch traced here: 214 us
  waiting for transfers between devices  78.8 us (37%)
  starting transfers between devices  48.9 us (23%)
  blocking collectives  27.4 us (13%)
  between operations  15.9 us (7%)
  local copies, waits for them, and re-layouts  13.7 us (6%)
  Pallas kernels  12.8 us (6%)
  matrix products  8.41 us (4%)
  other arithmetic  8.14 us (4%)
    ppermute x12, starting transfers between devices, shift(): lax.ppermute(value, axis, [(i, (i + step) % size) for i in range(size)])  34.5 us
    all_gather x1, waiting for transfers between devices, on_device(): total = lax.all_gather(total, 'y', axis=0, tiled=True)  31.9 us
    all_gather x1, blocking collectives, on_device(): own = {0: lax.all_gather(attended, 'zhi', axis=0, tiled=True)}  27.4 us
    all_to_all x2, waiting for transfers between devices, exchange(): spread = lax.all_to_all(part, 'y', split_axis=0, concat_axis=0, tiled=True)  19.6 us
    all_to_all x2, starting transfers between devices, exchange(): spread = lax.all_to_all(part, 'y', split_axis=0, concat_axis=0, tiled=True)  14.3 us
    ppermute x12, waiting for transfers between devices, shift(): lax.ppermute(value, axis, [(i, (i + step) % size) for i in range(size)])  13.8 us
    unnamed x42, local copies, waits for them, and re-layouts  13.7 us
    reduce_scatter x1, waiting for transfers between devices, on_device(): summed = lax.psum_scatter(summed, 'x', scatter_dimension=0, tiled=True)  13.3 us
  transfers between devices with their start and end apart: 17, of which 7 were waited for; matrix products, arithmetic and copies ran while one was open for 5% of the time, Pallas kernels for 4%

profile of v2, /device:TPU:2, one launch (start us, length us, event | category | flops | bytes accessed | tf_op | source)
XLA Modules:
  0.0 214.0 jit_solution(6718457342090403114)
XLA Ops:
  12.6 2.0 multiply_convert_fusion.1
  14.7 1.6 copy-done.1
  16.3 2.7 %shard_map.139 = bf16[2048,384]{1,0:T(8,128)(2,1)} custom-call(s32[2]{0:T(128)S(1)} %pad_add_fusion.place, bf16[32,128,256]{2,1,0:T(8,128)(2,1)S(1)} %bitcast.47, bf16[384,256]{1,0:T(8,128)(2,1)S(1)} %get-tuple-element.13.gated.refs_2_.refs_6_), custom_call_target="tpu_custom_call" | custom-call | flops 402653184 | bytes 3145728 | tf_op jit(solution)/shard_map/pallas_call | solution.py:71
  18.9 1.9 collective-permute-start.4
  22.3 27.4 %all_gather.6.refs_0_ = bf16[512,384]{1,0:T(8,128)(2,1)S(1)} all-gather(bf16[128,384]{1,0:T(8,128)(2,1)S(1)} %fusion.3), channel_id=1, replica_groups=mesh['zlo'=3,'y'=8,'zhi'=4,'x'=4,'core'=2] {'zhi'}, dimensions={0}, use_global_device_ids=true | all-gather | bytes 491520 | tf_op jit(solution)/shard_map/all_gather | solution.py:215
  49.6 1.9 collective-permute-start
  51.5 3.3 %collective-permute-start.1 = (bf16[512,384]{1,0:T(8,128)(2,1)S(1)}, bf16[512,384]{1,0:T(8,128)(2,1)}, u32[]{:S(2)}, u32[]{:S(2)}) collective-permute-start(bf16[512,384]{1,0:T(8,128)(2,1)S(1)} %all_gather.6.refs_0_), channel_id=1, source_target_pairs={{0,2},{2,4},{4,6},{6,0},{1,3},{3,5},{5,7},{7,1},{8,10},{10,12},{12... | collective-permute-start | bytes 1179656 | tf_op jit(solution)/shard_map/ppermute | solution.py:36
  54.9 3.5 %collective-permute-start.2 = (bf16[512,384]{1,0:T(8,128)(2,1)S(1)}, bf16[512,384]{1,0:T(8,128)(2,1)}, u32[]{:S(2)}, u32[]{:S(2)}) collective-permute-start(bf16[512,384]{1,0:T(8,128)(2,1)S(1)} %all_gather.6.refs_0_), channel_id=1, source_target_pairs={{0,4},{2,6},{4,0},{6,2},{1,5},{3,7},{5,1},{7,3},{8,12},{10,14},{12... | collective-permute-start | bytes 1179656 | tf_op jit(solution)/shard_map/ppermute | solution.py:36
  58.4 3.6 %collective-permute-start.3 = (bf16[512,384]{1,0:T(8,128)(2,1)S(1)}, bf16[512,384]{1,0:T(8,128)(2,1)}, u32[]{:S(2)}, u32[]{:S(2)}) collective-permute-start(bf16[512,384]{1,0:T(8,128)(2,1)S(1)} %all_gather.6.refs_0_), channel_id=1, source_target_pairs={{0,6},{2,0},{4,2},{6,4},{1,7},{3,1},{5,3},{7,5},{8,14},{10,8},{12,... | collective-permute-start | bytes 1179656 | tf_op jit(solution)/shard_map/ppermute | solution.py:36
  63.6 7.2 %all-to-all-start = ((bf16[8,128,256]{2,1,0:T(8,128)(2,1)}), bf16[8,128,256]{2,1,0:T(8,128)(2,1)}, u32[]{:S(2)}, u32[]{:S(2)}) async-start(bf16[8,128,256]{2,1,0:T(8,128)(2,1)} %bitcast.51), calls=%async_computation.2 | async-start | bytes 1048576 | tf_op jit(solution)/shard_map/all_to_all | solution.py:162
  70.8 2.4 %shard_map.140 = bf16[2048,384]{1,0:T(8,128)(2,1)S(1)} custom-call(s32[2]{0:T(128)S(1)} %pad_add_fusion.place, bf16[32,128,256]{2,1,0:T(8,128)(2,1)S(1)} %bitcast.48, bf16[384,256]{1,0:T(8,128)(2,1)S(1)} %get-tuple-element.13.gated.refs_2_.refs_6_, bf16[2048,384]{1,0:T(8,128)(2,1)} %collective-permute-done.4.refs_0_), custom_call_target="tpu_custom_call" | custom-call | flops 402653184 | bytes 3145728 | tf_op jit(solution)/shard_map/pallas_call | solution.py:71
  74.4 3.7 %collective-permute-done.3.refs_6_.refs_4_ = bf16[512,384]{1,0:T(8,128)(2,1)} collective-permute-done((bf16[512,384]{1,0:T(8,128)(2,1)S(1)}, bf16[512,384]{1,0:T(8,128)(2,1)}, u32[]{:S(2)}, u32[]{:S(2)}) %collective-permute-start.3) | collective-permute-done | bytes 393248 | tf_op jit(solution)/shard_map/ppermute | solution.py:36
  78.1 1.9 collective-permute-start.5
  80.0 2.4 %collective-permute-start.6 = (bf16[512,384]{1,0:T(8,128)(2,1)}, bf16[512,384]{1,0:T(8,128)(2,1)S(1)}, u32[]{:S(2)}, u32[]{:S(2)}) collective-permute-start(bf16[512,384]{1,0:T(8,128)(2,1)} %collective-permute-done.2.refs_4_.refs_2_), channel_id=1, source_target_pairs={{0,1},{1,0},{2,3},{3,2},{4,5},{5,4},{6,7},{7,6},{8,9},{9,8},{10,11... | collective-permute-start | bytes 1179656 | tf_op jit(solution)/shard_map/ppermute | solution.py:36
  82.4 1.9 collective-permute-start.7
  84.4 1.9 collective-permute-done.7.refs_7_.refs_5_
  86.2 2.2 %shard_map.143 = bf16[3072,256]{1,0:T(8,128)(2,1)S(1)} custom-call(bf16[512,384]{1,0:T(8,128)(2,1)} %collective-permute-done.1.refs_2_.refs_0_, bf16[512,384]{1,0:T(8,128)(2,1)S(1)} %collective-permute-done.5.refs_3_.refs_1_, bf16[512,384]{1,0:T(8,128)(2,1)} %collective-permute-done.2.refs_4_.refs_2_, ...), custom_call_target="tpu_custom_call" | custom-call | flops 603979776 | bytes 3932160 | tf_op jit(solution)/shard_map/pallas_call | solution.py:91
  91.9 7.1 %all-to-all-start.1 = ((bf16[8,384,256]{2,1,0:T(8,128)(2,1)}), bf16[8,384,256]{2,1,0:T(8,128)(2,1)}, u32[]{:S(2)}, u32[]{:S(2)}) async-start(bf16[8,384,256]{2,1,0:T(8,128)(2,1)} %bitcast.50), calls=%async_computation.3 | async-start | bytes 3145728 | tf_op jit(solution)/shard_map/all_to_all | solution.py:162
  99.0 13.3 %reduce-scatter.3.cloned.1.call-done = bf16[512,384]{1,0:T(8,128)(2,1)} async-done(((bf16[2048,384]{1,0:T(8,128)(2,1)}), bf16[512,384]{1,0:T(8,128)(2,1)}) %reduce-scatter.3.cloned.1.call-update) | async-done | bytes 393232 | tf_op jit(solution)/shard_map/reduce_scatter | solution.py:229
  113.6 4.2 %collective-permute-start.9 = (bf16[128,256]{1,0:T(8,128)(2,1)S(1)}, bf16[128,256]{1,0:T(8,128)(2,1)S(1)}, u32[]{:S(2)}, u32[]{:S(2)}) collective-permute-start(bf16[128,256]{1,0:T(8,128)(2,1)S(1)} %reduce_sum.54), channel_id=1, source_target_pairs={{0,512},{256,0},{512,256},{1,513},{257,1},{513,257},{2,514},{258,2... | collective-permute-start | bytes 196616 | tf_op jit(solution)/shard_map/ppermute | solution.py:36
  117.8 1.9 collective-permute-start.8
  119.7 19.6 %all-to-all-done.1 = bf16[8,384,256]{2,1,0:T(8,128)(2,1)} async-done(((bf16[8,384,256]{2,1,0:T(8,128)(2,1)}), bf16[8,384,256]{2,1,0:T(8,128)(2,1)}, u32[]{:S(2)}, u32[]{:S(2)}) %all-to-all-start.1) | async-done | bytes 1572896 | tf_op jit(solution)/shard_map/all_to_all | solution.py:162
  139.4 2.4 %reduce_sum.55 = bf16[384,256]{1,0:T(8,128)(2,1)} reduce(bf16[8,384,256]{2,1,0:T(8,128)(2,1)} %all-to-all-done.1, bf16[]{:T(256)} %constant.24.clone.1), dimensions={0}, to_apply=%region_8.9 | reduce | flops 688128 | bytes 1769474 | tf_op jit(solution)/shard_map/reduce_sum | solution.py:167
  141.7 5.9 %collective-permute-start.11 = (bf16[384,256]{1,0:T(8,128)(2,1)}, bf16[384,256]{1,0:T(8,128)(2,1)S(1)}, u32[]{:S(2)}, u32[]{:S(2)}) collective-permute-start(bf16[384,256]{1,0:T(8,128)(2,1)} %reduce_sum.55), channel_id=1, source_target_pairs={{0,512},{256,0},{512,256},{1,513},{257,1},{513,257},{2,514},{258,2... | collective-permute-start | bytes 589832 | tf_op jit(solution)/shard_map/ppermute | solution.py:36
  147.6 1.9 collective-permute-start.10
  150.5 4.4 %collective-permute-done.11 = bf16[384,256]{1,0:T(8,128)(2,1)S(1)} collective-permute-done((bf16[384,256]{1,0:T(8,128)(2,1)}, bf16[384,256]{1,0:T(8,128)(2,1)S(1)}, u32[]{:S(2)}, u32[]{:S(2)}) %collective-permute-start.11) | collective-permute-done | bytes 196640 | tf_op jit(solution)/shard_map/ppermute | solution.py:36
  154.8 3.9 %collective-permute-done.10 = bf16[384,256]{1,0:T(8,128)(2,1)S(1)} collective-permute-done((bf16[384,256]{1,0:T(8,128)(2,1)}, bf16[384,256]{1,0:T(8,128)(2,1)S(1)}, u32[]{:S(2)}, u32[]{:S(2)}) %collective-permute-start.10) | collective-permute-done | bytes 196640 | tf_op jit(solution)/shard_map/ppermute | solution.py:36
  164.5 3.0 %shard_map.141 = bf16[384,256]{1,0:T(8,128)(2,1)} custom-call(s32[2]{0:T(128)S(1)} %pad_add_fusion.place, bf16[32,128,256]{2,1,0:T(8,128)(2,1)S(1)} %bitcast.49, f32[384,256]{1,0:T(8,128)S(1)} %copy-done.7, bf16[512,384]{1,0:T(8,128)(2,1)S(1)} %all_gather.6.refs_0_, bf16[512,384]{1,0:T(8,128)(2,1)S(1)} %copy-done.9, ...), custom_call_target="tpu_custom_call" | custom-call | flops 805306368 | bytes 5242880 | tf_op jit(solution)/shard_map/pallas_call | solution.py:117
  167.4 1.5 multiply_reduce_fusion
  170.8 31.9 %all-gather.2.cloned.1.call-done = bf16[4096,256]{1,0:T(8,128)(2,1)} async-done(((bf16[512,256]{1,0:T(8,128)(2,1)}), bf16[4096,256]{1,0:T(8,128)(2,1)}) %all-gather.2.cloned.1.call-update) | async-done | bytes 2097168 | tf_op jit(solution)/shard_map/all_gather | solution.py:239
  202.8 1.6 copy-done.6
  204.4 2.1 shard_map.144
  (76 shorter events, 21.8 us)
Async XLA Ops:
  8.0 1.1 copy-start
  14.7 1.6 copy-start.1
  16.3 4.6 %copy-start.18 = (bf16[384,3,128]{2,0,1:T(8,128)(2,1)S(1)}, bf16[384,3,128]{2,0,1:T(8,128)(2,1)}, u32[]{:S(2)}) copy-start(bf16[384,3,128]{2,0,1:T(8,128)(2,1)} %param.12) | copy-start | bytes 884740
  18.9 51.8 %collective-permute-start.4 = (bf16[2048,384]{1,0:T(8,128)(2,1)}, bf16[2048,384]{1,0:T(8,128)(2,1)}, u32[]{:S(2)}, u32[]{:S(2)}) collective-permute-start(bf16[2048,384]{1,0:T(8,128)(2,1)} %shard_map.139), channel_id=1, source_target_pairs={{0,1},{1,0},{2,3},{3,2},{4,5},{5,4},{6,7},{7,6},{8,9},{9,8},{10,11... | collective-permute-start | bytes 4718600 | tf_op jit(solution)/shard_map/ppermute | solution.py:36
  22.2 48.5 %copy-start.2 = (bf16[4096,256]{1,0:T(8,128)(2,1)S(1)}, bf16[4096,256]{1,0:T(8,128)(2,1)}, u32[]{:S(2)}) copy-start(bf16[4096,256]{1,0:T(8,128)(2,1)} %param.13) | copy-start | bytes 6291460
  49.6 12.4 %collective-permute-start = (bf16[512,384]{1,0:T(8,128)(2,1)S(1)}, bf16[512,384]{1,0:T(8,128)(2,1)S(1)}, u32[]{:S(2)}, u32[]{:S(2)}) collective-permute-start(bf16[512,384]{1,0:T(8,128)(2,1)S(1)} %all_gather.6.refs_0_), channel_id=1, source_target_pairs={{0,1},{1,0},{2,3},{3,2},{4,5},{5,4},{6,7},{7,6},{8,9},{9,8},{10,11... | collective-permute-start | bytes 1179656 | tf_op jit(solution)/shard_map/ppermute | solution.py:36
  51.5 22.8 %collective-permute-start.1 = (bf16[512,384]{1,0:T(8,128)(2,1)S(1)}, bf16[512,384]{1,0:T(8,128)(2,1)}, u32[]{:S(2)}, u32[]{:S(2)}) collective-permute-start(bf16[512,384]{1,0:T(8,128)(2,1)S(1)} %all_gather.6.refs_0_), channel_id=1, source_target_pairs={{0,2},{2,4},{4,6},{6,0},{1,3},{3,5},{5,7},{7,1},{8,10},{10,12},{12... | collective-permute-start | bytes 1179656 | tf_op jit(solution)/shard_map/ppermute | solution.py:36
  54.9 19.5 %collective-permute-start.2 = (bf16[512,384]{1,0:T(8,128)(2,1)S(1)}, bf16[512,384]{1,0:T(8,128)(2,1)}, u32[]{:S(2)}, u32[]{:S(2)}) collective-permute-start(bf16[512,384]{1,0:T(8,128)(2,1)S(1)} %all_gather.6.refs_0_), channel_id=1, source_target_pairs={{0,4},{2,6},{4,0},{6,2},{1,5},{3,7},{5,1},{7,3},{8,12},{10,14},{12... | collective-permute-start | bytes 1179656 | tf_op jit(solution)/shard_map/ppermute | solution.py:36
  58.4 19.6 %collective-permute-start.3 = (bf16[512,384]{1,0:T(8,128)(2,1)S(1)}, bf16[512,384]{1,0:T(8,128)(2,1)}, u32[]{:S(2)}, u32[]{:S(2)}) collective-permute-start(bf16[512,384]{1,0:T(8,128)(2,1)S(1)} %all_gather.6.refs_0_), channel_id=1, source_target_pairs={{0,6},{2,0},{4,2},{6,4},{1,7},{3,1},{5,3},{7,5},{8,14},{10,8},{12,... | collective-permute-start | bytes 1179656 | tf_op jit(solution)/shard_map/ppermute | solution.py:36
  63.6 28.3 %all-to-all-start = ((bf16[8,128,256]{2,1,0:T(8,128)(2,1)}), bf16[8,128,256]{2,1,0:T(8,128)(2,1)}, u32[]{:S(2)}, u32[]{:S(2)}) async-start(bf16[8,128,256]{2,1,0:T(8,128)(2,1)} %bitcast.51), calls=%async_computation.2 | async-start | bytes 1048576 | tf_op jit(solution)/shard_map/all_to_all | solution.py:162
  70.7 41.7 %reduce-scatter.3.cloned.1.call-start = ((), (), s32[]{:S(2)}) async-start(), calls=%async_computation.4 | async-start | bytes 1966080 | tf_op jit(solution)/shard_map/reduce_scatter | solution.py:229
  73.2 1.1 copy-start.3
  78.1 6.3 %collective-permute-start.5 = (bf16[512,384]{1,0:T(8,128)(2,1)}, bf16[512,384]{1,0:T(8,128)(2,1)S(1)}, u32[]{:S(2)}, u32[]{:S(2)}) collective-permute-start(bf16[512,384]{1,0:T(8,128)(2,1)} %collective-permute-done.1.refs_2_.refs_0_), channel_id=1, source_target_pairs={{0,1},{1,0},{2,3},{3,2},{4,5},{5,4},{6,7},{7,6},{8,9},{9,8},{10,11... | collective-permute-start | bytes 1179656 | tf_op jit(solution)/shard_map/ppermute | solution.py:36
  80.0 4.4 %collective-permute-start.6 = (bf16[512,384]{1,0:T(8,128)(2,1)}, bf16[512,384]{1,0:T(8,128)(2,1)S(1)}, u32[]{:S(2)}, u32[]{:S(2)}) collective-permute-start(bf16[512,384]{1,0:T(8,128)(2,1)} %collective-permute-done.2.refs_4_.refs_2_), channel_id=1, source_target_pairs={{0,1},{1,0},{2,3},{3,2},{4,5},{5,4},{6,7},{7,6},{8,9},{9,8},{10,11... | collective-permute-start | bytes 1179656 | tf_op jit(solution)/shard_map/ppermute | solution.py:36
  82.4 3.8 %collective-permute-start.7 = (bf16[512,384]{1,0:T(8,128)(2,1)}, bf16[512,384]{1,0:T(8,128)(2,1)S(1)}, u32[]{:S(2)}, u32[]{:S(2)}) collective-permute-start(bf16[512,384]{1,0:T(8,128)(2,1)} %collective-permute-done.3.refs_6_.refs_4_), channel_id=1, source_target_pairs={{0,1},{1,0},{2,3},{3,2},{4,5},{5,4},{6,7},{7,6},{8,9},{9,8},{10,11... | collective-permute-start | bytes 1179656 | tf_op jit(solution)/shard_map/ppermute | solution.py:36
  88.5 1.2 copy-start.4
  91.9 47.5 %all-to-all-start.1 = ((bf16[8,384,256]{2,1,0:T(8,128)(2,1)}), bf16[8,384,256]{2,1,0:T(8,128)(2,1)}, u32[]{:S(2)}, u32[]{:S(2)}) async-start(bf16[8,384,256]{2,1,0:T(8,128)(2,1)} %bitcast.50), calls=%async_computation.3 | async-start | bytes 3145728 | tf_op jit(solution)/shard_map/all_to_all | solution.py:162
  99.0 68.5 %reduce-scatter.5.cloned.1.call-start = ((), (), s32[]{:S(2)}) async-start(), calls=%async_computation.5 | async-start | bytes 491520 | tf_op jit(solution)/shard_map/reduce_scatter | solution.py:230
  112.4 90.4 %all-gather.2.cloned.1.call-start = ((), (), s32[]{:S(2)}) async-start(), calls=%async_computation.6 | async-start | bytes 2359296 | tf_op jit(solution)/shard_map/all_gather | solution.py:239
  113.6 46.9 %copy-start.7 = (f32[384,256]{1,0:T(8,128)S(1)}, f32[384,256]{1,0:T(8,128)}, u32[]{:S(2)}) copy-start(f32[384,256]{1,0:T(8,128)} %get-tuple-element.14.gate) | copy-start | bytes 1179652
  113.6 36.0 %collective-permute-start.9 = (bf16[128,256]{1,0:T(8,128)(2,1)S(1)}, bf16[128,256]{1,0:T(8,128)(2,1)S(1)}, u32[]{:S(2)}, u32[]{:S(2)}) collective-permute-start(bf16[128,256]{1,0:T(8,128)(2,1)S(1)} %reduce_sum.54), channel_id=1, source_target_pairs={{0,512},{256,0},{512,256},{1,513},{257,1},{513,257},{2,514},{258,2... | collective-permute-start | bytes 196616 | tf_op jit(solution)/shard_map/ppermute | solution.py:36
  117.8 31.8 %collective-permute-start.8 = (bf16[128,256]{1,0:T(8,128)(2,1)S(1)}, bf16[128,256]{1,0:T(8,128)(2,1)}, u32[]{:S(2)}, u32[]{:S(2)}) collective-permute-start(bf16[128,256]{1,0:T(8,128)(2,1)S(1)} %reduce_sum.54), channel_id=1, source_target_pairs={{0,256},{256,512},{512,0},{1,257},{257,513},{513,1},{2,258},{258,5... | collective-permute-start | bytes 196616 | tf_op jit(solution)/shard_map/ppermute | solution.py:36
  141.7 13.1 %collective-permute-start.11 = (bf16[384,256]{1,0:T(8,128)(2,1)}, bf16[384,256]{1,0:T(8,128)(2,1)S(1)}, u32[]{:S(2)}, u32[]{:S(2)}) collective-permute-start(bf16[384,256]{1,0:T(8,128)(2,1)} %reduce_sum.55), channel_id=1, source_target_pairs={{0,512},{256,0},{512,256},{1,513},{257,1},{513,257},{2,514},{258,2... | collective-permute-start | bytes 589832 | tf_op jit(solution)/shard_map/ppermute | solution.py:36
  147.6 11.1 %collective-permute-start.10 = (bf16[384,256]{1,0:T(8,128)(2,1)}, bf16[384,256]{1,0:T(8,128)(2,1)S(1)}, u32[]{:S(2)}, u32[]{:S(2)}) collective-permute-start(bf16[384,256]{1,0:T(8,128)(2,1)} %reduce_sum.55), channel_id=1, source_target_pairs={{0,256},{256,512},{512,0},{1,257},{257,513},{513,1},{2,258},{258,5... | collective-permute-start | bytes 589832 | tf_op jit(solution)/shard_map/ppermute | solution.py:36
  160.5 1.0 copy-start.9
  161.5 1.0 copy-start.11
  162.5 1.0 copy-start.13
  163.5 1.0 copy-start.15
  167.4 1.5 copy-start.17
  167.4 1.7 copy-start.19
  168.9 0.9 copy-start.20
  202.8 1.6 copy-start.6
  (6 other events, 4.6 us)
Sparse Core Ops, SparseCore 0:
  78.2 34.1 reduce-scatter.2
  115.5 37.6 reduce-scatter.4
Sparse Core Ops, SparseCore 1:
  160.6 42.2 all-gather.1

commit v3 on v2

--- a/solution.py
+++ b/solution.py
@@ -9,12 +9,12 @@
 ROW = ("zlo", "y")
 COL = ("zhi", "x", "core")
 NZLO, NY, NZHI, NX, NCORE = 3, 8, 4, 4, 2
+SLAB = HEAD // NY
 F32 = jnp.float32
 BF = jnp.bfloat16
-LIMIT = 32 * 1024 * 1024
 SMEM = pl.BlockSpec(memory_space=pltpu.SMEM)
 VMEM = pl.BlockSpec(memory_space=pltpu.VMEM)
-ANY = pl.BlockSpec(memory_space=pl.ANY)
+HBM = pl.BlockSpec(memory_space=pltpu.HBM)
 
 
 def scene_of(lengths, count):
@@ -40,14 +40,14 @@
     return lax.optimization_barrier((value,) + others)[0]
 
 
-def call(body, out_shape, in_specs, out_specs, flops, nbytes, scratch=()):
+def call(body, out_shape, in_specs, out_specs, flops, nbytes, scratch=(), limit=60):
     return pl.pallas_call(
         body,
         out_shape=out_shape,
         in_specs=in_specs,
         out_specs=out_specs,
         scratch_shapes=list(scratch),
-        compiler_params=pltpu.CompilerParams(vmem_limit_bytes=LIMIT),
+        compiler_params=pltpu.CompilerParams(vmem_limit_bytes=limit * 1024 * 1024),
         cost_estimate=pl.CostEstimate(flops=flops, bytes_accessed=nbytes, transcendentals=0),
     )
 
@@ -75,70 +75,93 @@
         VMEM,
         2 * rows * toks * gated.shape[1],
         4 * rows * toks,
+        limit=16,
     )(place, weight, gated, *got)
 
 
+def fetch(pieces, held, sems):
+    copies = [pltpu.make_async_copy(p, held.at[i], sems.at[i]) for i, p in enumerate(pieces)]
+    for copy in copies:
+        copy.start()
+    for copy in copies:
+        copy.wait()
+
+
+def fetch_scratch(pieces):
+    count = len(pieces)
+    return [pltpu.VMEM((count, *pieces[0].shape), BF), pltpu.SemaphoreType.DMA((count,))]
+
+
+def slabs(held, y):
+    starts = [z * HEAD + y * SLAB for z in range(NZHI)]
+    return jnp.concatenate(
+        [held[i, start : start + SLAB, :] for i in range(held.shape[0]) for start in starts]
+    )
+
+
 def part_body(*refs):
-    *pieces, gated, out = refs
-    rows = pieces[0].shape[0]
-    for i, piece in enumerate(pieces):
-        out[i * rows : (i + 1) * rows, :] = dot(piece[...], gated[...], ((1,), (0,))).astype(BF)
+    *pieces, gated, out, acc, held, sems = refs
+    fetch(pieces, held, sems)
+    toks = held.shape[2]
+    for y in range(NY):
+        value = dot(slabs(held, y), gated[y * toks : (y + 1) * toks, :], ((1,), (0,)))
+        acc[...] = value if y == 0 else acc[...] + value
+    out[...] = acc[...].astype(BF)
 
 
 def weight_part(pieces, gated):
-    rows = sum(p.shape[0] for p in pieces)
+    rows = sum(p.shape[0] for p in pieces) // NY
     toks, width = gated.shape
     return call(
         part_body,
         jax.ShapeDtypeStruct((rows, width), BF),
-        [VMEM] * (len(pieces) + 1),
+        [HBM] * len(pieces) + [VMEM],
         VMEM,
         2 * rows * toks * width,
         2 * rows * (toks + width),
+        [pltpu.VMEM((rows, width), F32)] + fetch_scratch(pieces),
     )(*pieces, gated)
 
 
-def mix_body(place, weight, gate, *refs):
-    *pieces, out, acc = refs
-    x, core = place[0], place[1]
-    for i, piece in enumerate(pieces):
+def mix_body(place, weight, *refs):
+    *pieces, out, held, sems = refs
+    fetch(pieces, held, sems)
+    x, core, mine = place[0], place[1], place[2]
+    rows = []
+    for i in range(len(pieces)):
         s, c = i // 2, i % 2
         chip = lax.rem(x + NX - s, NX)
         pick = core if c == 0 else 1 - core
-        rows = jnp.concatenate([weight[(z * NX + chip) * NCORE + pick] for z in range(NZHI)])
-        value = dot(piece[...], rows, ((0,), (0,)))
-        acc[...] = value if i == 0 else acc[...] + value
-    out[...] = (gate[...] * acc[...]).astype(BF)
-
-
-def mix(place, weight, gate, pieces):
-    toks, width = gate.shape
+        for z in range(NZHI):
+            start = pl.multiple_of(mine * SLAB, SLAB)
+            rows.append(weight[(z * NX + chip) * NCORE + pick, pl.ds(start, SLAB), :])
+    rows = jnp.concatenate(rows)
+    for y in range(NY):
+        out[y] = dot(slabs(held, y), rows, ((0,), (0,))).astype(BF)
+
+
+def mix_part(place, weight, pieces):
+    toks, width = pieces[0].shape[1], weight.shape[2]
     rows = sum(p.shape[0] for p in pieces)
     return call(
         mix_body,
-        jax.ShapeDtypeStruct((toks, width), BF),
-        [SMEM] + [VMEM] * (2 + len(pieces)),
+        jax.ShapeDtypeStruct((NY, toks, width), BF),
+        [SMEM, VMEM] + [HBM] * len(pieces),
         VMEM,
         2 * rows * toks * width,
         2 * rows * (toks + width),
-        [pltpu.VMEM((toks, width), F32)],
-    )(place, weight, gate, *pieces)
+        fetch_scratch(pieces),
+    )(place, weight, *pieces)
 
 
 def place_body(place, src, dst, sems):
     x, core = place[0], place[1]
     copies = []
-    for y in range(NY):
-        for b in range(4):
-            if b == 0:
-                i, s = y, 0
-            else:
-                i = 3 * y + b - 1
-                s, i = 1 + i // 8, i % 8
-            c, z = i // NZHI, i % NZHI
-            chip = lax.rem(x + NX - s, NX)
-            head = (z * NX + chip) * NCORE + (core if c == 0 else 1 - core)
-            copies.append(pltpu.make_async_copy(src.at[y * 4 + b], dst.at[head], sems.at[y * 4 + b]))
+    for i in range(NX * NCORE * NZHI):
+        s, c, z = i // (NCORE * NZHI), i // NZHI % NCORE, i % NZHI
+        chip = lax.rem(x + NX - s, NX)
+        head = (z * NX + chip) * NCORE + (core if c == 0 else 1 - core)
+        copies.append(pltpu.make_async_copy(src.at[:, i], dst.at[head], sems.at[i]))
     for copy in copies:
         copy.start()
     for copy in copies:
@@ -146,25 +169,16 @@
 
 
 def put_heads(place, total):
-    heads = total.shape[0] // HEAD
+    heads, width = NX * NCORE * NZHI, total.shape[1]
     return call(
         place_body,
-        jax.ShapeDtypeStruct((heads, HEAD, total.shape[1]), BF),
-        [SMEM, ANY],
-        ANY,
+        jax.ShapeDtypeStruct((heads, NY, SLAB, width), BF),
+        [SMEM, HBM],
+        HBM,
         0,
         4 * total.size,
         [pltpu.SemaphoreType.DMA((heads,))],
-    )(place, total.reshape(heads, HEAD, -1)).reshape(total.shape)
-
-
-def exchange(part):
-    spread = lax.all_to_all(part, "y", split_axis=0, concat_axis=0, tiled=True)
-    return spread
-
-
-def fold(spread):
-    return spread.reshape(NY, -1, spread.shape[1]).astype(F32).sum(0).astype(BF)
+    )(place, total.reshape(NY, heads, SLAB, width)).reshape(total.shape)
 
 
 def fold_zlo(value):
@@ -191,7 +205,7 @@
     toks = qkv.shape[0]
     width = cotangent.shape[1]
     factor = HEAD ** (-0.5)
-    place = jnp.stack([lax.axis_index("x"), lax.axis_index("core")]).astype(jnp.int32)
+    place = jnp.stack([lax.axis_index(a) for a in ("x", "core", "y")]).astype(jnp.int32)
     weight = out_weight.reshape(-1, HEAD, width)
 
     segments = scene_of(scene_lengths, toks)
@@ -212,34 +226,34 @@
     gate = jnp.dot(member, gate_scene, precision=lax.Precision.HIGHEST, preferred_element_type=F32)
     gated = (gate * cotangent.astype(F32)).astype(BF)
 
+    gated_y = lax.all_gather(gated, "y", axis=0, tiled=True)
+
+    sent = upstream_part(place, weight, gated)
+    got = shift(sent, "core", NCORE, 1)
+
+    attended, sent = lax.optimization_barrier((attended, sent))
+    attended = lax.all_to_all(attended, "y", split_axis=0, concat_axis=0, tiled=True)
+
+    summed = upstream_part(place, weight, gated, got)
+    attended, summed = lax.optimization_barrier((attended, summed))
+    summed = lax.psum_scatter(summed, "x", scatter_dimension=0, tiled=True)
+
     own = {0: lax.all_gather(attended, "zhi", axis=0, tiled=True)}
     for s in (1, 3, 2):
         own[s] = shift(own[0], "x", NX, s)
-
-    sent = upstream_part(place, weight, gated)
-    got = shift(sent, "core", NCORE, 1)
-    summed = upstream_part(place, weight, gated, got)
-
-    other = {0: shift(own[0], "core", NCORE, 1)}
-    first = weight_part([own[0], other[0]], gated)
-    first = exchange(first)
-
-    held = lax.optimization_barrier((own[1], own[2], own[3], summed))
-    own[1], own[2], own[3], summed = held
-    summed = lax.psum_scatter(summed, "x", scatter_dimension=0, tiled=True)
-    summed = lax.psum_scatter(summed, "zhi", scatter_dimension=0, tiled=True)
-
-    for s in (1, 3, 2):
-        other[s] = shift(own[s], "core", NCORE, 1)
-    second = weight_part([p for s in (1, 2, 3) for p in (own[s], other[s])], gated)
-    second = exchange(second)
-    first = fold_zlo(fold(first))
-    second = fold_zlo(fold(second))
-    total = jnp.concatenate([first, second])
+    pieces = [p for s in range(NX) for p in (own[s], shift(own[s], "core", NCORE, 1))]
+
+    total = weight_part(pieces, gated_y)
+    *pieces, total, summed = lax.optimization_barrier((*pieces, total, summed))
+    parts = mix_part(place, weight, pieces)
+    total, parts = lax.optimization_barrier((fold_zlo(total), parts))
     total = lax.all_gather(total, "y", axis=0, tiled=True)
     total = put_heads(place, total)
 
-    mixed = mix(place, weight, gate, [p for s in range(NX) for p in (own[s], other[s])])
+    summed = lax.psum_scatter(summed, "zhi", scatter_dimension=0, tiled=True)
+
+    parts = lax.all_to_all(parts, "y", split_axis=0, concat_axis=0, tiled=True)
+    mixed = (gate * parts.astype(F32).sum(0)).astype(BF)
 
     upstream = summed.T
     grad_values = dot(rounded, upstream, ((0,), (0,))).astype(BF)

time: 215 us -> 263 us (1.22)
  Pallas kernels: 12.8 us -> 81.6 us
  local copies, waits for them, and re-layouts: 13.7 us -> 6.27 us
  starting transfers between devices: 48.9 us -> 41.5 us
  other arithmetic: 8.14 us -> 3.83 us
    pallas_call x4 -> x3, Pallas kernels: 7.73 us -> 76.5 us  [the longest x1 65.6 us: put_heads(): call(place_body, jax.ShapeDtypeStruct((heads, NY, SLAB, width), BF), [SME...]
    reduce_scatter x1, waiting for transfers between devices: 13.3 us -> 0.03 us  [on_device(): summed = lax.psum_scatter(summed, 'x', scatter_dimension=0, tiled=True)]
    reduce_scatter x1, waiting for transfers between devices: 0.01 us -> 12.7 us  [on_device(): summed = lax.psum_scatter(summed, 'zhi', scatter_dimension=0, tiled=True)]
    all_gather x1, waiting for transfers between devices: 31.9 us -> 23 us  [on_device(): total = lax.all_gather(total, 'y', axis=0, tiled=True)]
    all_to_all x2, waiting for transfers between devices: 19.6 us -> 28.5 us  [the longest x1 23.2 us: on_device(): parts = lax.all_to_all(parts, 'y', split_axis=0, concat_axis=0, tiled=True)]
    unnamed x42 -> x38, local copies, waits for them, and re-layouts: 13.7 us -> 5.51 us
    ppermute x12 -> x10, starting transfers between devices: 34.5 us -> 27.5 us  [shift(): lax.ppermute(value, axis, [(i, (i + step) % size) for i in range(size)])]
    reduce_sum x2 -> x1, other arithmetic: 3.47 us -> 0.22 us  [on_device(): mixed = (gate * parts.astype(F32).sum(0)).astype(BF)]
  transfers between devices with their start and end apart: 17 -> 16, of which waited for: 7 -> 7; matrix products, arithmetic and copies ran while one was open for 5% -> 2% of each run, Pallas kernels for 4% -> 6%
where the time goes in v3:
time: 263 us; the launch traced here: 262 us
  Pallas kernels  81.6 us (31%)
  waiting for transfers between devices  77.4 us (29%)
  starting transfers between devices  41.5 us (16%)
  blocking collectives  27.9 us (11%)
  between operations  15.6 us (6%)
  matrix products  8.23 us (3%)
  local copies, waits for them, and re-layouts  6.27 us (2%)
  other arithmetic  3.83 us (1%)
    pallas_call x1, Pallas kernels, put_heads(): call(place_body, jax.ShapeDtypeStruct((heads, NY, SLAB, width), BF), [SME...  65.6 us
    all_gather x1, blocking collectives, on_device(): own = {0: lax.all_gather(attended, 'zhi', axis=0, tiled=True)}  27.9 us
    ppermute x10, starting transfers between devices, shift(): lax.ppermute(value, axis, [(i, (i + step) % size) for i in range(size)])  27.5 us
    all_to_all x1, waiting for transfers between devices, on_device(): parts = lax.all_to_all(parts, 'y', split_axis=0, concat_axis=0, tiled=True)  23.2 us
    all_gather x1, waiting for transfers between devices, on_device(): total = lax.all_gather(total, 'y', axis=0, tiled=True)  23 us
    ppermute x10, waiting for transfers between devices, shift(): lax.ppermute(value, axis, [(i, (i + step) % size) for i in range(size)])  13.1 us
    reduce_scatter x1, waiting for transfers between devices, on_device(): summed = lax.psum_scatter(summed, 'zhi', scatter_dimension=0, tiled=True)  12.7 us
    all_to_all x1, starting transfers between devices, on_device(): lax.all_to_all(attended, 'y', split_axis=0, concat_axis=0, tiled=True)  7.1 us
  transfers between devices with their start and end apart: 16, of which 7 were waited for; matrix products, arithmetic and copies ran while one was open for 2% of the time, Pallas kernels for 6%

profile of v3, /device:TPU:2, one launch (start us, length us, event | category | flops | bytes accessed | tf_op | source)
XLA Modules:
  0.0 262.3 jit_solution(4221575718998341277)
XLA Ops:
  9.9 0.9 convolution_add_fusion.2
  10.8 0.9 convolution_add_fusion.1
  12.6 2.1 multiply_convert_fusion.2
  14.8 1.6 copy-done.1
  16.4 0.9 copy-done.4
  17.3 2.7 %shard_map.139 = bf16[2048,384]{1,0:T(8,128)(2,1)} custom-call(s32[3]{0:T(128)S(1)} %pad_add_fusion.place, bf16[32,128,256]{2,1,0:T(8,128)(2,1)S(1)} %bitcast.49, bf16[384,256]{1,0:T(8,128)(2,1)S(1)} %copy-done.4), custom_call_target="tpu_custom_call" | custom-call | flops 402653184 | bytes 3145728 | tf_op jit(solution)/shard_map/pallas_call | solution.py:71
  20.0 1.9 collective-permute-start
  23.4 7.1 %all-to-all-start = ((bf16[8,16,384]{2,1,0:T(8,128)(2,1)}), bf16[8,16,384]{2,1,0:T(8,128)(2,1)S(1)}, u32[]{:S(2)}, u32[]{:S(2)}) async-start(bf16[8,16,384]{2,1,0:T(8,128)(2,1)} %bitcast.10), calls=%async_computation | async-start | bytes 196608 | tf_op jit(solution)/shard_map/all_to_all | solution.py:235
  30.6 2.4 shard_map.140
  33.0 1.1 copy-done.3
  34.2 5.4 %all-to-all-done = bf16[8,16,384]{2,1,0:T(8,128)(2,1)S(1)} async-done(((bf16[8,16,384]{2,1,0:T(8,128)(2,1)}), bf16[8,16,384]{2,1,0:T(8,128)(2,1)S(1)}, u32[]{:S(2)}, u32[]{:S(2)}) %all-to-all-start) | async-done | bytes 98336 | tf_op jit(solution)/shard_map/all_to_all | solution.py:235
  39.6 27.9 %all_gather.9.refs_0_ = bf16[512,384]{1,0:T(8,128)(2,1)S(1)} all-gather(bf16[128,384]{1,0:T(8,128)(2,1)S(1)} %bitcast.53), channel_id=1, replica_groups=mesh['zlo'=3,'y'=8,'zhi'=4,'x'=4,'core'=2] {'zhi'}, dimensions={0}, use_global_device_ids=true | all-gather | bytes 491520 | tf_op jit(solution)/shard_map/all_gather | solution.py:241
  67.5 2.6 collective-permute-start.6
  70.1 4.4 %collective-permute-start.4 = (bf16[512,384]{1,0:T(8,128)(2,1)S(1)}, bf16[512,384]{1,0:T(8,128)(2,1)S(1)}, u32[]{:S(2)}, u32[]{:S(2)}) collective-permute-start(bf16[512,384]{1,0:T(8,128)(2,1)S(1)} %all_gather.9.refs_0_), channel_id=1, source_target_pairs={{0,4},{2,6},{4,0},{6,2},{1,5},{3,7},{5,1},{7,3},{8,12},{10,14},{12... | collective-permute-start | bytes 1179656 | tf_op jit(solution)/shard_map/ppermute | solution.py:36
  74.5 3.8 %collective-permute-start.2 = (bf16[512,384]{1,0:T(8,128)(2,1)S(1)}, bf16[512,384]{1,0:T(8,128)(2,1)S(1)}, u32[]{:S(2)}, u32[]{:S(2)}) collective-permute-start(bf16[512,384]{1,0:T(8,128)(2,1)S(1)} %all_gather.9.refs_0_), channel_id=1, source_target_pairs={{0,2},{2,4},{4,6},{6,0},{1,3},{3,5},{5,7},{7,1},{8,10},{10,12},{12... | collective-permute-start | bytes 1179656 | tf_op jit(solution)/shard_map/ppermute | solution.py:36
  78.3 1.9 collective-permute-start.1
  80.3 1.6 collective-permute-done.6.refs_6_
  81.8 1.9 collective-permute-start.7
  83.8 6.5 %collective-permute-done.4.refs_4_ = bf16[512,384]{1,0:T(8,128)(2,1)S(1)} collective-permute-done((bf16[512,384]{1,0:T(8,128)(2,1)S(1)}, bf16[512,384]{1,0:T(8,128)(2,1)S(1)}, u32[]{:S(2)}, u32[]{:S(2)}) %collective-permute-start.4) | collective-permute-done | bytes 393248 | tf_op jit(solution)/shard_map/ppermute | solution.py:36
  90.3 1.9 collective-permute-start.5
  92.2 2.4 collective-permute-start.3
  96.3 5.2 %shard_map.141 = bf16[512,256]{1,0:T(8,128)(2,1)} custom-call(bf16[512,384]{1,0:T(8,128)(2,1)} %copy-done.7, bf16[512,384]{1,0:T(8,128)(2,1)} %copy-done.12, bf16[512,384]{1,0:T(8,128)(2,1)} %copy-done.11, bf16[512,384]{1,0:T(8,128)(2,1)} %collective-permute-done.3.refs_3_, bf16[512,384]{1,0:T(8,128)(2,1)} %copy-done.10, bf16[512,384]{1,0:T(8,128)(2,1)} %copy-done.14, ...), custom_call_target="tpu_custom_call" | custom-call | flops 805306368 | bytes 3407872 | tf_op jit(solution)/shard_map/pallas_call | solution.py:115
  101.7 4.8 %collective-permute-start.9 = (bf16[512,256]{1,0:T(8,128)(2,1)}, bf16[512,256]{1,0:T(8,128)(2,1)S(1)}, u32[]{:S(2)}, u32[]{:S(2)}) collective-permute-start(bf16[512,256]{1,0:T(8,128)(2,1)} %shard_map.141), channel_id=1, source_target_pairs={{0,512},{256,0},{512,256},{1,513},{257,1},{513,257},{2,514},{258,2... | collective-permute-start | bytes 786440 | tf_op jit(solution)/shard_map/ppermute | solution.py:36
  106.4 1.9 collective-permute-start.8
  108.4 5.7 %shard_map.142 = bf16[8,384,256]{2,1,0:T(8,128)(2,1)} custom-call(s32[3]{0:T(128)} %copy-done.6, bf16[32,128,256]{2,1,0:T(8,128)(2,1)} %bitcast.48, bf16[512,384]{1,0:T(8,128)(2,1)} %copy-done.7, bf16[512,384]{1,0:T(8,128)(2,1)} %copy-done.12, bf16[512,384]{1,0:T(8,128)(2,1)} %copy-done.11, bf16[512,384]{1,0:T(8,128)(2,1)} %collective-permute-done.3.refs_3_, ...), custom_call_target="tpu_custom_call" | custom-call | flops 805306368 | bytes 5242880 | tf_op jit(solution)/shard_map/pallas_call | solution.py:146
  114.1 5.0 %collective-permute-done.8 = bf16[512,256]{1,0:T(8,128)(2,1)S(1)} collective-permute-done((bf16[512,256]{1,0:T(8,128)(2,1)}, bf16[512,256]{1,0:T(8,128)(2,1)S(1)}, u32[]{:S(2)}, u32[]{:S(2)}) %collective-permute-start.8) | collective-permute-done | bytes 262176 | tf_op jit(solution)/shard_map/ppermute | solution.py:36
  119.9 6.8 %all-to-all-start.1 = ((bf16[8,384,256]{2,1,0:T(8,128)(2,1)}), bf16[8,384,256]{2,1,0:T(8,128)(2,1)S(1)}, u32[]{:S(2)}, u32[]{:S(2)}) async-start(bf16[8,384,256]{2,1,0:T(8,128)(2,1)} %shard_map.142), calls=%async_computation.2 | async-start | bytes 3145728 | tf_op jit(solution)/shard_map/all_to_all | solution.py:255
  126.6 12.7 %reduce-scatter.5.cloned.1.call-done = bf16[128,384]{1,0:T(8,128)(2,1)} async-done(((bf16[512,384]{1,0:T(8,128)(2,1)}), bf16[128,384]{1,0:T(8,128)(2,1)}) %reduce-scatter.5.cloned.1.call-update) | async-done | bytes 98320 | tf_op jit(solution)/shard_map/reduce_scatter | solution.py:253
  139.3 1.2 multiply_reduce_fusion
  142.5 23.2 %all-to-all-done.1 = bf16[8,384,256]{2,1,0:T(8,128)(2,1)S(1)} async-done(((bf16[8,384,256]{2,1,0:T(8,128)(2,1)}), bf16[8,384,256]{2,1,0:T(8,128)(2,1)S(1)}, u32[]{:S(2)}, u32[]{:S(2)}) %all-to-all-start.1) | async-done | bytes 1572896 | tf_op jit(solution)/shard_map/all_to_all | solution.py:255
  166.6 23.0 %all-gather.5.cloned.1.call-done = bf16[4096,256]{1,0:T(8,128)(2,1)} async-done(((bf16[512,256]{1,0:T(8,128)(2,1)}), bf16[4096,256]{1,0:T(8,128)(2,1)}) %all-gather.5.cloned.1.call-update) | async-done | bytes 2097168 | tf_op jit(solution)/shard_map/all_gather | solution.py:250
  189.6 65.6 %shard_map.143 = bf16[32,8,16,256]{3,2,1,0:T(8,128)(2,1)} custom-call(s32[3]{0:T(128)} %copy-done.6, bf16[8,32,16,256]{3,2,1,0:T(8,128)(2,1)} %bitcast.51), custom_call_target="tpu_custom_call" | custom-call | bytes 4194304 | tf_op jit(solution)/shard_map/pallas_call | solution.py:173
  (69 shorter events, 9.8 us)
Async XLA Ops:
  8.0 1.1 copy-start
  8.0 88.3 %all-gather.3.cloned.1.call-start = ((), (), s32[]{:S(2)}) async-start(), calls=%async_computation.4 | async-start | bytes 1769472 | tf_op jit(solution)/shard_map/all_gather | solution.py:229
  14.8 15.8 %copy-start.6 = (s32[3]{0:T(128)}, s32[3]{0:T(128)S(1)}, u32[]{:S(2)}) copy-start(s32[3]{0:T(128)S(1)} %pad_add_fusion.place) | copy-start | bytes 40
  14.8 1.6 copy-start.1
  16.4 0.9 copy-start.4
  17.3 4.6 %copy-start.16 = (bf16[384,3,128]{2,0,1:T(8,128)(2,1)S(1)}, bf16[384,3,128]{2,0,1:T(8,128)(2,1)}, u32[]{:S(2)}) copy-start(bf16[384,3,128]{2,0,1:T(8,128)(2,1)} %param.12) | copy-start | bytes 884740
  20.0 10.5 %collective-permute-start = (bf16[2048,384]{1,0:T(8,128)(2,1)}, bf16[2048,384]{1,0:T(8,128)(2,1)}, u32[]{:S(2)}, u32[]{:S(2)}) collective-permute-start(bf16[2048,384]{1,0:T(8,128)(2,1)} %shard_map.139), channel_id=1, source_target_pairs={{0,1},{1,0},{2,3},{3,2},{4,5},{5,4},{6,7},{7,6},{8,9},{9,8},{10,11... | collective-permute-start | bytes 4718600 | tf_op jit(solution)/shard_map/ppermute | solution.py:36
  22.4 8.2 %copy-start.2 = (bf16[4096,256]{1,0:T(8,128)(2,1)S(1)}, bf16[4096,256]{1,0:T(8,128)(2,1)}, u32[]{:S(2)}) copy-start(bf16[4096,256]{1,0:T(8,128)(2,1)} %param.13) | copy-start | bytes 6291460
  22.4 8.2 %copy-start.5 = (bf16[384,256]{1,0:T(8,128)(2,1)S(1)}, bf16[384,256]{1,0:T(8,128)(2,1)}, u32[]{:S(2)}) copy-start(bf16[384,256]{1,0:T(8,128)(2,1)} %get-tuple-element.35.gated) | copy-start | bytes 589828
  23.4 16.1 %all-to-all-start = ((bf16[8,16,384]{2,1,0:T(8,128)(2,1)}), bf16[8,16,384]{2,1,0:T(8,128)(2,1)S(1)}, u32[]{:S(2)}, u32[]{:S(2)}) async-start(bf16[8,16,384]{2,1,0:T(8,128)(2,1)} %bitcast.10), calls=%async_computation | async-start | bytes 196608 | tf_op jit(solution)/shard_map/all_to_all | solution.py:235
  30.5 71.1 %reduce-scatter.3.cloned.1.call-start = ((), (), s32[]{:S(2)}) async-start(), calls=%async_computation.5 | async-start | bytes 1966080 | tf_op jit(solution)/shard_map/reduce_scatter | solution.py:239
  33.0 1.1 copy-start.3
  39.6 99.8 %reduce-scatter.5.cloned.1.call-start = ((), (), s32[]{:S(2)}) async-start(), calls=%async_computation.6 | async-start | bytes 491520 | tf_op jit(solution)/shard_map/reduce_scatter | solution.py:253
  67.5 28.7 %copy-start.7 = (bf16[512,384]{1,0:T(8,128)(2,1)}, bf16[512,384]{1,0:T(8,128)(2,1)S(1)}, u32[]{:S(2)}) copy-start(bf16[512,384]{1,0:T(8,128)(2,1)S(1)} %all_gather.9.refs_0_) | copy-start | bytes 1179652
  67.5 14.3 %collective-permute-start.6 = (bf16[512,384]{1,0:T(8,128)(2,1)S(1)}, bf16[512,384]{1,0:T(8,128)(2,1)S(1)}, u32[]{:S(2)}, u32[]{:S(2)}) collective-permute-start(bf16[512,384]{1,0:T(8,128)(2,1)S(1)} %all_gather.9.refs_0_), channel_id=1, source_target_pairs={{0,6},{2,0},{4,2},{6,4},{1,7},{3,1},{5,3},{7,5},{8,14},{10,8},{12,... | collective-permute-start | bytes 1179656 | tf_op jit(solution)/shard_map/ppermute | solution.py:36
  70.1 20.1 %collective-permute-start.4 = (bf16[512,384]{1,0:T(8,128)(2,1)S(1)}, bf16[512,384]{1,0:T(8,128)(2,1)S(1)}, u32[]{:S(2)}, u32[]{:S(2)}) collective-permute-start(bf16[512,384]{1,0:T(8,128)(2,1)S(1)} %all_gather.9.refs_0_), channel_id=1, source_target_pairs={{0,4},{2,6},{4,0},{6,2},{1,5},{3,7},{5,1},{7,3},{8,12},{10,14},{12... | collective-permute-start | bytes 1179656 | tf_op jit(solution)/shard_map/ppermute | solution.py:36
  74.5 17.7 %collective-permute-start.2 = (bf16[512,384]{1,0:T(8,128)(2,1)S(1)}, bf16[512,384]{1,0:T(8,128)(2,1)S(1)}, u32[]{:S(2)}, u32[]{:S(2)}) collective-permute-start(bf16[512,384]{1,0:T(8,128)(2,1)S(1)} %all_gather.9.refs_0_), channel_id=1, source_target_pairs={{0,2},{2,4},{4,6},{6,0},{1,3},{3,5},{5,7},{7,1},{8,10},{10,12},{12... | collective-permute-start | bytes 1179656 | tf_op jit(solution)/shard_map/ppermute | solution.py:36
  78.3 16.3 %collective-permute-start.1 = (bf16[512,384]{1,0:T(8,128)(2,1)S(1)}, bf16[512,384]{1,0:T(8,128)(2,1)S(1)}, u32[]{:S(2)}, u32[]{:S(2)}) collective-permute-start(bf16[512,384]{1,0:T(8,128)(2,1)S(1)} %all_gather.9.refs_0_), channel_id=1, source_target_pairs={{0,1},{1,0},{2,3},{3,2},{4,5},{5,4},{6,7},{7,6},{8,9},{9,8},{10,11... | collective-permute-start | bytes 1179656 | tf_op jit(solution)/shard_map/ppermute | solution.py:36
  81.8 14.4 %copy-start.9 = (bf16[512,384]{1,0:T(8,128)(2,1)}, bf16[512,384]{1,0:T(8,128)(2,1)S(1)}, u32[]{:S(2)}) copy-start(bf16[512,384]{1,0:T(8,128)(2,1)S(1)} %collective-permute-done.6.refs_6_) | copy-start | bytes 1179652
  81.8 12.8 %collective-permute-start.7 = (bf16[512,384]{1,0:T(8,128)(2,1)S(1)}, bf16[512,384]{1,0:T(8,128)(2,1)S(1)}, u32[]{:S(2)}, u32[]{:S(2)}) collective-permute-start(bf16[512,384]{1,0:T(8,128)(2,1)S(1)} %collective-permute-done.6.refs_6_), channel_id=1, source_target_pairs={{0,1},{1,0},{2,3},{3,2},{4,5},{5,4},{6,7},{7,6},{8,9},{9,8},{10,11... | collective-permute-start | bytes 1179656 | tf_op jit(solution)/shard_map/ppermute | solution.py:36
  90.3 6.0 %copy-start.10 = (bf16[512,384]{1,0:T(8,128)(2,1)}, bf16[512,384]{1,0:T(8,128)(2,1)S(1)}, u32[]{:S(2)}) copy-start(bf16[512,384]{1,0:T(8,128)(2,1)S(1)} %collective-permute-done.4.refs_4_) | copy-start | bytes 1179652
  90.3 4.4 %collective-permute-start.5 = (bf16[512,384]{1,0:T(8,128)(2,1)S(1)}, bf16[512,384]{1,0:T(8,128)(2,1)S(1)}, u32[]{:S(2)}, u32[]{:S(2)}) collective-permute-start(bf16[512,384]{1,0:T(8,128)(2,1)S(1)} %collective-permute-done.4.refs_4_), channel_id=1, source_target_pairs={{0,1},{1,0},{2,3},{3,2},{4,5},{5,4},{6,7},{7,6},{8,9},{9,8},{10,11... | collective-permute-start | bytes 1179656 | tf_op jit(solution)/shard_map/ppermute | solution.py:36
  92.2 4.1 %copy-start.11 = (bf16[512,384]{1,0:T(8,128)(2,1)}, bf16[512,384]{1,0:T(8,128)(2,1)S(1)}, u32[]{:S(2)}) copy-start(bf16[512,384]{1,0:T(8,128)(2,1)S(1)} %collective-permute-done.2.refs_2_) | copy-start | bytes 1179652
  92.2 4.0 %collective-permute-start.3 = (bf16[512,384]{1,0:T(8,128)(2,1)S(1)}, bf16[512,384]{1,0:T(8,128)(2,1)}, u32[]{:S(2)}, u32[]{:S(2)}) collective-permute-start(bf16[512,384]{1,0:T(8,128)(2,1)S(1)} %collective-permute-done.2.refs_2_), channel_id=1, source_target_pairs={{0,1},{1,0},{2,3},{3,2},{4,5},{5,4},{6,7},{7,6},{8,9},{9,8},{10,11... | collective-permute-start | bytes 1179656 | tf_op jit(solution)/shard_map/ppermute | solution.py:36
  94.7 1.6 copy-start.12
  101.6 17.4 %copy-start.15 = (bf16[512,256]{1,0:T(8,128)(2,1)S(1)}, bf16[512,256]{1,0:T(8,128)(2,1)}, u32[]{:S(2)}) copy-start(bf16[512,256]{1,0:T(8,128)(2,1)} %shard_map.141) | copy-start | bytes 786436
  101.6 88.0 %all-gather.5.cloned.1.call-start = ((), (), s32[]{:S(2)}) async-start(), calls=%async_computation.7 | async-start | bytes 2359296 | tf_op jit(solution)/shard_map/all_gather | solution.py:250
  101.7 12.4 %collective-permute-start.9 = (bf16[512,256]{1,0:T(8,128)(2,1)}, bf16[512,256]{1,0:T(8,128)(2,1)S(1)}, u32[]{:S(2)}, u32[]{:S(2)}) collective-permute-start(bf16[512,256]{1,0:T(8,128)(2,1)} %shard_map.141), channel_id=1, source_target_pairs={{0,512},{256,0},{512,256},{1,513},{257,1},{513,257},{2,514},{258,2... | collective-permute-start | bytes 786440 | tf_op jit(solution)/shard_map/ppermute | solution.py:36
  106.4 12.6 %collective-permute-start.8 = (bf16[512,256]{1,0:T(8,128)(2,1)}, bf16[512,256]{1,0:T(8,128)(2,1)S(1)}, u32[]{:S(2)}, u32[]{:S(2)}) collective-permute-start(bf16[512,256]{1,0:T(8,128)(2,1)} %shard_map.141), channel_id=1, source_target_pairs={{0,256},{256,512},{512,0},{1,257},{257,513},{513,1},{2,258},{258,5... | collective-permute-start | bytes 786440 | tf_op jit(solution)/shard_map/ppermute | solution.py:36
  119.9 45.8 %all-to-all-start.1 = ((bf16[8,384,256]{2,1,0:T(8,128)(2,1)}), bf16[8,384,256]{2,1,0:T(8,128)(2,1)S(1)}, u32[]{:S(2)}, u32[]{:S(2)}) async-start(bf16[8,384,256]{2,1,0:T(8,128)(2,1)} %shard_map.142), calls=%async_computation.2 | async-start | bytes 3145728 | tf_op jit(solution)/shard_map/all_to_all | solution.py:255
  139.3 1.4 copy-start.17
  141.7 24.2 %copy-start.8 = (f32[384,256]{1,0:T(8,128)S(1)}, f32[384,256]{1,0:T(8,128)}, u32[]{:S(2)}) copy-start(f32[384,256]{1,0:T(8,128)} %get-tuple-element.36) | copy-start | bytes 1179652
  (3 other events, 2.5 us)
Sparse Core Ops, SparseCore 0:
  14.9 51.9 all-gather.2
  101.7 37.5 reduce-scatter.4
  142.0 47.5 all-gather.4
Sparse Core Ops, SparseCore 1:
  39.7 37.2 reduce-scatter.2

commit v4 on v3

--- a/solution.py
+++ b/solution.py
@@ -154,38 +154,42 @@
     )(place, weight, *pieces)
 
 
-def place_body(place, src, dst, sems):
+def place_body(place, src, dst, taken, given, in_sems, out_sems):
     x, core = place[0], place[1]
-    copies = []
+    loads = [pltpu.make_async_copy(src.at[y], taken.at[y], in_sems.at[y]) for y in range(NY)]
+    for load in loads:
+        load.start()
+    for load in loads:
+        load.wait()
+    stores = []
     for i in range(NX * NCORE * NZHI):
         s, c, z = i // (NCORE * NZHI), i // NZHI % NCORE, i % NZHI
         chip = lax.rem(x + NX - s, NX)
         head = (z * NX + chip) * NCORE + (core if c == 0 else 1 - core)
-        copies.append(pltpu.make_async_copy(src.at[:, i], dst.at[head], sems.at[i]))
-    for copy in copies:
-        copy.start()
-    for copy in copies:
-        copy.wait()
+        for y in range(NY):
+            given[i, y * SLAB : (y + 1) * SLAB, :] = taken[y, i * SLAB : (i + 1) * SLAB, :]
+        stores.append(pltpu.make_async_copy(given.at[i], dst.at[head], out_sems.at[i]))
+        stores[-1].start()
+    for store in stores:
+        store.wait()
 
 
 def put_heads(place, total):
     heads, width = NX * NCORE * NZHI, total.shape[1]
     return call(
         place_body,
-        jax.ShapeDtypeStruct((heads, NY, SLAB, width), BF),
+        jax.ShapeDtypeStruct((heads, HEAD, width), BF),
         [SMEM, HBM],
         HBM,
         0,
         4 * total.size,
-        [pltpu.SemaphoreType.DMA((heads,))],
-    )(place, total.reshape(NY, heads, SLAB, width)).reshape(total.shape)
-
-
-def fold_zlo(value):
-    total = value.astype(F32)
-    for s in range(1, NZLO):
-        total = total + shift(value, "zlo", NZLO, s).astype(F32)
-    return total.astype(BF)
+        [
+            pltpu.VMEM((NY, heads * SLAB, width), BF),
+            pltpu.VMEM((heads, HEAD, width), BF),
+            pltpu.SemaphoreType.DMA((NY,)),
+            pltpu.SemaphoreType.DMA((heads,)),
+        ],
+    )(place, total.reshape(NY, heads * SLAB, width)).reshape(total.shape)
 
 
 def on_device(
@@ -220,20 +224,21 @@
     rounded = probs.astype(BF)
     attended = dot(values, rounded, ((0,), (1,))).astype(BF)
 
+    ids = (step_ids, gsd_ids, sensor_ids, bucket_ids)
+    attended, *ids = lax.optimization_barrier((attended, *ids))
+    step_ids, gsd_ids, sensor_ids, bucket_ids = ids
     gate_scene = lookup(step_ids, step_table) + lookup(gsd_ids, gsd_table)
     gate_scene = gate_scene + lookup(sensor_ids, sensor_table) + lookup(bucket_ids, bucket_table)
     member = (segments[:, None] == jnp.arange(scene_lengths.shape[0])[None, :]).astype(F32)
     gate = jnp.dot(member, gate_scene, precision=lax.Precision.HIGHEST, preferred_element_type=F32)
     gated = (gate * cotangent.astype(F32)).astype(BF)
 
+    attended, gated = lax.optimization_barrier((attended, gated))
     gated_y = lax.all_gather(gated, "y", axis=0, tiled=True)
+    attended = lax.all_to_all(attended, "y", split_axis=0, concat_axis=0, tiled=True)
 
     sent = upstream_part(place, weight, gated)
     got = shift(sent, "core", NCORE, 1)
-
-    attended, sent = lax.optimization_barrier((attended, sent))
-    attended = lax.all_to_all(attended, "y", split_axis=0, concat_axis=0, tiled=True)
-
     summed = upstream_part(place, weight, gated, got)
     attended, summed = lax.optimization_barrier((attended, summed))
     summed = lax.psum_scatter(summed, "x", scatter_dimension=0, tiled=True)
@@ -242,16 +247,17 @@
     for s in (1, 3, 2):
         own[s] = shift(own[0], "x", NX, s)
     pieces = [p for s in range(NX) for p in (own[s], shift(own[s], "core", NCORE, 1))]
+    *pieces, summed = lax.optimization_barrier((*pieces, summed))
 
     total = weight_part(pieces, gated_y)
-    *pieces, total, summed = lax.optimization_barrier((*pieces, total, summed))
-    parts = mix_part(place, weight, pieces)
-    total, parts = lax.optimization_barrier((fold_zlo(total), parts))
+    total = lax.all_gather(total, "zlo").astype(F32).sum(0).astype(BF)
+    *pieces, total = lax.optimization_barrier((*pieces, total))
     total = lax.all_gather(total, "y", axis=0, tiled=True)
     total = put_heads(place, total)
 
     summed = lax.psum_scatter(summed, "zhi", scatter_dimension=0, tiled=True)
 
+    parts = mix_part(place, weight, pieces)
     parts = lax.all_to_all(parts, "y", split_axis=0, concat_axis=0, tiled=True)
     mixed = (gate * parts.astype(F32).sum(0)).astype(BF)
 

time: 263 us -> 203 us (0.77)
  the two profiles are of different devices: /device:TPU:2 before, /device:TPU:8 now
where the time goes in v4:
time: 203 us; the launch traced here: 202 us
  waiting for transfers between devices  70.5 us (35%)
  starting transfers between devices  41.7 us (21%)
  blocking collectives  40.2 us (20%)
  Pallas kernels  19.8 us (10%)
  between operations  15.9 us (8%)
  matrix products  6.37 us (3%)
  other arithmetic  3.89 us (2%)
  local copies, waits for them, and re-layouts  3.69 us (2%)
    all_to_all x1, waiting for transfers between devices, on_device(): parts = lax.all_to_all(parts, 'y', split_axis=0, concat_axis=0, tiled=True)  47.7 us
    ppermute x8, starting transfers between devices, shift(): lax.ppermute(value, axis, [(i, (i + step) % size) for i in range(size)])  21.4 us
    all_gather x1, blocking collectives, on_device(): own = {0: lax.all_gather(attended, 'zhi', axis=0, tiled=True)}  21 us
    all_gather x1, blocking collectives, on_device(): total = lax.all_gather(total, 'zlo').astype(F32).sum(0).astype(BF)  19.2 us
    all_to_all x1, starting transfers between devices, on_device(): lax.all_to_all(attended, 'y', split_axis=0, concat_axis=0, tiled=True)  12.7 us
    ppermute x8, waiting for transfers between devices, shift(): lax.ppermute(value, axis, [(i, (i + step) % size) for i in range(size)])  10.7 us
    all_to_all x1, starting transfers between devices, on_device(): parts = lax.all_to_all(parts, 'y', split_axis=0, concat_axis=0, tiled=True)  7.42 us
    all_gather x1, waiting for transfers between devices, on_device(): total = lax.all_gather(total, 'y', axis=0, tiled=True)  7.35 us
  transfers between devices with their start and end apart: 14, of which 5 were waited for; matrix products, arithmetic and copies ran while one was open for 3% of the time, Pallas kernels for 7%

profile of v4, /device:TPU:8, one launch (start us, length us, event | category | flops | bytes accessed | tf_op | source)
XLA Modules:
  0.0 202.0 jit_solution(3266507006835056352)
XLA Ops:
  8.0 0.9 reduce-window.8
  9.0 1.2 fusion.33
  10.4 1.3 fusion.3
  12.6 1.1 multiply_convert_fusion.2
  13.8 2.7 %shard_map.139 = bf16[2048,384]{1,0:T(8,128)(2,1)} custom-call(s32[3]{0:T(128)S(1)} %pad_add_fusion.place, bf16[32,128,256]{2,1,0:T(8,128)(2,1)S(1)} %bitcast.50, bf16[384,256]{1,0:T(8,128)(2,1)S(1)} %get-tuple-element.36.gated), custom_call_target="tpu_custom_call" | custom-call | flops 402653184 | bytes 3145728 | tf_op jit(solution)/shard_map/pallas_call | solution.py:71
  16.5 1.9 collective-permute-start
  18.4 0.8 copy.17
  19.1 12.7 %all-to-all-start = ((bf16[8,16,384]{2,1,0:T(8,128)(2,1)}), bf16[8,16,384]{2,1,0:T(8,128)(2,1)S(1)}, u32[]{:S(2)}, u32[]{:S(2)}) async-start(bf16[8,16,384]{2,1,0:T(8,128)(2,1)} %bitcast.10), calls=%async_computation | async-start | bytes 196608 | tf_op jit(solution)/shard_map/all_to_all | solution.py:238
  31.9 2.4 %shard_map.140 = bf16[2048,384]{1,0:T(8,128)(2,1)S(1)} custom-call(s32[3]{0:T(128)S(1)} %pad_add_fusion.place, bf16[32,128,256]{2,1,0:T(8,128)(2,1)S(1)} %bitcast.51, bf16[384,256]{1,0:T(8,128)(2,1)S(1)} %get-tuple-element.36.gated, bf16[2048,384]{1,0:T(8,128)(2,1)} %collective-permute-done.refs_0_), custom_call_target="tpu_custom_call" | custom-call | flops 402653184 | bytes 3145728 | tf_op jit(solution)/shard_map/pallas_call | solution.py:71
  34.3 1.1 copy-done.2
  35.4 4.1 %all-to-all-done = bf16[8,16,384]{2,1,0:T(8,128)(2,1)S(1)} async-done(((bf16[8,16,384]{2,1,0:T(8,128)(2,1)}), bf16[8,16,384]{2,1,0:T(8,128)(2,1)S(1)}, u32[]{:S(2)}, u32[]{:S(2)}) %all-to-all-start) | async-done | bytes 98336 | tf_op jit(solution)/shard_map/all_to_all | solution.py:238
  40.2 21.0 %all_gather.15.refs_0_ = bf16[512,384]{1,0:T(8,128)(2,1)S(1)} all-gather(bf16[128,384]{1,0:T(8,128)(2,1)S(1)} %bitcast.55), channel_id=1, replica_groups=mesh['zlo'=3,'y'=8,'zhi'=4,'x'=4,'core'=2] {'zhi'}, dimensions={0}, use_global_device_ids=true | all-gather | bytes 491520 | tf_op jit(solution)/shard_map/all_gather | solution.py:246
  61.2 3.4 %collective-permute-start.2 = (bf16[512,384]{1,0:T(8,128)(2,1)S(1)}, bf16[512,384]{1,0:T(8,128)(2,1)S(1)}, u32[]{:S(2)}, u32[]{:S(2)}) collective-permute-start(bf16[512,384]{1,0:T(8,128)(2,1)S(1)} %all_gather.15.refs_0_), channel_id=1, source_target_pairs={{0,2},{2,4},{4,6},{6,0},{1,3},{3,5},{5,7},{7,1},{8,10},{10,12},{12... | collective-permute-start | bytes 1179656 | tf_op jit(solution)/shard_map/ppermute | solution.py:36
  64.6 4.6 %collective-permute-start.4 = (bf16[512,384]{1,0:T(8,128)(2,1)S(1)}, bf16[512,384]{1,0:T(8,128)(2,1)S(1)}, u32[]{:S(2)}, u32[]{:S(2)}) collective-permute-start(bf16[512,384]{1,0:T(8,128)(2,1)S(1)} %all_gather.15.refs_0_), channel_id=1, source_target_pairs={{0,4},{2,6},{4,0},{6,2},{1,5},{3,7},{5,1},{7,3},{8,12},{10,14},{12... | collective-permute-start | bytes 1179656 | tf_op jit(solution)/shard_map/ppermute | solution.py:36
  69.2 3.3 %collective-permute-start.6 = (bf16[512,384]{1,0:T(8,128)(2,1)S(1)}, bf16[512,384]{1,0:T(8,128)(2,1)S(1)}, u32[]{:S(2)}, u32[]{:S(2)}) collective-permute-start(bf16[512,384]{1,0:T(8,128)(2,1)S(1)} %all_gather.15.refs_0_), channel_id=1, source_target_pairs={{0,6},{2,0},{4,2},{6,4},{1,7},{3,1},{5,3},{7,5},{8,14},{10,8},{12,... | collective-permute-start | bytes 1179656 | tf_op jit(solution)/shard_map/ppermute | solution.py:36
  72.6 1.9 collective-permute-start.1
  74.5 4.5 %collective-permute-done.2.refs_2_ = bf16[512,384]{1,0:T(8,128)(2,1)S(1)} collective-permute-done((bf16[512,384]{1,0:T(8,128)(2,1)S(1)}, bf16[512,384]{1,0:T(8,128)(2,1)S(1)}, u32[]{:S(2)}, u32[]{:S(2)}) %collective-permute-start.2) | collective-permute-done | bytes 393248 | tf_op jit(solution)/shard_map/ppermute | solution.py:36
  79.0 1.9 collective-permute-start.3
  80.9 6.2 %collective-permute-done.4.refs_4_ = bf16[512,384]{1,0:T(8,128)(2,1)S(1)} collective-permute-done((bf16[512,384]{1,0:T(8,128)(2,1)S(1)}, bf16[512,384]{1,0:T(8,128)(2,1)S(1)}, u32[]{:S(2)}, u32[]{:S(2)}) %collective-permute-start.4) | collective-permute-done | bytes 393248 | tf_op jit(solution)/shard_map/ppermute | solution.py:36
  87.1 1.9 collective-permute-start.5
  89.1 2.4 %collective-permute-start.7 = (bf16[512,384]{1,0:T(8,128)(2,1)S(1)}, bf16[512,384]{1,0:T(8,128)(2,1)}, u32[]{:S(2)}, u32[]{:S(2)}) collective-permute-start(bf16[512,384]{1,0:T(8,128)(2,1)S(1)} %collective-permute-done.6.refs_6_), channel_id=1, source_target_pairs={{0,1},{1,0},{2,3},{3,2},{4,5},{5,4},{6,7},{7,6},{8,9},{9,8},{10,11... | collective-permute-start | bytes 1179656 | tf_op jit(solution)/shard_map/ppermute | solution.py:36
  91.5 0.8 copy-done.11
  93.2 5.2 %shard_map.141 = bf16[512,256]{1,0:T(8,128)(2,1)} custom-call(bf16[512,384]{1,0:T(8,128)(2,1)} %copy-done.5, bf16[512,384]{1,0:T(8,128)(2,1)} %copy-done.10, bf16[512,384]{1,0:T(8,128)(2,1)} %copy-done.7, bf16[512,384]{1,0:T(8,128)(2,1)} %copy-done.11, bf16[512,384]{1,0:T(8,128)(2,1)} %copy-done.8, bf16[512,384]{1,0:T(8,128)(2,1)} %copy-done.12, ...), custom_call_target="tpu_custom_call" | custom-call | flops 805306368 | bytes 3407872 | tf_op jit(solution)/shard_map/pallas_call | solution.py:115
  98.4 19.2 %all-gather = bf16[1536,256]{1,0:T(8,128)(2,1)S(1)} all-gather(bf16[512,256]{1,0:T(8,128)(2,1)} %shard_map.141), channel_id=2, replica_groups=mesh['zlo'=3,'y'=8,'zhi'=4,'x'=4,'core'=2] {'zlo'}, dimensions={0}, use_global_device_ids=true | all-gather | bytes 1048576 | tf_op jit(solution)/shard_map/all_gather | solution.py:253
  117.6 0.9 reduce_sum.50
  118.5 5.7 %shard_map.142 = bf16[8,384,256]{2,1,0:T(8,128)(2,1)} custom-call(s32[3]{0:T(128)} %copy-done.4, bf16[32,128,256]{2,1,0:T(8,128)(2,1)} %bitcast.49, bf16[512,384]{1,0:T(8,128)(2,1)} %copy-done.5, bf16[512,384]{1,0:T(8,128)(2,1)} %copy-done.10, bf16[512,384]{1,0:T(8,128)(2,1)} %copy-done.7, bf16[512,384]{1,0:T(8,128)(2,1)} %copy-done.11, ...), custom_call_target="tpu_custom_call" | custom-call | flops 805306368 | bytes 5242880 | tf_op jit(solution)/shard_map/pallas_call | solution.py:146
  124.2 7.4 %all-to-all-start.1 = ((bf16[8,384,256]{2,1,0:T(8,128)(2,1)}), bf16[8,384,256]{2,1,0:T(8,128)(2,1)S(1)}, u32[]{:S(2)}, u32[]{:S(2)}) async-start(bf16[8,384,256]{2,1,0:T(8,128)(2,1)} %shard_map.142), calls=%async_computation.2 | async-start | bytes 3145728 | tf_op jit(solution)/shard_map/all_to_all | solution.py:261
  131.7 1.1 multiply_reduce_fusion
  134.0 0.7 pad_maximum_fusion
  134.7 47.7 %all-to-all-done.1 = bf16[8,384,256]{2,1,0:T(8,128)(2,1)S(1)} async-done(((bf16[8,384,256]{2,1,0:T(8,128)(2,1)}), bf16[8,384,256]{2,1,0:T(8,128)(2,1)S(1)}, u32[]{:S(2)}, u32[]{:S(2)}) %all-to-all-start.1) | async-done | bytes 1572896 | tf_op jit(solution)/shard_map/all_to_all | solution.py:261
  183.4 7.4 %all-gather.6.cloned.1.call-done = bf16[4096,256]{1,0:T(8,128)(2,1)} async-done(((bf16[512,256]{1,0:T(8,128)(2,1)}), bf16[4096,256]{1,0:T(8,128)(2,1)}) %all-gather.6.cloned.1.call-update) | async-done | bytes 2097168 | tf_op jit(solution)/shard_map/all_gather | solution.py:255
  190.8 3.8 %shard_map.143 = bf16[32,128,256]{2,1,0:T(8,128)(2,1)} custom-call(s32[3]{0:T(128)} %copy-done.4, bf16[8,512,256]{2,1,0:T(8,128)(2,1)} %bitcast.53), custom_call_target="tpu_custom_call" | custom-call | bytes 4194304 | tf_op jit(solution)/shard_map/pallas_call | solution.py:179
  (74 shorter events, 4.7 us)
Async XLA Ops:
  8.0 3.8 %copy-start = (bf16[1000,256]{1,0:T(8,128)(2,1)S(1)}, bf16[1000,256]{1,0:T(8,128)(2,1)}, u32[]{:S(2)}) copy-start(bf16[1000,256]{1,0:T(8,128)(2,1)} %param.20) | copy-start | bytes 1536004
  10.3 1.7 copy-start.17
  10.4 1.7 copy-start.20
  10.4 1.8 copy-start.18
  10.4 1.8 copy-start.21
  10.4 2.0 copy-start.19
  10.4 2.0 copy-start.22
  10.4 2.2 %copy-start.13 = (bf16[384,256]{1,0:T(8,128)(2,1)S(1)}, bf16[384,256]{1,0:T(8,128)(2,1)}, u32[]{:S(2)}) copy-start(bf16[384,256]{1,0:T(8,128)(2,1)} %param.14) | copy-start | bytes 589828
  10.4 3.4 %copy-start.1 = (bf16[4096,256]{1,0:T(8,128)(2,1)S(1)}, bf16[4096,256]{1,0:T(8,128)(2,1)}, u32[]{:S(2)}) copy-start(bf16[4096,256]{1,0:T(8,128)(2,1)} %param.13) | copy-start | bytes 6291460
  13.7 18.2 %copy-start.3 = (bf16[384,256]{1,0:T(8,128)(2,1)}, bf16[384,256]{1,0:T(8,128)(2,1)S(1)}, u32[]{:S(2)}) copy-start(bf16[384,256]{1,0:T(8,128)(2,1)S(1)} %get-tuple-element.36.gated) | copy-start | bytes 589828
  13.8 18.1 %copy-start.4 = (s32[3]{0:T(128)}, s32[3]{0:T(128)S(1)}, u32[]{:S(2)}) copy-start(s32[3]{0:T(128)S(1)} %pad_add_fusion.place) | copy-start | bytes 40
  16.5 15.4 %collective-permute-start = (bf16[2048,384]{1,0:T(8,128)(2,1)}, bf16[2048,384]{1,0:T(8,128)(2,1)}, u32[]{:S(2)}, u32[]{:S(2)}) collective-permute-start(bf16[2048,384]{1,0:T(8,128)(2,1)} %shard_map.139), channel_id=1, source_target_pairs={{0,1},{1,0},{2,3},{3,2},{4,5},{5,4},{6,7},{7,6},{8,9},{9,8},{10,11... | collective-permute-start | bytes 4718600 | tf_op jit(solution)/shard_map/ppermute | solution.py:36
  19.1 20.4 %all-to-all-start = ((bf16[8,16,384]{2,1,0:T(8,128)(2,1)}), bf16[8,16,384]{2,1,0:T(8,128)(2,1)S(1)}, u32[]{:S(2)}, u32[]{:S(2)}) async-start(bf16[8,16,384]{2,1,0:T(8,128)(2,1)} %bitcast.10), calls=%async_computation | async-start | bytes 196608 | tf_op jit(solution)/shard_map/all_to_all | solution.py:238
  31.9 61.2 %reduce-scatter.3.cloned.1.call-start = ((), (), s32[]{:S(2)}) async-start(), calls=%async_computation.4 | async-start | bytes 1966080 | tf_op jit(solution)/shard_map/reduce_scatter | solution.py:244
  39.6 53.5 %all-gather.4.cloned.1.call-start = ((), (), s32[]{:S(2)}) async-start(), calls=%async_computation.5 | async-start | bytes 1769472 | tf_op jit(solution)/shard_map/all_gather | solution.py:237
  40.2 91.5 %reduce-scatter.5.cloned.1.call-start = ((), (), s32[]{:S(2)}) async-start(), calls=%async_computation.6 | async-start | bytes 491520 | tf_op jit(solution)/shard_map/reduce_scatter | solution.py:258
  61.2 32.0 %copy-start.5 = (bf16[512,384]{1,0:T(8,128)(2,1)}, bf16[512,384]{1,0:T(8,128)(2,1)S(1)}, u32[]{:S(2)}) copy-start(bf16[512,384]{1,0:T(8,128)(2,1)S(1)} %all_gather.15.refs_0_) | copy-start | bytes 1179652
  61.2 17.9 %collective-permute-start.2 = (bf16[512,384]{1,0:T(8,128)(2,1)S(1)}, bf16[512,384]{1,0:T(8,128)(2,1)S(1)}, u32[]{:S(2)}, u32[]{:S(2)}) collective-permute-start(bf16[512,384]{1,0:T(8,128)(2,1)S(1)} %all_gather.15.refs_0_), channel_id=1, source_target_pairs={{0,2},{2,4},{4,6},{6,0},{1,3},{3,5},{5,7},{7,1},{8,10},{10,12},{12... | collective-permute-start | bytes 1179656 | tf_op jit(solution)/shard_map/ppermute | solution.py:36
  64.6 22.6 %collective-permute-start.4 = (bf16[512,384]{1,0:T(8,128)(2,1)S(1)}, bf16[512,384]{1,0:T(8,128)(2,1)S(1)}, u32[]{:S(2)}, u32[]{:S(2)}) collective-permute-start(bf16[512,384]{1,0:T(8,128)(2,1)S(1)} %all_gather.15.refs_0_), channel_id=1, source_target_pairs={{0,4},{2,6},{4,0},{6,2},{1,5},{3,7},{5,1},{7,3},{8,12},{10,14},{12... | collective-permute-start | bytes 1179656 | tf_op jit(solution)/shard_map/ppermute | solution.py:36
  69.2 19.8 %collective-permute-start.6 = (bf16[512,384]{1,0:T(8,128)(2,1)S(1)}, bf16[512,384]{1,0:T(8,128)(2,1)S(1)}, u32[]{:S(2)}, u32[]{:S(2)}) collective-permute-start(bf16[512,384]{1,0:T(8,128)(2,1)S(1)} %all_gather.15.refs_0_), channel_id=1, source_target_pairs={{0,6},{2,0},{4,2},{6,4},{1,7},{3,1},{5,3},{7,5},{8,14},{10,8},{12,... | collective-permute-start | bytes 1179656 | tf_op jit(solution)/shard_map/ppermute | solution.py:36
  72.6 18.9 %collective-permute-start.1 = (bf16[512,384]{1,0:T(8,128)(2,1)S(1)}, bf16[512,384]{1,0:T(8,128)(2,1)S(1)}, u32[]{:S(2)}, u32[]{:S(2)}) collective-permute-start(bf16[512,384]{1,0:T(8,128)(2,1)S(1)} %all_gather.15.refs_0_), channel_id=1, source_target_pairs={{0,1},{1,0},{2,3},{3,2},{4,5},{5,4},{6,7},{7,6},{8,9},{9,8},{10,11... | collective-permute-start | bytes 1179656 | tf_op jit(solution)/shard_map/ppermute | solution.py:36
  79.0 14.1 %copy-start.7 = (bf16[512,384]{1,0:T(8,128)(2,1)}, bf16[512,384]{1,0:T(8,128)(2,1)S(1)}, u32[]{:S(2)}) copy-start(bf16[512,384]{1,0:T(8,128)(2,1)S(1)} %collective-permute-done.2.refs_2_) | copy-start | bytes 1179652
  79.0 12.5 %collective-permute-start.3 = (bf16[512,384]{1,0:T(8,128)(2,1)S(1)}, bf16[512,384]{1,0:T(8,128)(2,1)S(1)}, u32[]{:S(2)}, u32[]{:S(2)}) collective-permute-start(bf16[512,384]{1,0:T(8,128)(2,1)S(1)} %collective-permute-done.2.refs_2_), channel_id=1, source_target_pairs={{0,1},{1,0},{2,3},{3,2},{4,5},{5,4},{6,7},{7,6},{8,9},{9,8},{10,11... | collective-permute-start | bytes 1179656 | tf_op jit(solution)/shard_map/ppermute | solution.py:36
  87.1 6.0 %copy-start.8 = (bf16[512,384]{1,0:T(8,128)(2,1)}, bf16[512,384]{1,0:T(8,128)(2,1)S(1)}, u32[]{:S(2)}) copy-start(bf16[512,384]{1,0:T(8,128)(2,1)S(1)} %collective-permute-done.4.refs_4_) | copy-start | bytes 1179652
  87.1 4.4 %collective-permute-start.5 = (bf16[512,384]{1,0:T(8,128)(2,1)S(1)}, bf16[512,384]{1,0:T(8,128)(2,1)S(1)}, u32[]{:S(2)}, u32[]{:S(2)}) collective-permute-start(bf16[512,384]{1,0:T(8,128)(2,1)S(1)} %collective-permute-done.4.refs_4_), channel_id=1, source_target_pairs={{0,1},{1,0},{2,3},{3,2},{4,5},{5,4},{6,7},{7,6},{8,9},{9,8},{10,11... | collective-permute-start | bytes 1179656 | tf_op jit(solution)/shard_map/ppermute | solution.py:36
  89.0 4.1 %copy-start.9 = (bf16[512,384]{1,0:T(8,128)(2,1)}, bf16[512,384]{1,0:T(8,128)(2,1)S(1)}, u32[]{:S(2)}) copy-start(bf16[512,384]{1,0:T(8,128)(2,1)S(1)} %collective-permute-done.6.refs_6_) | copy-start | bytes 1179652
  89.1 4.0 %collective-permute-start.7 = (bf16[512,384]{1,0:T(8,128)(2,1)S(1)}, bf16[512,384]{1,0:T(8,128)(2,1)}, u32[]{:S(2)}, u32[]{:S(2)}) collective-permute-start(bf16[512,384]{1,0:T(8,128)(2,1)S(1)} %collective-permute-done.6.refs_6_), channel_id=1, source_target_pairs={{0,1},{1,0},{2,3},{3,2},{4,5},{5,4},{6,7},{7,6},{8,9},{9,8},{10,11... | collective-permute-start | bytes 1179656 | tf_op jit(solution)/shard_map/ppermute | solution.py:36
  91.5 1.7 copy-start.10
  93.1 97.7 %all-gather.6.cloned.1.call-start = ((), (), s32[]{:S(2)}) async-start(), calls=%async_computation.7 | async-start | bytes 2359296 | tf_op jit(solution)/shard_map/all_gather | solution.py:255
  124.2 7.4 %copy-start.14 = (bf16[384,3,128]{2,0,1:T(8,128)(2,1)S(1)}, bf16[384,3,128]{2,0,1:T(8,128)(2,1)}, u32[]{:S(2)}) copy-start(bf16[384,3,128]{2,0,1:T(8,128)(2,1)} %param.12) | copy-start | bytes 884740
  124.2 58.2 %all-to-all-start.1 = ((bf16[8,384,256]{2,1,0:T(8,128)(2,1)}), bf16[8,384,256]{2,1,0:T(8,128)(2,1)S(1)}, u32[]{:S(2)}, u32[]{:S(2)}) async-start(bf16[8,384,256]{2,1,0:T(8,128)(2,1)} %shard_map.142), calls=%async_computation.2 | async-start | bytes 3145728 | tf_op jit(solution)/shard_map/all_to_all | solution.py:261
  134.0 48.7 %copy-start.6 = (f32[384,256]{1,0:T(8,128)S(1)}, f32[384,256]{1,0:T(8,128)}, u32[]{:S(2)}) copy-start(f32[384,256]{1,0:T(8,128)} %get-tuple-element.60) | copy-start | bytes 1179652
  (5 other events, 5.1 us)
Sparse Core Ops, SparseCore 0:
  39.7 35.4 reduce-scatter.2
  93.2 35.6 reduce-scatter.4
Sparse Core Ops, SparseCore 1:
  43.3 42.2 all-gather.3
  118.6 72.1 all-gather.5

commit v5 on v4

--- a/solution.py
+++ b/solution.py
@@ -87,11 +87,6 @@
         copy.wait()
 
 
-def fetch_scratch(pieces):
-    count = len(pieces)
-    return [pltpu.VMEM((count, *pieces[0].shape), BF), pltpu.SemaphoreType.DMA((count,))]
-
-
 def slabs(held, y):
     starts = [z * HEAD + y * SLAB for z in range(NZHI)]
     return jnp.concatenate(
@@ -100,58 +95,65 @@
 
 
 def part_body(*refs):
-    *pieces, gated, out, acc, held, sems = refs
+    *pieces, mine, theirs, out_mine, out_theirs, rows, sems, held = refs
     fetch(pieces, held, sems)
     toks = held.shape[2]
     for y in range(NY):
-        value = dot(slabs(held, y), gated[y * toks : (y + 1) * toks, :], ((1,), (0,)))
-        acc[...] = value if y == 0 else acc[...] + value
-    out[...] = acc[...].astype(BF)
-
-
-def weight_part(pieces, gated):
+        rows[:, y * toks : (y + 1) * toks] = slabs(held, y)
+    out_theirs[...] = dot(rows[...], theirs[...], ((1,), (0,))).astype(BF)
+    out_mine[...] = dot(rows[...], mine[...], ((1,), (0,))).astype(BF)
+
+
+def weight_part(pieces, mine, theirs):
     rows = sum(p.shape[0] for p in pieces) // NY
-    toks, width = gated.shape
+    toks, width = mine.shape
+    count = len(pieces)
     return call(
         part_body,
-        jax.ShapeDtypeStruct((rows, width), BF),
-        [HBM] * len(pieces) + [VMEM],
-        VMEM,
-        2 * rows * toks * width,
-        2 * rows * (toks + width),
-        [pltpu.VMEM((rows, width), F32)] + fetch_scratch(pieces),
-    )(*pieces, gated)
-
-
-def mix_body(place, weight, *refs):
-    *pieces, out, held, sems = refs
+        (jax.ShapeDtypeStruct((rows, width), BF),) * 2,
+        [HBM] * count + [VMEM] * 2,
+        (VMEM, VMEM),
+        4 * rows * toks * width,
+        2 * rows * toks + 4 * toks * width,
+        [
+            pltpu.VMEM((rows, toks), BF),
+            pltpu.SemaphoreType.DMA((count,)),
+            pltpu.VMEM((count, *pieces[0].shape), BF),
+        ],
+    )(*pieces, mine, theirs)
+
+
+def mix_body(place, weight, gate, *refs):
+    *pieces, out, acc, sems, held = refs
     fetch(pieces, held, sems)
-    x, core, mine = place[0], place[1], place[2]
-    rows = []
+    x, core = place[0], place[1]
     for i in range(len(pieces)):
         s, c = i // 2, i % 2
         chip = lax.rem(x + NX - s, NX)
         pick = core if c == 0 else 1 - core
-        for z in range(NZHI):
-            start = pl.multiple_of(mine * SLAB, SLAB)
-            rows.append(weight[(z * NX + chip) * NCORE + pick, pl.ds(start, SLAB), :])
-    rows = jnp.concatenate(rows)
-    for y in range(NY):
-        out[y] = dot(slabs(held, y), rows, ((0,), (0,))).astype(BF)
-
-
-def mix_part(place, weight, pieces):
-    toks, width = pieces[0].shape[1], weight.shape[2]
+        rows = jnp.concatenate([weight[(z * NX + chip) * NCORE + pick] for z in range(NZHI)])
+        value = dot(held[i], rows, ((0,), (0,)))
+        acc[...] = value if i == 0 else acc[...] + value
+    out[...] = (gate[...] * acc[...]).astype(BF)
+
+
+def mix(place, weight, gate, pieces):
+    toks, width = gate.shape
     rows = sum(p.shape[0] for p in pieces)
+    count = len(pieces)
     return call(
         mix_body,
-        jax.ShapeDtypeStruct((NY, toks, width), BF),
-        [SMEM, VMEM] + [HBM] * len(pieces),
+        jax.ShapeDtypeStruct((toks, width), BF),
+        [SMEM] + [VMEM] * 2 + [HBM] * count,
         VMEM,
         2 * rows * toks * width,
         2 * rows * (toks + width),
-        fetch_scratch(pieces),
-    )(place, weight, *pieces)
+        [
+            pltpu.VMEM((toks, width), F32),
+            pltpu.SemaphoreType.DMA((count,)),
+            pltpu.VMEM((count, *pieces[0].shape), BF),
+        ],
+    )(place, weight, gate, *pieces)
 
 
 def place_body(place, src, dst, taken, given, in_sems, out_sems):
@@ -163,7 +165,7 @@
         load.wait()
     stores = []
     for i in range(NX * NCORE * NZHI):
-        s, c, z = i // (NCORE * NZHI), i // NZHI % NCORE, i % NZHI
+        c, s, z = i // (NX * NZHI), i // NZHI % NX, i % NZHI
         chip = lax.rem(x + NX - s, NX)
         head = (z * NX + chip) * NCORE + (core if c == 0 else 1 - core)
         for y in range(NY):
@@ -209,7 +211,7 @@
     toks = qkv.shape[0]
     width = cotangent.shape[1]
     factor = HEAD ** (-0.5)
-    place = jnp.stack([lax.axis_index(a) for a in ("x", "core", "y")]).astype(jnp.int32)
+    place = jnp.stack([lax.axis_index(a) for a in ("x", "core")]).astype(jnp.int32)
     weight = out_weight.reshape(-1, HEAD, width)
 
     segments = scene_of(scene_lengths, toks)
@@ -235,6 +237,7 @@
 
     attended, gated = lax.optimization_barrier((attended, gated))
     gated_y = lax.all_gather(gated, "y", axis=0, tiled=True)
+    natural = attended
     attended = lax.all_to_all(attended, "y", split_axis=0, concat_axis=0, tiled=True)
 
     sent = upstream_part(place, weight, gated)
@@ -243,23 +246,24 @@
     attended, summed = lax.optimization_barrier((attended, summed))
     summed = lax.psum_scatter(summed, "x", scatter_dimension=0, tiled=True)
 
-    own = {0: lax.all_gather(attended, "zhi", axis=0, tiled=True)}
-    for s in (1, 3, 2):
-        own[s] = shift(own[0], "x", NX, s)
-    pieces = [p for s in range(NX) for p in (own[s], shift(own[s], "core", NCORE, 1))]
-    *pieces, summed = lax.optimization_barrier((*pieces, summed))
-
-    total = weight_part(pieces, gated_y)
+    own = [lax.all_gather(attended, "zhi", axis=0, tiled=True)]
+    gated_y, own[0] = lax.optimization_barrier((gated_y, own[0]))
+    own += [shift(own[0], "x", NX, s) for s in (1, 2, 3)]
+
+    theirs_y = shift(gated_y, "core", NCORE, 1)
+
+    total, swap = weight_part(own, gated_y, theirs_y)
+    total = jnp.concatenate([total, shift(swap, "core", NCORE, 1)])
     total = lax.all_gather(total, "zlo").astype(F32).sum(0).astype(BF)
-    *pieces, total = lax.optimization_barrier((*pieces, total))
+    natural, total = lax.optimization_barrier((natural, total))
     total = lax.all_gather(total, "y", axis=0, tiled=True)
     total = put_heads(place, total)
 
     summed = lax.psum_scatter(summed, "zhi", scatter_dimension=0, tiled=True)
 
-    parts = mix_part(place, weight, pieces)
-    parts = lax.all_to_all(parts, "y", split_axis=0, concat_axis=0, tiled=True)
-    mixed = (gate * parts.astype(F32).sum(0)).astype(BF)
+    whole = [lax.all_gather(natural, "zhi", axis=0, tiled=True)]
+    whole += [shift(whole[0], "x", NX, s) for s in (1, 2, 3)]
+    mixed = mix(place, weight, gate, [p for w in whole for p in (w, shift(w, "core", NCORE, 1))])
 
     upstream = summed.T
     grad_values = dot(rounded, upstream, ((0,), (0,))).astype(BF)

time: 203 us -> 193 us (0.951)
  the two profiles are of different devices: /device:TPU:8 before, /device:TPU:2 now
where the time goes in v5:
time: 193 us; the launch traced here: 191 us
  blocking collectives  66.9 us (35%)
  starting transfers between devices  40.5 us (21%)
  waiting for transfers between devices  33.6 us (17%)
  Pallas kernels  19.1 us (10%)
  between operations  15.9 us (8%)
  matrix products  7.14 us (4%)
  local copies, waits for them, and re-layouts  4.26 us (2%)
  other arithmetic  3.88 us (2%)
    ppermute x13, starting transfers between devices, shift(): lax.ppermute(value, axis, [(i, (i + step) % size) for i in range(size)])  33.2 us
    all_gather x1, blocking collectives, on_device(): own = [lax.all_gather(attended, 'zhi', axis=0, tiled=True)]  26.6 us
    ppermute x13, waiting for transfers between devices, shift(): lax.ppermute(value, axis, [(i, (i + step) % size) for i in range(size)])  24.4 us
    all_gather x1, blocking collectives, on_device(): whole = [lax.all_gather(natural, 'zhi', axis=0, tiled=True)]  23.6 us
    all_gather x1, blocking collectives, on_device(): total = lax.all_gather(total, 'zlo').astype(F32).sum(0).astype(BF)  16.7 us
    all_to_all x1, starting transfers between devices, on_device(): lax.all_to_all(attended, 'y', split_axis=0, concat_axis=0, tiled=True)  7.12 us
    all_to_all x1, waiting for transfers between devices, on_device(): lax.all_to_all(attended, 'y', split_axis=0, concat_axis=0, tiled=True)  5.39 us
    pallas_call x1, Pallas kernels, mix(): call(mix_body, jax.ShapeDtypeStruct((toks, width), BF), [SMEM] + [VMEM] *...  5.25 us
  transfers between devices with their start and end apart: 18, of which 9 were waited for; matrix products, arithmetic and copies ran while one was open for 3% of the time, Pallas kernels for 8%

profile of v5, /device:TPU:2, one launch (start us, length us, event | category | flops | bytes accessed | tf_op | source)
XLA Modules:
  0.0 191.3 jit_solution(13983196620218284096)
XLA Ops:
  10.5 2.0 %fusion.3 = bf16[128,384]{1,0:T(8,128)(2,1)} fusion(bf16[384,3,128]{2,0,1:T(8,128)(2,1)} %param.12, f32[384,384]{0,1:T(8,128)S(1)} %get-tuple-element.34, f32[384]{0:T(512)S(1)} %fusion.8, f32[384]{0:T(512)S(1)} %get-tuple-element.33), kind=kOutput, calls=%fused_computation.8 | convolution fusion | flops 38240256 | bytes 789504 | tf_op jit(solution)/shard_map/dot_general | solution.py:32
  15.5 2.7 %shard_map.139 = bf16[2048,384]{1,0:T(8,128)(2,1)} custom-call(s32[2]{0:T(128)S(1)} %pad_add_fusion.place, bf16[32,128,256]{2,1,0:T(8,128)(2,1)S(1)} %bitcast.49, bf16[384,256]{1,0:T(8,128)(2,1)S(1)} %copy-done.3), custom_call_target="tpu_custom_call" | custom-call | flops 402653184 | bytes 3145728 | tf_op jit(solution)/shard_map/pallas_call | solution.py:71
  18.1 1.9 collective-permute-start
  20.0 7.1 %all-to-all-start = ((bf16[8,16,384]{2,1,0:T(8,128)(2,1)}), bf16[8,16,384]{2,1,0:T(8,128)(2,1)S(1)}, u32[]{:S(2)}, u32[]{:S(2)}) async-start(bf16[8,16,384]{2,1,0:T(8,128)(2,1)} %bitcast.9), calls=%async_computation | async-start | bytes 196608 | tf_op jit(solution)/shard_map/all_to_all | solution.py:241
  27.2 2.4 %shard_map.140 = bf16[2048,384]{1,0:T(8,128)(2,1)S(1)} custom-call(s32[2]{0:T(128)S(1)} %pad_add_fusion.place, bf16[32,128,256]{2,1,0:T(8,128)(2,1)S(1)} %bitcast.50, bf16[384,256]{1,0:T(8,128)(2,1)S(1)} %copy-done.4, bf16[2048,384]{1,0:T(8,128)(2,1)} %collective-permute-done.refs_0_), custom_call_target="tpu_custom_call" | custom-call | flops 402653184 | bytes 3145728 | tf_op jit(solution)/shard_map/pallas_call | solution.py:71
  30.8 5.4 %all-to-all-done = bf16[8,16,384]{2,1,0:T(8,128)(2,1)S(1)} async-done(((bf16[8,16,384]{2,1,0:T(8,128)(2,1)}), bf16[8,16,384]{2,1,0:T(8,128)(2,1)S(1)}, u32[]{:S(2)}, u32[]{:S(2)}) %all-to-all-start) | async-done | bytes 98336 | tf_op jit(solution)/shard_map/all_to_all | solution.py:241
  36.3 26.6 %all_gather.19.refs_0_ = bf16[512,384]{1,0:T(8,128)(2,1)S(1)} all-gather(bf16[128,384]{1,0:T(8,128)(2,1)S(1)} %bitcast.54), channel_id=1, replica_groups=mesh['zlo'=3,'y'=8,'zhi'=4,'x'=4,'core'=2] {'zhi'}, dimensions={0}, use_global_device_ids=true | all-gather | bytes 491520 | tf_op jit(solution)/shard_map/all_gather | solution.py:249
  62.8 3.7 %all-gather.4.cloned.1.call-done.refs_4_ = bf16[3072,256]{1,0:T(8,128)(2,1)} async-done(((bf16[384,256]{1,0:T(8,128)(2,1)}), bf16[3072,256]{1,0:T(8,128)(2,1)}) %all-gather.4.cloned.1.call-update) | async-done | bytes 1572880 | tf_op jit(solution)/shard_map/all_gather | solution.py:239
  66.5 1.9 collective-permute-start.4
  68.4 3.4 %collective-permute-start.1 = (bf16[512,384]{1,0:T(8,128)(2,1)S(1)}, bf16[512,384]{1,0:T(8,128)(2,1)S(1)}, u32[]{:S(2)}, u32[]{:S(2)}) collective-permute-start(bf16[512,384]{1,0:T(8,128)(2,1)S(1)} %all_gather.19.refs_0_), channel_id=1, source_target_pairs={{0,2},{2,4},{4,6},{6,0},{1,3},{3,5},{5,7},{7,1},{8,10},{10,12},{12... | collective-permute-start | bytes 1179656 | tf_op jit(solution)/shard_map/ppermute | solution.py:36
  71.8 2.9 %collective-permute-start.2 = (bf16[512,384]{1,0:T(8,128)(2,1)S(1)}, bf16[512,384]{1,0:T(8,128)(2,1)}, u32[]{:S(2)}, u32[]{:S(2)}) collective-permute-start(bf16[512,384]{1,0:T(8,128)(2,1)S(1)} %all_gather.19.refs_0_), channel_id=1, source_target_pairs={{0,4},{2,6},{4,0},{6,2},{1,5},{3,7},{5,1},{7,3},{8,12},{10,14},{12... | collective-permute-start | bytes 1179656 | tf_op jit(solution)/shard_map/ppermute | solution.py:36
  74.7 4.2 %collective-permute-start.3 = (bf16[512,384]{1,0:T(8,128)(2,1)S(1)}, bf16[512,384]{1,0:T(8,128)(2,1)}, u32[]{:S(2)}, u32[]{:S(2)}) collective-permute-start(bf16[512,384]{1,0:T(8,128)(2,1)S(1)} %all_gather.19.refs_0_), channel_id=1, source_target_pairs={{0,6},{2,0},{4,2},{6,4},{1,7},{3,1},{5,3},{7,5},{8,14},{10,8},{12,... | collective-permute-start | bytes 1179656 | tf_op jit(solution)/shard_map/ppermute | solution.py:36
  79.0 3.2 %collective-permute-done.1.refs_1_ = bf16[512,384]{1,0:T(8,128)(2,1)S(1)} collective-permute-done((bf16[512,384]{1,0:T(8,128)(2,1)S(1)}, bf16[512,384]{1,0:T(8,128)(2,1)S(1)}, u32[]{:S(2)}, u32[]{:S(2)}) %collective-permute-start.1) | collective-permute-done | bytes 393248 | tf_op jit(solution)/shard_map/ppermute | solution.py:36
  82.3 5.1 %collective-permute-done.2.refs_2_ = bf16[512,384]{1,0:T(8,128)(2,1)} collective-permute-done((bf16[512,384]{1,0:T(8,128)(2,1)S(1)}, bf16[512,384]{1,0:T(8,128)(2,1)}, u32[]{:S(2)}, u32[]{:S(2)}) %collective-permute-start.2) | collective-permute-done | bytes 393248 | tf_op jit(solution)/shard_map/ppermute | solution.py:36
  87.3 7.7 %collective-permute-done.3.refs_3_ = bf16[512,384]{1,0:T(8,128)(2,1)} collective-permute-done((bf16[512,384]{1,0:T(8,128)(2,1)S(1)}, bf16[512,384]{1,0:T(8,128)(2,1)}, u32[]{:S(2)}, u32[]{:S(2)}) %collective-permute-start.3) | collective-permute-done | bytes 393248 | tf_op jit(solution)/shard_map/ppermute | solution.py:36
  96.2 5.0 %shard_map.141 = (bf16[256,256]{1,0:T(8,128)(2,1)}, bf16[256,256]{1,0:T(8,128)(2,1)}) custom-call(bf16[512,384]{1,0:T(8,128)(2,1)} %copy-done.7, bf16[512,384]{1,0:T(8,128)(2,1)} %copy-done.12, bf16[512,384]{1,0:T(8,128)(2,1)} %collective-permute-done.2.refs_2_, bf16[512,384]{1,0:T(8,128)(2,1)} %collective-permute-done.3.refs_3_, ...), custom_call_target="tpu_custom_call" | custom-call | flops 805306368 | bytes 4718592 | tf_op jit(solution)/shard_map/pallas_call | solution.py:111
  101.1 1.9 %collective-permute-start.5 = (bf16[256,256]{1,0:T(8,128)(2,1)}, bf16[256,256]{1,0:T(8,128)(2,1)S(1)}, u32[]{:S(2)}, u32[]{:S(2)}) collective-permute-start(bf16[256,256]{1,0:T(8,128)(2,1)} %get-tuple-element.29), channel_id=1, source_target_pairs={{0,1},{1,0},{2,3},{3,2},{4,5},{5,4},{6,7},{7,6},{8,9},{9,8},{10,11... | collective-permute-start | bytes 393224 | tf_op jit(solution)/shard_map/ppermute | solution.py:36
  103.1 1.5 collective-permute-done.5
  105.5 16.7 %all-gather = bf16[1536,256]{1,0:T(8,128)(2,1)S(1)} all-gather(bf16[512,256]{1,0:T(8,128)(2,1)S(1)} %pad_maximum_fusion.1), channel_id=2, replica_groups=mesh['zlo'=3,'y'=8,'zhi'=4,'x'=4,'core'=2] {'zlo'}, dimensions={0}, use_global_device_ids=true | all-gather | bytes 1048576 | tf_op jit(solution)/shard_map/all_gather | solution.py:257
  123.1 23.6 %all_gather.22.refs_0_ = bf16[512,384]{1,0:T(8,128)(2,1)S(1)} all-gather(bf16[128,384]{1,0:T(8,128)(2,1)} %fusion.3), channel_id=1, replica_groups=mesh['zlo'=3,'y'=8,'zhi'=4,'x'=4,'core'=2] {'zhi'}, dimensions={0}, use_global_device_ids=true | all-gather | bytes 491520 | tf_op jit(solution)/shard_map/all_gather | solution.py:264
  146.7 3.0 %collective-permute-start.9 = (bf16[512,384]{1,0:T(8,128)(2,1)S(1)}, bf16[512,384]{1,0:T(8,128)(2,1)S(1)}, u32[]{:S(2)}, u32[]{:S(2)}) collective-permute-start(bf16[512,384]{1,0:T(8,128)(2,1)S(1)} %all_gather.22.refs_0_), channel_id=1, source_target_pairs={{0,4},{2,6},{4,0},{6,2},{1,5},{3,7},{5,1},{7,3},{8,12},{10,14},{12... | collective-permute-start | bytes 1179656 | tf_op jit(solution)/shard_map/ppermute | solution.py:36
  149.8 3.4 %collective-permute-start.11 = (bf16[512,384]{1,0:T(8,128)(2,1)S(1)}, bf16[512,384]{1,0:T(8,128)(2,1)S(1)}, u32[]{:S(2)}, u32[]{:S(2)}) collective-permute-start(bf16[512,384]{1,0:T(8,128)(2,1)S(1)} %all_gather.22.refs_0_), channel_id=1, source_target_pairs={{0,6},{2,0},{4,2},{6,4},{1,7},{3,1},{5,3},{7,5},{8,14},{10,8},{12,... | collective-permute-start | bytes 1179656 | tf_op jit(solution)/shard_map/ppermute | solution.py:36
  153.2 2.5 %collective-permute-start.7 = (bf16[512,384]{1,0:T(8,128)(2,1)S(1)}, bf16[512,384]{1,0:T(8,128)(2,1)S(1)}, u32[]{:S(2)}, u32[]{:S(2)}) collective-permute-start(bf16[512,384]{1,0:T(8,128)(2,1)S(1)} %all_gather.22.refs_0_), channel_id=1, source_target_pairs={{0,2},{2,4},{4,6},{6,0},{1,3},{3,5},{5,7},{7,1},{8,10},{10,12},{12... | collective-permute-start | bytes 1179656 | tf_op jit(solution)/shard_map/ppermute | solution.py:36
  155.6 1.9 %collective-permute-start.6 = (bf16[512,384]{1,0:T(8,128)(2,1)S(1)}, bf16[512,384]{1,0:T(8,128)(2,1)S(1)}, u32[]{:S(2)}, u32[]{:S(2)}) collective-permute-start(bf16[512,384]{1,0:T(8,128)(2,1)S(1)} %all_gather.22.refs_0_), channel_id=1, source_target_pairs={{0,1},{1,0},{2,3},{3,2},{4,5},{5,4},{6,7},{7,6},{8,9},{9,8},{10,11... | collective-permute-start | bytes 1179656 | tf_op jit(solution)/shard_map/ppermute | solution.py:36
  157.6 3.5 %collective-permute-done.9.refs_4_ = bf16[512,384]{1,0:T(8,128)(2,1)S(1)} collective-permute-done((bf16[512,384]{1,0:T(8,128)(2,1)S(1)}, bf16[512,384]{1,0:T(8,128)(2,1)S(1)}, u32[]{:S(2)}, u32[]{:S(2)}) %collective-permute-start.9) | collective-permute-done | bytes 393248 | tf_op jit(solution)/shard_map/ppermute | solution.py:36
  161.1 1.9 collective-permute-start.10
  163.0 2.1 %collective-permute-done.11.refs_6_ = bf16[512,384]{1,0:T(8,128)(2,1)S(1)} collective-permute-done((bf16[512,384]{1,0:T(8,128)(2,1)S(1)}, bf16[512,384]{1,0:T(8,128)(2,1)S(1)}, u32[]{:S(2)}, u32[]{:S(2)}) %collective-permute-start.11) | collective-permute-done | bytes 393248 | tf_op jit(solution)/shard_map/ppermute | solution.py:36
  165.2 1.9 collective-permute-start.12
  167.1 2.4 %collective-permute-start.8 = (bf16[512,384]{1,0:T(8,128)(2,1)S(1)}, bf16[512,384]{1,0:T(8,128)(2,1)S(1)}, u32[]{:S(2)}, u32[]{:S(2)}) collective-permute-start(bf16[512,384]{1,0:T(8,128)(2,1)S(1)} %collective-permute-done.7.refs_2_), channel_id=1, source_target_pairs={{0,1},{1,0},{2,3},{3,2},{4,5},{5,4},{6,7},{7,6},{8,9},{9,8},{10,11... | collective-permute-start | bytes 1179656 | tf_op jit(solution)/shard_map/ppermute | solution.py:36
  169.6 1.3 collective-permute-done.8.refs_3_
  171.6 5.3 %shard_map.142 = bf16[384,256]{1,0:T(8,128)(2,1)} custom-call(s32[2]{0:T(128)} %copy-done.5, bf16[32,128,256]{2,1,0:T(8,128)(2,1)} %bitcast.48, f32[384,256]{1,0:T(8,128)} %get-tuple-element.36.gate, bf16[512,384]{1,0:T(8,128)(2,1)} %copy-done.6, bf16[512,384]{1,0:T(8,128)(2,1)} %copy-done.13, bf16[512,384]{1,0:T(8,128)(2,1)} %copy-done.11, ...), custom_call_target="tpu_custom_call" | custom-call | flops 805306368 | bytes 5242880 | tf_op jit(solution)/shard_map/pallas_call | solution.py:144
  180.1 3.8 %shard_map.143 = bf16[32,128,256]{2,1,0:T(8,128)(2,1)} custom-call(s32[2]{0:T(128)} %copy-done.5, bf16[8,512,256]{2,1,0:T(8,128)(2,1)} %bitcast.52), custom_call_target="tpu_custom_call" | custom-call | bytes 4194304 | tf_op jit(solution)/shard_map/pallas_call | solution.py:181
  (89 shorter events, 13.6 us)
Async XLA Ops:
  8.0 4.4 %copy-start = (bf16[1000,256]{1,0:T(8,128)(2,1)S(1)}, bf16[1000,256]{1,0:T(8,128)(2,1)}, u32[]{:S(2)}) copy-start(bf16[1000,256]{1,0:T(8,128)(2,1)} %param.20) | copy-start | bytes 1536004
  8.0 58.5 %all-gather.4.cloned.1.call-start = ((), (), s32[]{:S(2)}) async-start(), calls=%async_computation.3 | async-start | bytes 1769472 | tf_op jit(solution)/shard_map/all_gather | solution.py:239
  10.4 2.4 %copy-start.22 = (bf16[8,256]{1,0:T(8,128)(2,1)S(1)}, bf16[8,256]{1,0:T(8,128)(2,1)}, u32[]{:S(2)}) copy-start(bf16[8,256]{1,0:T(8,128)(2,1)} %param.22) | copy-start | bytes 12292
  10.4 2.6 %copy-start.23 = (bf16[8,256]{1,0:T(8,128)(2,1)S(1)}, bf16[8,256]{1,0:T(8,128)(2,1)}, u32[]{:S(2)}) copy-start(bf16[8,256]{1,0:T(8,128)(2,1)} %param.23) | copy-start | bytes 12292
  10.4 2.6 %copy-start.26 = (s32[8]{0:T(128)S(1)}, s32[8]{0:T(128)}, u32[]{:S(2)}) copy-start(s32[8]{0:T(128)} %param.16) | copy-start | bytes 100
  10.4 2.8 %copy-start.17 = (bf16[384,256]{1,0:T(8,128)(2,1)S(1)}, bf16[384,256]{1,0:T(8,128)(2,1)}, u32[]{:S(2)}) copy-start(bf16[384,256]{1,0:T(8,128)(2,1)} %param.14) | copy-start | bytes 589828
  10.5 4.1 %copy-start.1 = (bf16[4096,256]{1,0:T(8,128)(2,1)S(1)}, bf16[4096,256]{1,0:T(8,128)(2,1)}, u32[]{:S(2)}) copy-start(bf16[4096,256]{1,0:T(8,128)(2,1)} %param.13) | copy-start | bytes 6291460
  14.5 12.7 %copy-start.5 = (s32[2]{0:T(128)}, s32[2]{0:T(128)S(1)}, u32[]{:S(2)}) copy-start(s32[2]{0:T(128)S(1)} %pad_add_fusion.place) | copy-start | bytes 28
  15.4 11.8 %copy-start.4 = (bf16[384,256]{1,0:T(8,128)(2,1)S(1)}, bf16[384,256]{1,0:T(8,128)(2,1)}, u32[]{:S(2)}) copy-start(bf16[384,256]{1,0:T(8,128)(2,1)} %get-tuple-element.24.gated) | copy-start | bytes 589828
  18.1 9.1 %collective-permute-start = (bf16[2048,384]{1,0:T(8,128)(2,1)}, bf16[2048,384]{1,0:T(8,128)(2,1)}, u32[]{:S(2)}, u32[]{:S(2)}) collective-permute-start(bf16[2048,384]{1,0:T(8,128)(2,1)} %shard_map.139), channel_id=1, source_target_pairs={{0,1},{1,0},{2,3},{3,2},{4,5},{5,4},{6,7},{7,6},{8,9},{9,8},{10,11... | collective-permute-start | bytes 4718600 | tf_op jit(solution)/shard_map/ppermute | solution.py:36
  20.0 16.1 %all-to-all-start = ((bf16[8,16,384]{2,1,0:T(8,128)(2,1)}), bf16[8,16,384]{2,1,0:T(8,128)(2,1)S(1)}, u32[]{:S(2)}, u32[]{:S(2)}) async-start(bf16[8,16,384]{2,1,0:T(8,128)(2,1)} %bitcast.9), calls=%async_computation | async-start | bytes 196608 | tf_op jit(solution)/shard_map/all_to_all | solution.py:241
  27.2 51.8 %reduce-scatter.3.cloned.1.call-start = ((), (), s32[]{:S(2)}) async-start(), calls=%async_computation.4 | async-start | bytes 1966080 | tf_op jit(solution)/shard_map/reduce_scatter | solution.py:247
  36.2 140.7 %reduce-scatter.5.cloned.1.call-start = ((), (), s32[]{:S(2)}) async-start(), calls=%async_computation.5 | async-start | bytes 491520 | tf_op jit(solution)/shard_map/reduce_scatter | solution.py:262
  62.8 32.2 %copy-start.7 = (bf16[512,384]{1,0:T(8,128)(2,1)}, bf16[512,384]{1,0:T(8,128)(2,1)S(1)}, u32[]{:S(2)}) copy-start(bf16[512,384]{1,0:T(8,128)(2,1)S(1)} %all_gather.19.refs_0_) | copy-start | bytes 1179652
  66.5 28.5 %collective-permute-start.4 = (bf16[3072,256]{1,0:T(8,128)(2,1)}, bf16[3072,256]{1,0:T(8,128)(2,1)S(1)}, u32[]{:S(2)}, u32[]{:S(2)}) collective-permute-start(bf16[3072,256]{1,0:T(8,128)(2,1)} %all-gather.4.cloned.1.call-done.refs_4_), channel_id=1, source_target_pairs={{0,1},{1,0},{2,3},{3,2},{4,5},{5,4},{6,7},{7,6},{8,9},{9,8},{10,11... | collective-permute-start | bytes 4718600 | tf_op jit(solution)/shard_map/ppermute | solution.py:36
  68.4 13.8 %collective-permute-start.1 = (bf16[512,384]{1,0:T(8,128)(2,1)S(1)}, bf16[512,384]{1,0:T(8,128)(2,1)S(1)}, u32[]{:S(2)}, u32[]{:S(2)}) collective-permute-start(bf16[512,384]{1,0:T(8,128)(2,1)S(1)} %all_gather.19.refs_0_), channel_id=1, source_target_pairs={{0,2},{2,4},{4,6},{6,0},{1,3},{3,5},{5,7},{7,1},{8,10},{10,12},{12... | collective-permute-start | bytes 1179656 | tf_op jit(solution)/shard_map/ppermute | solution.py:36
  71.8 15.5 %collective-permute-start.2 = (bf16[512,384]{1,0:T(8,128)(2,1)S(1)}, bf16[512,384]{1,0:T(8,128)(2,1)}, u32[]{:S(2)}, u32[]{:S(2)}) collective-permute-start(bf16[512,384]{1,0:T(8,128)(2,1)S(1)} %all_gather.19.refs_0_), channel_id=1, source_target_pairs={{0,4},{2,6},{4,0},{6,2},{1,5},{3,7},{5,1},{7,3},{8,12},{10,14},{12... | collective-permute-start | bytes 1179656 | tf_op jit(solution)/shard_map/ppermute | solution.py:36
  74.7 20.3 %collective-permute-start.3 = (bf16[512,384]{1,0:T(8,128)(2,1)S(1)}, bf16[512,384]{1,0:T(8,128)(2,1)}, u32[]{:S(2)}, u32[]{:S(2)}) collective-permute-start(bf16[512,384]{1,0:T(8,128)(2,1)S(1)} %all_gather.19.refs_0_), channel_id=1, source_target_pairs={{0,6},{2,0},{4,2},{6,4},{1,7},{3,1},{5,3},{7,5},{8,14},{10,8},{12,... | collective-permute-start | bytes 1179656 | tf_op jit(solution)/shard_map/ppermute | solution.py:36
  79.0 101.1 %all-gather.6.cloned.1.call-start = ((), (), s32[]{:S(2)}) async-start(), calls=%async_computation.6 | async-start | bytes 2359296 | tf_op jit(solution)/shard_map/all_gather | solution.py:259
  82.3 12.8 %copy-start.12 = (bf16[512,384]{1,0:T(8,128)(2,1)}, bf16[512,384]{1,0:T(8,128)(2,1)S(1)}, u32[]{:S(2)}) copy-start(bf16[512,384]{1,0:T(8,128)(2,1)S(1)} %collective-permute-done.1.refs_1_) | copy-start | bytes 1179652
  101.1 3.5 %collective-permute-start.5 = (bf16[256,256]{1,0:T(8,128)(2,1)}, bf16[256,256]{1,0:T(8,128)(2,1)S(1)}, u32[]{:S(2)}, u32[]{:S(2)}) collective-permute-start(bf16[256,256]{1,0:T(8,128)(2,1)} %get-tuple-element.29), channel_id=1, source_target_pairs={{0,1},{1,0},{2,3},{3,2},{4,5},{5,4},{6,7},{7,6},{8,9},{9,8},{10,11... | collective-permute-start | bytes 393224 | tf_op jit(solution)/shard_map/ppermute | solution.py:36
  146.7 24.9 %copy-start.6 = (bf16[512,384]{1,0:T(8,128)(2,1)}, bf16[512,384]{1,0:T(8,128)(2,1)S(1)}, u32[]{:S(2)}) copy-start(bf16[512,384]{1,0:T(8,128)(2,1)S(1)} %all_gather.22.refs_0_) | copy-start | bytes 1179652
  146.7 14.3 %collective-permute-start.9 = (bf16[512,384]{1,0:T(8,128)(2,1)S(1)}, bf16[512,384]{1,0:T(8,128)(2,1)S(1)}, u32[]{:S(2)}, u32[]{:S(2)}) collective-permute-start(bf16[512,384]{1,0:T(8,128)(2,1)S(1)} %all_gather.22.refs_0_), channel_id=1, source_target_pairs={{0,4},{2,6},{4,0},{6,2},{1,5},{3,7},{5,1},{7,3},{8,12},{10,14},{12... | collective-permute-start | bytes 1179656 | tf_op jit(solution)/shard_map/ppermute | solution.py:36
  149.8 15.4 %collective-permute-start.11 = (bf16[512,384]{1,0:T(8,128)(2,1)S(1)}, bf16[512,384]{1,0:T(8,128)(2,1)S(1)}, u32[]{:S(2)}, u32[]{:S(2)}) collective-permute-start(bf16[512,384]{1,0:T(8,128)(2,1)S(1)} %all_gather.22.refs_0_), channel_id=1, source_target_pairs={{0,6},{2,0},{4,2},{6,4},{1,7},{3,1},{5,3},{7,5},{8,14},{10,8},{12,... | collective-permute-start | bytes 1179656 | tf_op jit(solution)/shard_map/ppermute | solution.py:36
  153.2 13.9 %collective-permute-start.7 = (bf16[512,384]{1,0:T(8,128)(2,1)S(1)}, bf16[512,384]{1,0:T(8,128)(2,1)S(1)}, u32[]{:S(2)}, u32[]{:S(2)}) collective-permute-start(bf16[512,384]{1,0:T(8,128)(2,1)S(1)} %all_gather.22.refs_0_), channel_id=1, source_target_pairs={{0,2},{2,4},{4,6},{6,0},{1,3},{3,5},{5,7},{7,1},{8,10},{10,12},{12... | collective-permute-start | bytes 1179656 | tf_op jit(solution)/shard_map/ppermute | solution.py:36
  155.6 13.9 %collective-permute-start.6 = (bf16[512,384]{1,0:T(8,128)(2,1)S(1)}, bf16[512,384]{1,0:T(8,128)(2,1)S(1)}, u32[]{:S(2)}, u32[]{:S(2)}) collective-permute-start(bf16[512,384]{1,0:T(8,128)(2,1)S(1)} %all_gather.22.refs_0_), channel_id=1, source_target_pairs={{0,1},{1,0},{2,3},{3,2},{4,5},{5,4},{6,7},{7,6},{8,9},{9,8},{10,11... | collective-permute-start | bytes 1179656 | tf_op jit(solution)/shard_map/ppermute | solution.py:36
  161.1 10.5 %copy-start.9 = (bf16[512,384]{1,0:T(8,128)(2,1)}, bf16[512,384]{1,0:T(8,128)(2,1)S(1)}, u32[]{:S(2)}) copy-start(bf16[512,384]{1,0:T(8,128)(2,1)S(1)} %collective-permute-done.9.refs_4_) | copy-start | bytes 1179652
  161.1 8.4 %collective-permute-start.10 = (bf16[512,384]{1,0:T(8,128)(2,1)S(1)}, bf16[512,384]{1,0:T(8,128)(2,1)S(1)}, u32[]{:S(2)}, u32[]{:S(2)}) collective-permute-start(bf16[512,384]{1,0:T(8,128)(2,1)S(1)} %collective-permute-done.9.refs_4_), channel_id=1, source_target_pairs={{0,1},{1,0},{2,3},{3,2},{4,5},{5,4},{6,7},{7,6},{8,9},{9,8},{10,11... | collective-permute-start | bytes 1179656 | tf_op jit(solution)/shard_map/ppermute | solution.py:36
  165.2 6.5 %copy-start.10 = (bf16[512,384]{1,0:T(8,128)(2,1)}, bf16[512,384]{1,0:T(8,128)(2,1)S(1)}, u32[]{:S(2)}) copy-start(bf16[512,384]{1,0:T(8,128)(2,1)S(1)} %collective-permute-done.11.refs_6_) | copy-start | bytes 1179652
  165.2 4.4 %collective-permute-start.12 = (bf16[512,384]{1,0:T(8,128)(2,1)S(1)}, bf16[512,384]{1,0:T(8,128)(2,1)S(1)}, u32[]{:S(2)}, u32[]{:S(2)}) collective-permute-start(bf16[512,384]{1,0:T(8,128)(2,1)S(1)} %collective-permute-done.11.refs_6_), channel_id=1, source_target_pairs={{0,1},{1,0},{2,3},{3,2},{4,5},{5,4},{6,7},{7,6},{8,9},{9,8},{10,11... | collective-permute-start | bytes 1179656 | tf_op jit(solution)/shard_map/ppermute | solution.py:36
  167.1 4.5 %copy-start.11 = (bf16[512,384]{1,0:T(8,128)(2,1)}, bf16[512,384]{1,0:T(8,128)(2,1)S(1)}, u32[]{:S(2)}) copy-start(bf16[512,384]{1,0:T(8,128)(2,1)S(1)} %collective-permute-done.7.refs_2_) | copy-start | bytes 1179652
  167.1 3.7 %collective-permute-start.8 = (bf16[512,384]{1,0:T(8,128)(2,1)S(1)}, bf16[512,384]{1,0:T(8,128)(2,1)S(1)}, u32[]{:S(2)}, u32[]{:S(2)}) collective-permute-start(bf16[512,384]{1,0:T(8,128)(2,1)S(1)} %collective-permute-done.7.refs_2_), channel_id=1, source_target_pairs={{0,1},{1,0},{2,3},{3,2},{4,5},{5,4},{6,7},{7,6},{8,9},{9,8},{10,11... | collective-permute-start | bytes 1179656 | tf_op jit(solution)/shard_map/ppermute | solution.py:36
  (13 other events, 21.7 us)
Sparse Core Ops, SparseCore 0:
  14.6 51.9 all-gather.3
  123.2 44.4 all-gather.5
Sparse Core Ops, SparseCore 1:
  36.3 34.8 reduce-scatter.2
  79.0 34.4 reduce-scatter.4

commit v6 on v5

--- a/solution.py
+++ b/solution.py
@@ -52,31 +52,29 @@
     )
 
 
-def up_body(place, weight, gated, *refs):
-    out = refs[-1]
+def up_body(place, weight, other, gated, theirs, out):
     core = place[1]
-    pick = core if len(refs) == 2 else 1 - core
     for x in range(NX):
         for z in range(NZHI):
+            head = z * NX + x
+            value = dot(weight[head * NCORE + core], gated[...], ((1,), (1,)))
+            value = value + dot(other[head], theirs[...], ((1,), (1,)))
             rows = pl.ds((x * NZHI + z) * HEAD, HEAD)
-            value = dot(weight[(z * NX + x) * NCORE + pick], gated[...], ((1,), (1,)))
-            if len(refs) == 2:
-                value = value + refs[0][rows, :].astype(F32)
             out[rows, :] = value.astype(BF)
 
 
-def upstream_part(place, weight, gated, *got):
+def upstream_part(place, weight, other, gated, theirs):
     toks = gated.shape[0]
     rows = NX * NZHI * HEAD
     return call(
         up_body,
         jax.ShapeDtypeStruct((rows, toks), BF),
-        [SMEM] + [VMEM] * (2 + len(got)),
+        [SMEM] + [VMEM] * 4,
         VMEM,
-        2 * rows * toks * gated.shape[1],
+        4 * rows * toks * gated.shape[1],
         4 * rows * toks,
         limit=16,
-    )(place, weight, gated, *got)
+    )(place, weight, other, gated, theirs)
 
 
 def fetch(pieces, held, sems):
@@ -123,37 +121,43 @@
     )(*pieces, mine, theirs)
 
 
-def mix_body(place, weight, gate, *refs):
-    *pieces, out, acc, sems, held = refs
+def mix_body(place, weight, other, *refs):
+    *pieces, out_mine, out_theirs, sems, held = refs
     fetch(pieces, held, sems)
     x, core = place[0], place[1]
-    for i in range(len(pieces)):
-        s, c = i // 2, i % 2
-        chip = lax.rem(x + NX - s, NX)
-        pick = core if c == 0 else 1 - core
-        rows = jnp.concatenate([weight[(z * NX + chip) * NCORE + pick] for z in range(NZHI)])
-        value = dot(held[i], rows, ((0,), (0,)))
-        acc[...] = value if i == 0 else acc[...] + value
-    out[...] = (gate[...] * acc[...]).astype(BF)
-
-
-def mix(place, weight, gate, pieces):
-    toks, width = gate.shape
+    for mine in (False, True):
+        rows = []
+        for s in range(len(pieces)):
+            chip = lax.rem(x + NX - s, NX)
+            for z in range(NZHI):
+                head = z * NX + chip
+                rows.append(weight[head * NCORE + core] if mine else other[head])
+        value = dot(held[...].reshape(-1, held.shape[2]), jnp.concatenate(rows), ((0,), (0,)))
+        if mine:
+            out_mine[...] = value
+        else:
+            out_theirs[...] = value.astype(BF)
+
+
+def mix_part(place, weight, other, pieces):
+    toks, width = pieces[0].shape[1], weight.shape[2]
     rows = sum(p.shape[0] for p in pieces)
     count = len(pieces)
     return call(
         mix_body,
-        jax.ShapeDtypeStruct((toks, width), BF),
+        (
+            jax.ShapeDtypeStruct((toks, width), F32),
+            jax.ShapeDtypeStruct((toks, width), BF),
+        ),
         [SMEM] + [VMEM] * 2 + [HBM] * count,
-        VMEM,
-        2 * rows * toks * width,
-        2 * rows * (toks + width),
+        (VMEM, VMEM),
+        4 * rows * toks * width,
+        2 * rows * (toks + 2 * width),
         [
-            pltpu.VMEM((toks, width), F32),
             pltpu.SemaphoreType.DMA((count,)),
             pltpu.VMEM((count, *pieces[0].shape), BF),
         ],
-    )(place, weight, gate, *pieces)
+    )(place, weight, other, *pieces)
 
 
 def place_body(place, src, dst, taken, given, in_sems, out_sems):
@@ -214,6 +218,10 @@
     place = jnp.stack([lax.axis_index(a) for a in ("x", "core")]).astype(jnp.int32)
     weight = out_weight.reshape(-1, HEAD, width)
 
+    other = weight.reshape(-1, NCORE, HEAD, width)
+    other = lax.dynamic_index_in_dim(other, 1 - place[1], 1, keepdims=False)
+    other = shift(other, "core", NCORE, 1)
+
     segments = scene_of(scene_lengths, toks)
     same = segments[:, None] == segments[None, :]
     queries, keys, values = qkv[:, 0], qkv[:, 1], qkv[:, 2]
@@ -240,16 +248,13 @@
     natural = attended
     attended = lax.all_to_all(attended, "y", split_axis=0, concat_axis=0, tiled=True)
 
-    sent = upstream_part(place, weight, gated)
-    got = shift(sent, "core", NCORE, 1)
-    summed = upstream_part(place, weight, gated, got)
+    summed = upstream_part(place, weight, other, gated, shift(gated, "core", NCORE, 1))
     attended, summed = lax.optimization_barrier((attended, summed))
     summed = lax.psum_scatter(summed, "x", scatter_dimension=0, tiled=True)
 
     own = [lax.all_gather(attended, "zhi", axis=0, tiled=True)]
     gated_y, own[0] = lax.optimization_barrier((gated_y, own[0]))
     own += [shift(own[0], "x", NX, s) for s in (1, 2, 3)]
-
     theirs_y = shift(gated_y, "core", NCORE, 1)
 
     total, swap = weight_part(own, gated_y, theirs_y)
@@ -263,8 +268,6 @@
 
     whole = [lax.all_gather(natural, "zhi", axis=0, tiled=True)]
     whole += [shift(whole[0], "x", NX, s) for s in (1, 2, 3)]
-    mixed = mix(place, weight, gate, [p for w in whole for p in (w, shift(w, "core", NCORE, 1))])
-
     upstream = summed.T
     grad_values = dot(rounded, upstream, ((0,), (0,))).astype(BF)
     grad_probs = dot(upstream, values, ((1,), (1,)))
@@ -273,6 +276,10 @@
     grad_queries = (dot(grad_scores, keys, ((1,), (0,))) * factor).astype(BF)
     grad_keys = (dot(grad_scores, queries, ((0,), (0,))) * factor).astype(BF)
     grad_qkv = jnp.stack([grad_queries, grad_keys, grad_values], axis=1)
+
+    *whole, grad_qkv = lax.optimization_barrier((*whole, grad_qkv))
+    mixed, swap = mix_part(place, weight, other, whole)
+    mixed = (gate * (mixed + shift(swap, "core", NCORE, 1).astype(F32))).astype(BF)
     return (mixed, grad_qkv, total)
 
 

time: 193 us -> 192 us (level)
  the two profiles are of different devices: /device:TPU:2 before, /device:TPU:1 now
where the time goes in v6:
time: 192 us; the launch traced here: 191 us
  blocking collectives  52.1 us (27%)
  starting transfers between devices  49.7 us (26%)
  waiting for transfers between devices  39.8 us (21%)
  Pallas kernels  17 us (9%)
  between operations  15.9 us (8%)
  matrix products  7.07 us (4%)
  other arithmetic  5.6 us (3%)
  local copies, waits for them, and re-layouts  4.16 us (2%)
    ppermute x11, starting transfers between devices, shift(): lax.ppermute(value, axis, [(i, (i + step) % size) for i in range(size)])  46.2 us
    ppermute x11, waiting for transfers between devices, shift(): lax.ppermute(value, axis, [(i, (i + step) % size) for i in range(size)])  32 us
    all_gather x1, blocking collectives, on_device(): own = [lax.all_gather(attended, 'zhi', axis=0, tiled=True)]  17.8 us
    all_gather x1, blocking collectives, on_device(): whole = [lax.all_gather(natural, 'zhi', axis=0, tiled=True)]  17.6 us
    all_gather x1, blocking collectives, on_device(): total = lax.all_gather(total, 'zlo').astype(F32).sum(0).astype(BF)  16.6 us
    dot_general x6, matrix products, dot(): return lax.dot_general(a, b, (dims, ((), ())), preferred_element_type=F32)  5.24 us
    pallas_call x1, Pallas kernels, mix_part(): call(mix_body, (jax.ShapeDtypeStruct((toks, width), F32), jax.ShapeDtypeS...  5.09 us
    pallas_call x1, Pallas kernels, weight_part(): call(part_body, (jax.ShapeDtypeStruct((rows, width), BF),) * 2, [HBM] * c...  4.95 us
  transfers between devices with their start and end apart: 16, of which 8 were waited for; matrix products, arithmetic and copies ran while one was open for 4% of the time, Pallas kernels for 7%

profile of v6, /device:TPU:1, one launch (start us, length us, event | category | flops | bytes accessed | tf_op | source)
XLA Modules:
  0.0 191.3 jit_solution(5951528125074375051)
XLA Ops:
  9.1 1.3 fusion.33
  10.5 2.0 %fusion.3 = bf16[128,384]{1,0:T(8,128)(2,1)} fusion(bf16[384,3,128]{2,0,1:T(8,128)(2,1)} %param.12, f32[384,384]{0,1:T(8,128)S(1)} %get-tuple-element.48, f32[384]{0:T(512)S(1)} %fusion.8, f32[384]{0:T(512)S(1)} %get-tuple-element.47), kind=kOutput, calls=%fused_computation.8 | convolution fusion | flops 38240256 | bytes 789504 | tf_op jit(solution)/shard_map/dot_general | solution.py:32
  15.4 12.4 %collective-permute-start = (bf16[16,128,256]{2,1,0:T(8,128)(2,1)}, bf16[16,128,256]{2,1,0:T(8,128)(2,1)}, u32[]{:S(2)}, u32[]{:S(2)}) collective-permute-start(bf16[16,128,256]{2,1,0:T(8,128)(2,1)} %dynamic-slice_bitcast_fusion), channel_id=1, source_target_pairs={{0,1},{1,0},{2,3},{3,2},{4,5},{5,4},{6,7},{7,6},{8,9},{9,8},{10,11... | collective-permute-start | bytes 3145736 | tf_op jit(solution)/shard_map/ppermute | solution.py:36
  27.9 1.9 %collective-permute-start.1 = (bf16[384,256]{1,0:T(8,128)(2,1)S(1)}, bf16[384,256]{1,0:T(8,128)(2,1)S(1)}, u32[]{:S(2)}, u32[]{:S(2)}) collective-permute-start(bf16[384,256]{1,0:T(8,128)(2,1)S(1)} %copy-done.3), channel_id=1, source_target_pairs={{0,1},{1,0},{2,3},{3,2},{4,5},{5,4},{6,7},{7,6},{8,9},{9,8},{10,11... | collective-permute-start | bytes 589832 | tf_op jit(solution)/shard_map/ppermute | solution.py:36
  29.8 3.4 %all-to-all-start = ((bf16[8,16,384]{2,1,0:T(8,128)(2,1)}), bf16[8,16,384]{2,1,0:T(8,128)(2,1)S(1)}, u32[]{:S(2)}, u32[]{:S(2)}) async-start(bf16[8,16,384]{2,1,0:T(8,128)(2,1)} %bitcast.11), calls=%async_computation | async-start | bytes 196608 | tf_op jit(solution)/shard_map/all_to_all | solution.py:249
  33.3 3.2 %shard_map.139 = bf16[2048,384]{1,0:T(8,128)(2,1)S(1)} custom-call(s32[2]{0:T(128)S(1)} %pad_add_fusion.place, bf16[32,128,256]{2,1,0:T(8,128)(2,1)S(1)} %bitcast.55, bf16[16,128,256]{2,1,0:T(8,128)(2,1)} %collective-permute-done.other, bf16[384,256]{1,0:T(8,128)(2,1)S(1)} %copy-done.3, bf16[384,256]{1,0:T(8,128)(2,1)S(1)} %collective-permute-done.1.theirs), custom_call_target="tpu_custom_call" | custom-call | flops 805306368 | bytes 3145728 | tf_op jit(solution)/shard_map/pallas_call | solution.py:69
  36.5 1.1 copy-done.2
  37.6 2.9 %all-to-all-done = bf16[8,16,384]{2,1,0:T(8,128)(2,1)S(1)} async-done(((bf16[8,16,384]{2,1,0:T(8,128)(2,1)}), bf16[8,16,384]{2,1,0:T(8,128)(2,1)S(1)}, u32[]{:S(2)}, u32[]{:S(2)}) %all-to-all-start) | async-done | bytes 98336 | tf_op jit(solution)/shard_map/all_to_all | solution.py:249
  40.6 17.8 %all_gather.19.refs_0_ = bf16[512,384]{1,0:T(8,128)(2,1)S(1)} all-gather(bf16[128,384]{1,0:T(8,128)(2,1)S(1)} %bitcast.59), channel_id=1, replica_groups=mesh['zlo'=3,'y'=8,'zhi'=4,'x'=4,'core'=2] {'zhi'}, dimensions={0}, use_global_device_ids=true | all-gather | bytes 491520 | tf_op jit(solution)/shard_map/all_gather | solution.py:255
  58.5 4.8 %all-gather.4.cloned.1.call-done.refs_4_ = bf16[3072,256]{1,0:T(8,128)(2,1)} async-done(((bf16[384,256]{1,0:T(8,128)(2,1)}), bf16[3072,256]{1,0:T(8,128)(2,1)}) %all-gather.4.cloned.1.call-update) | async-done | bytes 1572880 | tf_op jit(solution)/shard_map/all_gather | solution.py:247
  63.2 6.6 %collective-permute-start.5 = (bf16[3072,256]{1,0:T(8,128)(2,1)}, bf16[3072,256]{1,0:T(8,128)(2,1)S(1)}, u32[]{:S(2)}, u32[]{:S(2)}) collective-permute-start(bf16[3072,256]{1,0:T(8,128)(2,1)} %all-gather.4.cloned.1.call-done.refs_4_), channel_id=1, source_target_pairs={{0,1},{1,0},{2,3},{3,2},{4,5},{5,4},{6,7},{7,6},{8,9},{9,8},{10,11... | collective-permute-start | bytes 4718600 | tf_op jit(solution)/shard_map/ppermute | solution.py:36
  69.9 4.3 %collective-permute-start.4 = (bf16[512,384]{1,0:T(8,128)(2,1)S(1)}, bf16[512,384]{1,0:T(8,128)(2,1)S(1)}, u32[]{:S(2)}, u32[]{:S(2)}) collective-permute-start(bf16[512,384]{1,0:T(8,128)(2,1)S(1)} %all_gather.19.refs_0_), channel_id=1, source_target_pairs={{0,6},{2,0},{4,2},{6,4},{1,7},{3,1},{5,3},{7,5},{8,14},{10,8},{12,... | collective-permute-start | bytes 1179656 | tf_op jit(solution)/shard_map/ppermute | solution.py:36
  74.2 2.5 %collective-permute-start.3 = (bf16[512,384]{1,0:T(8,128)(2,1)S(1)}, bf16[512,384]{1,0:T(8,128)(2,1)}, u32[]{:S(2)}, u32[]{:S(2)}) collective-permute-start(bf16[512,384]{1,0:T(8,128)(2,1)S(1)} %all_gather.19.refs_0_), channel_id=1, source_target_pairs={{0,4},{2,6},{4,0},{6,2},{1,5},{3,7},{5,1},{7,3},{8,12},{10,14},{12... | collective-permute-start | bytes 1179656 | tf_op jit(solution)/shard_map/ppermute | solution.py:36
  76.7 2.5 %collective-permute-start.2 = (bf16[512,384]{1,0:T(8,128)(2,1)S(1)}, bf16[512,384]{1,0:T(8,128)(2,1)}, u32[]{:S(2)}, u32[]{:S(2)}) collective-permute-start(bf16[512,384]{1,0:T(8,128)(2,1)S(1)} %all_gather.19.refs_0_), channel_id=1, source_target_pairs={{0,2},{2,4},{4,6},{6,0},{1,3},{3,5},{5,7},{7,1},{8,10},{10,12},{12... | collective-permute-start | bytes 1179656 | tf_op jit(solution)/shard_map/ppermute | solution.py:36
  79.3 11.7 %collective-permute-done.4.refs_3_ = bf16[512,384]{1,0:T(8,128)(2,1)S(1)} collective-permute-done((bf16[512,384]{1,0:T(8,128)(2,1)S(1)}, bf16[512,384]{1,0:T(8,128)(2,1)S(1)}, u32[]{:S(2)}, u32[]{:S(2)}) %collective-permute-start.4) | collective-permute-done | bytes 393248 | tf_op jit(solution)/shard_map/ppermute | solution.py:36
  91.0 6.2 %collective-permute-done.2.refs_1_ = bf16[512,384]{1,0:T(8,128)(2,1)} collective-permute-done((bf16[512,384]{1,0:T(8,128)(2,1)S(1)}, bf16[512,384]{1,0:T(8,128)(2,1)}, u32[]{:S(2)}, u32[]{:S(2)}) %collective-permute-start.2) | collective-permute-done | bytes 393248 | tf_op jit(solution)/shard_map/ppermute | solution.py:36
  98.3 5.0 %shard_map.140 = (bf16[256,256]{1,0:T(8,128)(2,1)}, bf16[256,256]{1,0:T(8,128)(2,1)}) custom-call(bf16[512,384]{1,0:T(8,128)(2,1)} %copy-done.7, bf16[512,384]{1,0:T(8,128)(2,1)} %collective-permute-done.2.refs_1_, bf16[512,384]{1,0:T(8,128)(2,1)} %collective-permute-done.3.refs_2_, bf16[512,384]{1,0:T(8,128)(2,1)} %copy-done.12, ...), custom_call_target="tpu_custom_call" | custom-call | flops 805306368 | bytes 4718592 | tf_op jit(solution)/shard_map/pallas_call | solution.py:109
  103.3 2.5 %collective-permute-start.6 = (bf16[256,256]{1,0:T(8,128)(2,1)}, bf16[256,256]{1,0:T(8,128)(2,1)S(1)}, u32[]{:S(2)}, u32[]{:S(2)}) collective-permute-start(bf16[256,256]{1,0:T(8,128)(2,1)} %get-tuple-element.36), channel_id=1, source_target_pairs={{0,1},{1,0},{2,3},{3,2},{4,5},{5,4},{6,7},{7,6},{8,9},{9,8},{10,11... | collective-permute-start | bytes 393224 | tf_op jit(solution)/shard_map/ppermute | solution.py:36
  105.9 1.2 collective-permute-done.6
  108.0 16.6 %all-gather = bf16[1536,256]{1,0:T(8,128)(2,1)S(1)} all-gather(bf16[512,256]{1,0:T(8,128)(2,1)S(1)} %pad_maximum_fusion.1), channel_id=2, replica_groups=mesh['zlo'=3,'y'=8,'zhi'=4,'x'=4,'core'=2] {'zlo'}, dimensions={0}, use_global_device_ids=true | all-gather | bytes 1048576 | tf_op jit(solution)/shard_map/all_gather | solution.py:262
  125.5 17.6 %all_gather.22.refs_0_ = bf16[512,384]{1,0:T(8,128)(2,1)S(1)} all-gather(bf16[128,384]{1,0:T(8,128)(2,1)} %fusion.3), channel_id=1, replica_groups=mesh['zlo'=3,'y'=8,'zhi'=4,'x'=4,'core'=2] {'zhi'}, dimensions={0}, use_global_device_ids=true | all-gather | bytes 491520 | tf_op jit(solution)/shard_map/all_gather | solution.py:269
  143.1 2.9 %collective-permute-start.9 = (bf16[512,384]{1,0:T(8,128)(2,1)S(1)}, bf16[512,384]{1,0:T(8,128)(2,1)S(1)}, u32[]{:S(2)}, u32[]{:S(2)}) collective-permute-start(bf16[512,384]{1,0:T(8,128)(2,1)S(1)} %all_gather.22.refs_0_), channel_id=1, source_target_pairs={{0,6},{2,0},{4,2},{6,4},{1,7},{3,1},{5,3},{7,5},{8,14},{10,8},{12,... | collective-permute-start | bytes 1179656 | tf_op jit(solution)/shard_map/ppermute | solution.py:36
  145.9 2.6 %collective-permute-start.8 = (bf16[512,384]{1,0:T(8,128)(2,1)S(1)}, bf16[512,384]{1,0:T(8,128)(2,1)S(1)}, u32[]{:S(2)}, u32[]{:S(2)}) collective-permute-start(bf16[512,384]{1,0:T(8,128)(2,1)S(1)} %all_gather.22.refs_0_), channel_id=1, source_target_pairs={{0,4},{2,6},{4,0},{6,2},{1,5},{3,7},{5,1},{7,3},{8,12},{10,14},{12... | collective-permute-start | bytes 1179656 | tf_op jit(solution)/shard_map/ppermute | solution.py:36
  148.6 2.3 %collective-permute-start.7 = (bf16[512,384]{1,0:T(8,128)(2,1)S(1)}, bf16[512,384]{1,0:T(8,128)(2,1)S(1)}, u32[]{:S(2)}, u32[]{:S(2)}) collective-permute-start(bf16[512,384]{1,0:T(8,128)(2,1)S(1)} %all_gather.22.refs_0_), channel_id=1, source_target_pairs={{0,2},{2,4},{4,6},{6,0},{1,3},{3,5},{5,7},{7,1},{8,10},{10,12},{12... | collective-permute-start | bytes 1179656 | tf_op jit(solution)/shard_map/ppermute | solution.py:36
  151.0 1.2 multiply_reduce_fusion
  153.9 2.2 %collective-permute-done.8.refs_2_ = bf16[512,384]{1,0:T(8,128)(2,1)S(1)} collective-permute-done((bf16[512,384]{1,0:T(8,128)(2,1)S(1)}, bf16[512,384]{1,0:T(8,128)(2,1)S(1)}, u32[]{:S(2)}, u32[]{:S(2)}) %collective-permute-start.8) | collective-permute-done | bytes 393248 | tf_op jit(solution)/shard_map/ppermute | solution.py:36
  156.1 9.6 %collective-permute-done.7.refs_1_ = bf16[512,384]{1,0:T(8,128)(2,1)S(1)} collective-permute-done((bf16[512,384]{1,0:T(8,128)(2,1)S(1)}, bf16[512,384]{1,0:T(8,128)(2,1)S(1)}, u32[]{:S(2)}, u32[]{:S(2)}) %collective-permute-start.7) | collective-permute-done | bytes 393248 | tf_op jit(solution)/shard_map/ppermute | solution.py:36
  166.4 5.1 %shard_map.141 = (f32[384,256]{1,0:T(8,128)}, bf16[384,256]{1,0:T(8,128)(2,1)}) custom-call(s32[2]{0:T(128)} %copy-done.4, bf16[32,128,256]{2,1,0:T(8,128)(2,1)} %bitcast.53, bf16[16,128,256]{2,1,0:T(8,128)(2,1)} %collective-permute-done.other, bf16[512,384]{1,0:T(8,128)(2,1)} %copy-done.8, bf16[512,384]{1,0:T(8,128)(2,1)} %copy-done.13, ...), custom_call_target="tpu_custom_call" | custom-call | flops 805306368 | bytes 3670016 | tf_op jit(solution)/shard_map/pallas_call | solution.py:146
  171.5 5.6 %collective-permute-start.10 = (bf16[384,256]{1,0:T(8,128)(2,1)}, bf16[384,256]{1,0:T(8,128)(2,1)S(1)}, u32[]{:S(2)}, u32[]{:S(2)}) collective-permute-start(bf16[384,256]{1,0:T(8,128)(2,1)} %get-tuple-element.44), channel_id=1, source_target_pairs={{0,1},{1,0},{2,3},{3,2},{4,5},{5,4},{6,7},{7,6},{8,9},{9,8},{10,11... | collective-permute-start | bytes 589832 | tf_op jit(solution)/shard_map/ppermute | solution.py:36
  177.1 1.3 collective-permute-done.10
  178.3 1.8 multiply_convert_fusion.1
  180.1 3.8 %shard_map.142 = bf16[32,128,256]{2,1,0:T(8,128)(2,1)} custom-call(s32[2]{0:T(128)} %copy-done.4, bf16[8,512,256]{2,1,0:T(8,128)(2,1)} %bitcast.57), custom_call_target="tpu_custom_call" | custom-call | bytes 4194304 | tf_op jit(solution)/shard_map/pallas_call | solution.py:185
  (80 shorter events, 9.8 us)
Async XLA Ops:
  8.0 4.5 %copy-start = (bf16[1000,256]{1,0:T(8,128)(2,1)S(1)}, bf16[1000,256]{1,0:T(8,128)(2,1)}, u32[]{:S(2)}) copy-start(bf16[1000,256]{1,0:T(8,128)(2,1)} %param.20) | copy-start | bytes 1536004
  8.0 4.5 %copy-start.16 = (s32[8]{0:T(128)S(1)}, s32[8]{0:T(128)}, u32[]{:S(2)}) copy-start(s32[8]{0:T(128)} %param.19) | copy-start | bytes 100
  8.0 55.2 %all-gather.4.cloned.1.call-start = ((), (), s32[]{:S(2)}) async-start(), calls=%async_computation.3 | async-start | bytes 1769472 | tf_op jit(solution)/shard_map/all_gather | solution.py:247
  9.0 3.7 %copy-start.18 = (bf16[16,256]{1,0:T(8,128)(2,1)S(1)}, bf16[16,256]{1,0:T(8,128)(2,1)}, u32[]{:S(2)}) copy-start(bf16[16,256]{1,0:T(8,128)(2,1)} %param.21) | copy-start | bytes 24580
  9.0 3.7 %copy-start.21 = (s32[8]{0:T(128)S(1)}, s32[8]{0:T(128)}, u32[]{:S(2)}) copy-start(s32[8]{0:T(128)} %param.18) | copy-start | bytes 100
  9.0 3.9 %copy-start.19 = (bf16[8,256]{1,0:T(8,128)(2,1)S(1)}, bf16[8,256]{1,0:T(8,128)(2,1)}, u32[]{:S(2)}) copy-start(bf16[8,256]{1,0:T(8,128)(2,1)} %param.22) | copy-start | bytes 12292
  9.0 3.8 %copy-start.22 = (s32[8]{0:T(128)S(1)}, s32[8]{0:T(128)}, u32[]{:S(2)}) copy-start(s32[8]{0:T(128)} %param.17) | copy-start | bytes 100
  10.3 4.0 %copy-start.5 = (f32[384,384]{0,1:T(8,128)}, f32[384,384]{0,1:T(8,128)S(1)}, u32[]{:S(2)}) copy-start(f32[384,384]{0,1:T(8,128)S(1)} %get-tuple-element.48) | copy-start | bytes 1769476
  10.5 3.9 %copy-start.1 = (bf16[4096,256]{1,0:T(8,128)(2,1)S(1)}, bf16[4096,256]{1,0:T(8,128)(2,1)}, u32[]{:S(2)}) copy-start(bf16[4096,256]{1,0:T(8,128)(2,1)} %param.13) | copy-start | bytes 6291460
  14.3 13.5 %copy-start.3 = (bf16[384,256]{1,0:T(8,128)(2,1)S(1)}, bf16[384,256]{1,0:T(8,128)(2,1)}, u32[]{:S(2)}) copy-start(bf16[384,256]{1,0:T(8,128)(2,1)} %get-tuple-element.31.gated) | copy-start | bytes 589828
  15.4 17.9 %collective-permute-start = (bf16[16,128,256]{2,1,0:T(8,128)(2,1)}, bf16[16,128,256]{2,1,0:T(8,128)(2,1)}, u32[]{:S(2)}, u32[]{:S(2)}) collective-permute-start(bf16[16,128,256]{2,1,0:T(8,128)(2,1)} %dynamic-slice_bitcast_fusion), channel_id=1, source_target_pairs={{0,1},{1,0},{2,3},{3,2},{4,5},{5,4},{6,7},{7,6},{8,9},{9,8},{10,11... | collective-permute-start | bytes 3145736 | tf_op jit(solution)/shard_map/ppermute | solution.py:36
  27.9 5.4 %collective-permute-start.1 = (bf16[384,256]{1,0:T(8,128)(2,1)S(1)}, bf16[384,256]{1,0:T(8,128)(2,1)S(1)}, u32[]{:S(2)}, u32[]{:S(2)}) collective-permute-start(bf16[384,256]{1,0:T(8,128)(2,1)S(1)} %copy-done.3), channel_id=1, source_target_pairs={{0,1},{1,0},{2,3},{3,2},{4,5},{5,4},{6,7},{7,6},{8,9},{9,8},{10,11... | collective-permute-start | bytes 589832 | tf_op jit(solution)/shard_map/ppermute | solution.py:36
  29.8 10.7 %all-to-all-start = ((bf16[8,16,384]{2,1,0:T(8,128)(2,1)}), bf16[8,16,384]{2,1,0:T(8,128)(2,1)S(1)}, u32[]{:S(2)}, u32[]{:S(2)}) async-start(bf16[8,16,384]{2,1,0:T(8,128)(2,1)} %bitcast.11), calls=%async_computation | async-start | bytes 196608 | tf_op jit(solution)/shard_map/all_to_all | solution.py:249
  33.2 46.1 %reduce-scatter.3.cloned.1.call-start = ((), (), s32[]{:S(2)}) async-start(), calls=%async_computation.4 | async-start | bytes 1966080 | tf_op jit(solution)/shard_map/reduce_scatter | solution.py:253
  40.6 110.4 %reduce-scatter.5.cloned.1.call-start = ((), (), s32[]{:S(2)}) async-start(), calls=%async_computation.5 | async-start | bytes 491520 | tf_op jit(solution)/shard_map/reduce_scatter | solution.py:267
  58.5 38.7 %copy-start.7 = (bf16[512,384]{1,0:T(8,128)(2,1)}, bf16[512,384]{1,0:T(8,128)(2,1)S(1)}, u32[]{:S(2)}) copy-start(bf16[512,384]{1,0:T(8,128)(2,1)S(1)} %all_gather.19.refs_0_) | copy-start | bytes 1179652
  63.2 33.9 %collective-permute-start.5 = (bf16[3072,256]{1,0:T(8,128)(2,1)}, bf16[3072,256]{1,0:T(8,128)(2,1)S(1)}, u32[]{:S(2)}, u32[]{:S(2)}) collective-permute-start(bf16[3072,256]{1,0:T(8,128)(2,1)} %all-gather.4.cloned.1.call-done.refs_4_), channel_id=1, source_target_pairs={{0,1},{1,0},{2,3},{3,2},{4,5},{5,4},{6,7},{7,6},{8,9},{9,8},{10,11... | collective-permute-start | bytes 4718600 | tf_op jit(solution)/shard_map/ppermute | solution.py:36
  69.9 21.1 %collective-permute-start.4 = (bf16[512,384]{1,0:T(8,128)(2,1)S(1)}, bf16[512,384]{1,0:T(8,128)(2,1)S(1)}, u32[]{:S(2)}, u32[]{:S(2)}) collective-permute-start(bf16[512,384]{1,0:T(8,128)(2,1)S(1)} %all_gather.19.refs_0_), channel_id=1, source_target_pairs={{0,6},{2,0},{4,2},{6,4},{1,7},{3,1},{5,3},{7,5},{8,14},{10,8},{12,... | collective-permute-start | bytes 1179656 | tf_op jit(solution)/shard_map/ppermute | solution.py:36
  74.2 16.8 %collective-permute-start.3 = (bf16[512,384]{1,0:T(8,128)(2,1)S(1)}, bf16[512,384]{1,0:T(8,128)(2,1)}, u32[]{:S(2)}, u32[]{:S(2)}) collective-permute-start(bf16[512,384]{1,0:T(8,128)(2,1)S(1)} %all_gather.19.refs_0_), channel_id=1, source_target_pairs={{0,4},{2,6},{4,0},{6,2},{1,5},{3,7},{5,1},{7,3},{8,12},{10,14},{12... | collective-permute-start | bytes 1179656 | tf_op jit(solution)/shard_map/ppermute | solution.py:36
  76.7 20.5 %collective-permute-start.2 = (bf16[512,384]{1,0:T(8,128)(2,1)S(1)}, bf16[512,384]{1,0:T(8,128)(2,1)}, u32[]{:S(2)}, u32[]{:S(2)}) collective-permute-start(bf16[512,384]{1,0:T(8,128)(2,1)S(1)} %all_gather.19.refs_0_), channel_id=1, source_target_pairs={{0,2},{2,4},{4,6},{6,0},{1,3},{3,5},{5,7},{7,1},{8,10},{10,12},{12... | collective-permute-start | bytes 1179656 | tf_op jit(solution)/shard_map/ppermute | solution.py:36
  79.3 100.8 %all-gather.6.cloned.1.call-start = ((), (), s32[]{:S(2)}) async-start(), calls=%async_computation.6 | async-start | bytes 2359296 | tf_op jit(solution)/shard_map/all_gather | solution.py:264
  91.0 6.2 %copy-start.12 = (bf16[512,384]{1,0:T(8,128)(2,1)}, bf16[512,384]{1,0:T(8,128)(2,1)S(1)}, u32[]{:S(2)}) copy-start(bf16[512,384]{1,0:T(8,128)(2,1)S(1)} %collective-permute-done.4.refs_3_) | copy-start | bytes 1179652
  103.3 47.6 %copy-start.6 = (f32[384,384]{0,1:T(8,128)S(1)}, f32[384,384]{0,1:T(8,128)}, u32[]{:S(2)}) copy-start(f32[384,384]{0,1:T(8,128)} %copy-done.5) | copy-start | bytes 1769476
  103.3 47.6 %copy-start.15 = (bf16[384,3,128]{2,0,1:T(8,128)(2,1)S(1)}, bf16[384,3,128]{2,0,1:T(8,128)(2,1)}, u32[]{:S(2)}) copy-start(bf16[384,3,128]{2,0,1:T(8,128)(2,1)} %param.12) | copy-start | bytes 884740
  103.3 3.7 %collective-permute-start.6 = (bf16[256,256]{1,0:T(8,128)(2,1)}, bf16[256,256]{1,0:T(8,128)(2,1)S(1)}, u32[]{:S(2)}, u32[]{:S(2)}) collective-permute-start(bf16[256,256]{1,0:T(8,128)(2,1)} %get-tuple-element.36), channel_id=1, source_target_pairs={{0,1},{1,0},{2,3},{3,2},{4,5},{5,4},{6,7},{7,6},{8,9},{9,8},{10,11... | collective-permute-start | bytes 393224 | tf_op jit(solution)/shard_map/ppermute | solution.py:36
  143.1 9.5 %copy-start.8 = (bf16[512,384]{1,0:T(8,128)(2,1)}, bf16[512,384]{1,0:T(8,128)(2,1)S(1)}, u32[]{:S(2)}) copy-start(bf16[512,384]{1,0:T(8,128)(2,1)S(1)} %all_gather.22.refs_0_) | copy-start | bytes 1179652
  143.1 10.8 %collective-permute-start.9 = (bf16[512,384]{1,0:T(8,128)(2,1)S(1)}, bf16[512,384]{1,0:T(8,128)(2,1)S(1)}, u32[]{:S(2)}, u32[]{:S(2)}) collective-permute-start(bf16[512,384]{1,0:T(8,128)(2,1)S(1)} %all_gather.22.refs_0_), channel_id=1, source_target_pairs={{0,6},{2,0},{4,2},{6,4},{1,7},{3,1},{5,3},{7,5},{8,14},{10,8},{12,... | collective-permute-start | bytes 1179656 | tf_op jit(solution)/shard_map/ppermute | solution.py:36
  145.9 10.1 %collective-permute-start.8 = (bf16[512,384]{1,0:T(8,128)(2,1)S(1)}, bf16[512,384]{1,0:T(8,128)(2,1)S(1)}, u32[]{:S(2)}, u32[]{:S(2)}) collective-permute-start(bf16[512,384]{1,0:T(8,128)(2,1)S(1)} %all_gather.22.refs_0_), channel_id=1, source_target_pairs={{0,4},{2,6},{4,0},{6,2},{1,5},{3,7},{5,1},{7,3},{8,12},{10,14},{12... | collective-permute-start | bytes 1179656 | tf_op jit(solution)/shard_map/ppermute | solution.py:36
  148.6 17.1 %collective-permute-start.7 = (bf16[512,384]{1,0:T(8,128)(2,1)S(1)}, bf16[512,384]{1,0:T(8,128)(2,1)S(1)}, u32[]{:S(2)}, u32[]{:S(2)}) collective-permute-start(bf16[512,384]{1,0:T(8,128)(2,1)S(1)} %all_gather.22.refs_0_), channel_id=1, source_target_pairs={{0,2},{2,4},{4,6},{6,0},{1,3},{3,5},{5,7},{7,1},{8,10},{10,12},{12... | collective-permute-start | bytes 1179656 | tf_op jit(solution)/shard_map/ppermute | solution.py:36
  153.9 11.7 %copy-start.10 = (bf16[512,384]{1,0:T(8,128)(2,1)}, bf16[512,384]{1,0:T(8,128)(2,1)S(1)}, u32[]{:S(2)}) copy-start(bf16[512,384]{1,0:T(8,128)(2,1)S(1)} %collective-permute-done.9.refs_3_) | copy-start | bytes 1179652
  156.1 9.6 %copy-start.11 = (bf16[512,384]{1,0:T(8,128)(2,1)}, bf16[512,384]{1,0:T(8,128)(2,1)S(1)}, u32[]{:S(2)}) copy-start(bf16[512,384]{1,0:T(8,128)(2,1)S(1)} %collective-permute-done.8.refs_2_) | copy-start | bytes 1179652
  171.5 6.8 %collective-permute-start.10 = (bf16[384,256]{1,0:T(8,128)(2,1)}, bf16[384,256]{1,0:T(8,128)(2,1)S(1)}, u32[]{:S(2)}, u32[]{:S(2)}) collective-permute-start(bf16[384,256]{1,0:T(8,128)(2,1)} %get-tuple-element.44), channel_id=1, source_target_pairs={{0,1},{1,0},{2,3},{3,2},{4,5},{5,4},{6,7},{7,6},{8,9},{9,8},{10,11... | collective-permute-start | bytes 589832 | tf_op jit(solution)/shard_map/ppermute | solution.py:36
  (8 other events, 16.6 us)
Sparse Core Ops, SparseCore 0:
  14.5 48.7 all-gather.3
  125.6 39.5 all-gather.5
Sparse Core Ops, SparseCore 1:
  40.6 31.1 reduce-scatter.2
  79.3 33.8 reduce-scatter.4

commit v7 on v6

--- a/solution.py
+++ b/solution.py
@@ -2,6 +2,7 @@
 import jax.numpy as jnp
 from jax import lax
 from jax.experimental import pallas as pl
+from jax.experimental.layout import Layout, with_layout_constraint
 from jax.experimental.pallas import tpu as pltpu
 from jax.sharding import Mesh, PartitionSpec as P
 
@@ -36,6 +37,10 @@
     return lax.ppermute(value, axis, [(i, (i + step) % size) for i in range(size)])
 
 
+def gather_x(value):
+    return lax.all_to_all(value, "x", split_axis=0, concat_axis=0, tiled=True)
+
+
 def after(value, *others):
     return lax.optimization_barrier((value,) + others)[0]
 
@@ -53,7 +58,7 @@
 
 
 def up_body(place, weight, other, gated, theirs, out):
-    core = place[1]
+    core = place[0]
     for x in range(NX):
         for z in range(NZHI):
             head = z * NX + x
@@ -77,91 +82,62 @@
     )(place, weight, other, gated, theirs)
 
 
-def fetch(pieces, held, sems):
-    copies = [pltpu.make_async_copy(p, held.at[i], sems.at[i]) for i, p in enumerate(pieces)]
-    for copy in copies:
-        copy.start()
-    for copy in copies:
-        copy.wait()
-
-
 def slabs(held, y):
-    starts = [z * HEAD + y * SLAB for z in range(NZHI)]
-    return jnp.concatenate(
-        [held[i, start : start + SLAB, :] for i in range(held.shape[0]) for start in starts]
-    )
-
-
-def part_body(*refs):
-    *pieces, mine, theirs, out_mine, out_theirs, rows, sems, held = refs
-    fetch(pieces, held, sems)
-    toks = held.shape[2]
+    starts = [h * HEAD + y * SLAB for h in range(held.shape[0] // HEAD)]
+    return jnp.concatenate([held[start : start + SLAB, :] for start in starts])
+
+
+def part_body(held, mine, theirs, out_mine, out_theirs, rows):
+    toks = held.shape[1]
     for y in range(NY):
         rows[:, y * toks : (y + 1) * toks] = slabs(held, y)
     out_theirs[...] = dot(rows[...], theirs[...], ((1,), (0,))).astype(BF)
     out_mine[...] = dot(rows[...], mine[...], ((1,), (0,))).astype(BF)
 
 
-def weight_part(pieces, mine, theirs):
-    rows = sum(p.shape[0] for p in pieces) // NY
+def weight_part(held, mine, theirs):
+    rows = held.shape[0] // NY
     toks, width = mine.shape
-    count = len(pieces)
     return call(
         part_body,
         (jax.ShapeDtypeStruct((rows, width), BF),) * 2,
-        [HBM] * count + [VMEM] * 2,
+        [VMEM] * 3,
         (VMEM, VMEM),
         4 * rows * toks * width,
         2 * rows * toks + 4 * toks * width,
-        [
-            pltpu.VMEM((rows, toks), BF),
-            pltpu.SemaphoreType.DMA((count,)),
-            pltpu.VMEM((count, *pieces[0].shape), BF),
-        ],
-    )(*pieces, mine, theirs)
-
-
-def mix_body(place, weight, other, *refs):
-    *pieces, out_mine, out_theirs, sems, held = refs
-    fetch(pieces, held, sems)
-    x, core = place[0], place[1]
-    for mine in (False, True):
-        rows = []
-        for s in range(len(pieces)):
-            chip = lax.rem(x + NX - s, NX)
-            for z in range(NZHI):
-                head = z * NX + chip
-                rows.append(weight[head * NCORE + core] if mine else other[head])
-        value = dot(held[...].reshape(-1, held.shape[2]), jnp.concatenate(rows), ((0,), (0,)))
-        if mine:
-            out_mine[...] = value
-        else:
-            out_theirs[...] = value.astype(BF)
-
-
-def mix_part(place, weight, other, pieces):
-    toks, width = pieces[0].shape[1], weight.shape[2]
-    rows = sum(p.shape[0] for p in pieces)
-    count = len(pieces)
+        [pltpu.VMEM((rows, toks), BF)],
+        limit=16,
+    )(held, mine, theirs)
+
+
+def mix_body(place, weight, other, held, out_mine, out_theirs):
+    core = place[0]
+    heads = [z * NX + x for x in range(NX) for z in range(NZHI)]
+    theirs = jnp.concatenate([other[head] for head in heads])
+    out_theirs[...] = dot(held[...], theirs, ((0,), (0,))).astype(BF)
+    mine = jnp.concatenate([weight[head * NCORE + core] for head in heads])
+    out_mine[...] = dot(held[...], mine, ((0,), (0,)))
+
+
+def mix_part(place, weight, other, held):
+    rows, toks = held.shape
+    width = weight.shape[2]
     return call(
         mix_body,
         (
             jax.ShapeDtypeStruct((toks, width), F32),
             jax.ShapeDtypeStruct((toks, width), BF),
         ),
-        [SMEM] + [VMEM] * 2 + [HBM] * count,
+        [SMEM] + [VMEM] * 3,
         (VMEM, VMEM),
         4 * rows * toks * width,
         2 * rows * (toks + 2 * width),
-        [
-            pltpu.SemaphoreType.DMA((count,)),
-            pltpu.VMEM((count, *pieces[0].shape), BF),
-        ],
-    )(place, weight, other, *pieces)
+        limit=16,
+    )(place, weight, other, held)
 
 
 def place_body(place, src, dst, taken, given, in_sems, out_sems):
-    x, core = place[0], place[1]
+    core = place[0]
     loads = [pltpu.make_async_copy(src.at[y], taken.at[y], in_sems.at[y]) for y in range(NY)]
     for load in loads:
         load.start()
@@ -169,9 +145,8 @@
         load.wait()
     stores = []
     for i in range(NX * NCORE * NZHI):
-        c, s, z = i // (NX * NZHI), i // NZHI % NX, i % NZHI
-        chip = lax.rem(x + NX - s, NX)
-        head = (z * NX + chip) * NCORE + (core if c == 0 else 1 - core)
+        c, x, z = i // (NX * NZHI), i // NZHI % NX, i % NZHI
+        head = (z * NX + x) * NCORE + (core if c == 0 else 1 - core)
         for y in range(NY):
             given[i, y * SLAB : (y + 1) * SLAB, :] = taken[y, i * SLAB : (i + 1) * SLAB, :]
         stores.append(pltpu.make_async_copy(given.at[i], dst.at[head], out_sems.at[i]))
@@ -215,11 +190,12 @@
     toks = qkv.shape[0]
     width = cotangent.shape[1]
     factor = HEAD ** (-0.5)
-    place = jnp.stack([lax.axis_index(a) for a in ("x", "core")]).astype(jnp.int32)
+    core = lax.axis_index("core")
+    place = core.reshape(1).astype(jnp.int32)
     weight = out_weight.reshape(-1, HEAD, width)
 
     other = weight.reshape(-1, NCORE, HEAD, width)
-    other = lax.dynamic_index_in_dim(other, 1 - place[1], 1, keepdims=False)
+    other = lax.dynamic_index_in_dim(other, 1 - core, 1, keepdims=False)
     other = shift(other, "core", NCORE, 1)
 
     segments = scene_of(scene_lengths, toks)
@@ -233,6 +209,7 @@
     probs = weights / jnp.sum(weights, axis=-1, keepdims=True)
     rounded = probs.astype(BF)
     attended = dot(values, rounded, ((0,), (1,))).astype(BF)
+    attended = with_layout_constraint(attended, Layout((0, 1)))
 
     ids = (step_ids, gsd_ids, sensor_ids, bucket_ids)
     attended, *ids = lax.optimization_barrier((attended, *ids))
@@ -252,9 +229,10 @@
     attended, summed = lax.optimization_barrier((attended, summed))
     summed = lax.psum_scatter(summed, "x", scatter_dimension=0, tiled=True)
 
-    own = [lax.all_gather(attended, "zhi", axis=0, tiled=True)]
-    gated_y, own[0] = lax.optimization_barrier((gated_y, own[0]))
-    own += [shift(own[0], "x", NX, s) for s in (1, 2, 3)]
+    own = lax.all_gather(attended, "zhi", axis=0, tiled=True)
+    own = jnp.concatenate([own] * NX)
+    gated_y = after(gated_y, own)
+    own = gather_x(own)
     theirs_y = shift(gated_y, "core", NCORE, 1)
 
     total, swap = weight_part(own, gated_y, theirs_y)
@@ -266,8 +244,9 @@
 
     summed = lax.psum_scatter(summed, "zhi", scatter_dimension=0, tiled=True)
 
-    whole = [lax.all_gather(natural, "zhi", axis=0, tiled=True)]
-    whole += [shift(whole[0], "x", NX, s) for s in (1, 2, 3)]
+    whole = lax.all_gather(natural, "zhi", axis=0, tiled=True)
+    whole = gather_x(jnp.concatenate([whole] * NX))
+
     upstream = summed.T
     grad_values = dot(rounded, upstream, ((0,), (0,))).astype(BF)
     grad_probs = dot(upstream, values, ((1,), (1,)))
@@ -277,7 +256,7 @@
     grad_keys = (dot(grad_scores, queries, ((0,), (0,))) * factor).astype(BF)
     grad_qkv = jnp.stack([grad_queries, grad_keys, grad_values], axis=1)
 
-    *whole, grad_qkv = lax.optimization_barrier((*whole, grad_qkv))
+    whole, grad_qkv = lax.optimization_barrier((whole, grad_qkv))
     mixed, swap = mix_part(place, weight, other, whole)
     mixed = (gate * (mixed + shift(swap, "core", NCORE, 1).astype(F32))).astype(BF)
     return (mixed, grad_qkv, total)

time: 192 us -> 185 us (0.964)
  the two profiles are of different devices: /device:TPU:1 before, /device:TPU:49 now
where the time goes in v7:
time: 185 us; the launch traced here: 184 us
  blocking collectives  56.1 us (30%)
  starting transfers between devices  41.7 us (23%)
  waiting for transfers between devices  39.6 us (21%)
  between operations  15.8 us (9%)
  Pallas kernels  12 us (6%)
  local copies, waits for them, and re-layouts  7.13 us (4%)
  matrix products  7.05 us (4%)
  other arithmetic  4.91 us (3%)
    all_to_all x2, waiting for transfers between devices, gather_x(): return lax.all_to_all(value, 'x', split_axis=0, concat_axis=0, tiled=True)  36 us
    all_gather x1, blocking collectives, on_device(): own = lax.all_gather(attended, 'zhi', axis=0, tiled=True)  19.7 us
    all_gather x1, blocking collectives, on_device(): total = lax.all_gather(total, 'zlo').astype(F32).sum(0).astype(BF)  19 us
    ppermute x5, starting transfers between devices, shift(): lax.ppermute(value, axis, [(i, (i + step) % size) for i in range(size)])  18.5 us
    all_gather x1, blocking collectives, on_device(): whole = lax.all_gather(natural, 'zhi', axis=0, tiled=True)  17.5 us
    all_to_all x1, starting transfers between devices, on_device(): lax.all_to_all(attended, 'y', split_axis=0, concat_axis=0, tiled=True)  11.9 us
    all_to_all x2, starting transfers between devices, gather_x(): return lax.all_to_all(value, 'x', split_axis=0, concat_axis=0, tiled=True)  11.1 us
    unnamed x39, local copies, waits for them, and re-layouts  5.28 us
  transfers between devices with their start and end apart: 12, of which 6 were waited for; matrix products, arithmetic and copies ran while one was open for 5% of the time, Pallas kernels for 5%

profile of v7, /device:TPU:49, one launch (start us, length us, event | category | flops | bytes accessed | tf_op | source)
XLA Modules:
  0.0 184.3 jit_solution(1458785611262805822)
XLA Ops:
  8.1 0.9 reduce-window.8
  9.0 1.2 fusion.33
  10.5 2.0 %fusion.3 = bf16[128,384]{1,0:T(8,128)(2,1)} fusion(bf16[384,3,128]{2,0,1:T(8,128)(2,1)} %param.12, f32[384,384]{0,1:T(8,128)S(1)} %get-tuple-element.40, f32[384]{0:T(512)S(1)} %fusion.8, f32[384]{0:T(512)S(1)} %get-tuple-element.39), kind=kOutput, calls=%fused_computation.9 | convolution fusion | flops 38240256 | bytes 789504 | tf_op jit(solution)/shard_map/dot_general | solution.py:33
  13.3 1.2 multiply_convert_fusion.2
  14.5 1.1 dynamic-slice_bitcast_fusion
  15.5 2.6 %collective-permute-start = (bf16[16,128,256]{2,1,0:T(8,128)(2,1)}, bf16[16,128,256]{2,1,0:T(8,128)(2,1)}, u32[]{:S(2)}, u32[]{:S(2)}) collective-permute-start(bf16[16,128,256]{2,1,0:T(8,128)(2,1)} %dynamic-slice_bitcast_fusion), channel_id=1, source_target_pairs={{0,1},{1,0},{2,3},{3,2},{4,5},{5,4},{6,7},{7,6},{8,9},{9,8},{10,11... | collective-permute-start | bytes 3145736 | tf_op jit(solution)/shard_map/ppermute | solution.py:37
  18.1 1.9 %collective-permute-start.1 = (bf16[384,256]{1,0:T(8,128)(2,1)S(1)}, bf16[384,256]{1,0:T(8,128)(2,1)S(1)}, u32[]{:S(2)}, u32[]{:S(2)}) collective-permute-start(bf16[384,256]{1,0:T(8,128)(2,1)S(1)} %copy-done.3), channel_id=1, source_target_pairs={{0,1},{1,0},{2,3},{3,2},{4,5},{5,4},{6,7},{7,6},{8,9},{9,8},{10,11... | collective-permute-start | bytes 589832 | tf_op jit(solution)/shard_map/ppermute | solution.py:37
  20.0 11.9 %all-to-all-start = ((bf16[8,16,384]{2,1,0:T(8,128)(2,1)}), bf16[8,16,384]{2,1,0:T(8,128)(2,1)S(1)}, u32[]{:S(2)}, u32[]{:S(2)}) async-start(bf16[8,16,384]{2,1,0:T(8,128)(2,1)} %bitcast.10), calls=%async_computation | async-start | bytes 196608 | tf_op jit(solution)/shard_map/all_to_all | solution.py:226
  32.0 3.2 %shard_map.139 = bf16[2048,384]{1,0:T(8,128)(2,1)S(1)} custom-call(s32[1]{0:T(128)} %bitcast.6.place, bf16[32,128,256]{2,1,0:T(8,128)(2,1)S(1)} %bitcast.57, bf16[16,128,256]{2,1,0:T(8,128)(2,1)} %collective-permute-done.other, bf16[384,256]{1,0:T(8,128)(2,1)S(1)} %copy-done.3, bf16[384,256]{1,0:T(8,128)(2,1)S(1)} %collective-permute-done.1.theirs), custom_call_target="tpu_custom_call" | custom-call | flops 805306368 | bytes 3145728 | tf_op jit(solution)/shard_map/pallas_call | solution.py:74
  35.2 1.1 copy-done.2
  36.9 19.7 %all_gather.18 = bf16[512,384]{1,0:T(8,128)(2,1)S(1)} all-gather(bf16[128,384]{1,0:T(8,128)(2,1)S(1)} %bitcast.63), channel_id=1, replica_groups=mesh['zlo'=3,'y'=8,'zhi'=4,'x'=4,'core'=2] {'zhi'}, dimensions={0}, use_global_device_ids=true | all-gather | bytes 491520 | tf_op jit(solution)/shard_map/all_gather | solution.py:232
  56.5 0.8 constant_dynamic-update-slice_fusion.3
  57.3 0.8 constant_dynamic-update-slice_fusion.2
  58.9 0.8 constant_dynamic-update-slice_fusion
  60.2 6.4 %collective-permute-start.2 = (bf16[3072,256]{1,0:T(8,128)(2,1)}, bf16[3072,256]{1,0:T(8,128)(2,1)}, u32[]{:S(2)}, u32[]{:S(2)}) collective-permute-start(bf16[3072,256]{1,0:T(8,128)(2,1)} %all-gather.4.cloned.1.call-done.mine), channel_id=1, source_target_pairs={{0,1},{1,0},{2,3},{3,2},{4,5},{5,4},{6,7},{7,6},{8,9},{9,8},{10,11... | collective-permute-start | bytes 4718600 | tf_op jit(solution)/shard_map/ppermute | solution.py:37
  66.6 4.4 %all-to-all-start.1 = ((bf16[4,512,384]{2,1,0:T(8,128)(2,1)}), bf16[4,512,384]{2,1,0:T(8,128)(2,1)}, u32[]{:S(2)}, u32[]{:S(2)}) async-start(bf16[4,512,384]{2,1,0:T(8,128)(2,1)} %bitcast.12), calls=%async_computation.1 | async-start | bytes 3145728 | tf_op jit(solution)/shard_map/all_to_all | solution.py:41
  71.6 20.3 %all-to-all-done.1 = bf16[4,512,384]{2,1,0:T(8,128)(2,1)} async-done(((bf16[4,512,384]{2,1,0:T(8,128)(2,1)}), bf16[4,512,384]{2,1,0:T(8,128)(2,1)}, u32[]{:S(2)}, u32[]{:S(2)}) %all-to-all-start.1) | async-done | bytes 1572896 | tf_op jit(solution)/shard_map/all_to_all | solution.py:41
  91.9 1.4 copy-done.4
  93.4 2.9 %shard_map.140 = (bf16[256,256]{1,0:T(8,128)(2,1)S(1)}, bf16[256,256]{1,0:T(8,128)(2,1)S(1)}) custom-call(bf16[2048,384]{1,0:T(8,128)(2,1)} %bitcast.13.held, bf16[3072,256]{1,0:T(8,128)(2,1)S(1)} %copy-done.4, bf16[3072,256]{1,0:T(8,128)(2,1)} %collective-permute-done.2.theirs), custom_call_target="tpu_custom_call" | custom-call | flops 805306368 | bytes 4718592 | tf_op jit(solution)/shard_map/pallas_call | solution.py:101
  96.3 2.7 %collective-permute-start.3 = (bf16[256,256]{1,0:T(8,128)(2,1)S(1)}, bf16[256,256]{1,0:T(8,128)(2,1)S(1)}, u32[]{:S(2)}, u32[]{:S(2)}) collective-permute-start(bf16[256,256]{1,0:T(8,128)(2,1)S(1)} %get-tuple-element.31), channel_id=1, source_target_pairs={{0,1},{1,0},{2,3},{3,2},{4,5},{5,4},{6,7},{7,6},{8,9},{9,8},{10,11... | collective-permute-start | bytes 393224 | tf_op jit(solution)/shard_map/ppermute | solution.py:37
  99.0 1.0 collective-permute-done.3
  99.9 19.0 %all-gather = bf16[1536,256]{1,0:T(8,128)(2,1)S(1)} all-gather(bf16[512,256]{1,0:T(8,128)(2,1)S(1)} %pad_maximum_fusion.2), channel_id=2, replica_groups=mesh['zlo'=3,'y'=8,'zhi'=4,'x'=4,'core'=2] {'zlo'}, dimensions={0}, use_global_device_ids=true | all-gather | bytes 1048576 | tf_op jit(solution)/shard_map/all_gather | solution.py:240
  118.9 0.9 reduce_sum.41
  119.8 17.5 %all_gather.22 = bf16[512,384]{1,0:T(8,128)(2,1)S(1)} all-gather(bf16[128,384]{1,0:T(8,128)(2,1)} %fusion.3), channel_id=1, replica_groups=mesh['zlo'=3,'y'=8,'zhi'=4,'x'=4,'core'=2] {'zhi'}, dimensions={0}, use_global_device_ids=true | all-gather | bytes 491520 | tf_op jit(solution)/shard_map/all_gather | solution.py:247
  137.3 1.3 pad_maximum_fusion
  138.6 6.8 %all-to-all-start.2 = ((bf16[4,512,384]{2,1,0:T(8,128)(2,1)}), bf16[4,512,384]{2,1,0:T(8,128)(2,1)}, u32[]{:S(2)}, u32[]{:S(2)}) async-start(bf16[4,512,384]{2,1,0:T(8,128)(2,1)} %bitcast.59), calls=%async_computation.2 | async-start | bytes 3145728 | tf_op jit(solution)/shard_map/all_to_all | solution.py:41
  145.4 1.2 multiply_reduce_fusion
  148.5 15.7 %all-to-all-done.2 = bf16[4,512,384]{2,1,0:T(8,128)(2,1)} async-done(((bf16[4,512,384]{2,1,0:T(8,128)(2,1)}), bf16[4,512,384]{2,1,0:T(8,128)(2,1)}, u32[]{:S(2)}, u32[]{:S(2)}) %all-to-all-start.2) | async-done | bytes 1572896 | tf_op jit(solution)/shard_map/all_to_all | solution.py:41
  164.2 2.8 %shard_map.141 = (f32[384,256]{1,0:T(8,128)S(1)}, bf16[384,256]{1,0:T(8,128)(2,1)S(1)}) custom-call(s32[1]{0:T(128)} %bitcast.6.place, bf16[32,128,256]{2,1,0:T(8,128)(2,1)S(1)} %bitcast.58, bf16[16,128,256]{2,1,0:T(8,128)(2,1)} %collective-permute-done.other, bf16[2048,384]{1,0:T(8,128)(2,1)} %bitcast.16.held), custom_call_target="tpu_custom_call" | custom-call | flops 805306368 | bytes 3670016 | tf_op jit(solution)/shard_map/pallas_call | solution.py:125
  167.0 5.0 %collective-permute-start.4 = (bf16[384,256]{1,0:T(8,128)(2,1)S(1)}, bf16[384,256]{1,0:T(8,128)(2,1)S(1)}, u32[]{:S(2)}, u32[]{:S(2)}) collective-permute-start(bf16[384,256]{1,0:T(8,128)(2,1)S(1)} %get-tuple-element.36), channel_id=1, source_target_pairs={{0,1},{1,0},{2,3},{3,2},{4,5},{5,4},{6,7},{7,6},{8,9},{9,8},{10,11... | collective-permute-start | bytes 589832 | tf_op jit(solution)/shard_map/ppermute | solution.py:37
  171.9 1.0 collective-permute-done.4
  173.7 3.1 %shard_map.142 = bf16[32,128,256]{2,1,0:T(8,128)(2,1)} custom-call(s32[1]{0:T(128)} %bitcast.6.place, bf16[8,512,256]{2,1,0:T(8,128)(2,1)} %bitcast.61), custom_call_target="tpu_custom_call" | custom-call | bytes 4194304 | tf_op jit(solution)/shard_map/pallas_call | solution.py:160
  (64 shorter events, 6.3 us)
Async XLA Ops:
  8.0 4.4 %copy-start = (bf16[1000,256]{1,0:T(8,128)(2,1)S(1)}, bf16[1000,256]{1,0:T(8,128)(2,1)}, u32[]{:S(2)}) copy-start(bf16[1000,256]{1,0:T(8,128)(2,1)} %param.20) | copy-start | bytes 1536004
  8.0 52.2 %all-gather.4.cloned.1.call-start = ((), (), s32[]{:S(2)}) async-start(), calls=%async_computation.5 | async-start | bytes 1769472 | tf_op jit(solution)/shard_map/all_gather | solution.py:224
  10.2 2.4 %copy-start.5 = (f32[384,384]{0,1:T(8,128)}, f32[384,384]{0,1:T(8,128)S(1)}, u32[]{:S(2)}) copy-start(f32[384,384]{0,1:T(8,128)S(1)} %get-tuple-element.40) | copy-start | bytes 1769476
  10.3 2.2 %copy-start.10 = (s32[8]{0:T(128)S(1)}, s32[8]{0:T(128)}, u32[]{:S(2)}) copy-start(s32[8]{0:T(128)} %param.19) | copy-start | bytes 100
  10.4 2.3 %copy-start.12 = (bf16[16,256]{1,0:T(8,128)(2,1)S(1)}, bf16[16,256]{1,0:T(8,128)(2,1)}, u32[]{:S(2)}) copy-start(bf16[16,256]{1,0:T(8,128)(2,1)} %param.21) | copy-start | bytes 24580
  10.4 2.3 %copy-start.15 = (s32[8]{0:T(128)S(1)}, s32[8]{0:T(128)}, u32[]{:S(2)}) copy-start(s32[8]{0:T(128)} %param.18) | copy-start | bytes 100
  10.4 2.5 %copy-start.13 = (bf16[8,256]{1,0:T(8,128)(2,1)S(1)}, bf16[8,256]{1,0:T(8,128)(2,1)}, u32[]{:S(2)}) copy-start(bf16[8,256]{1,0:T(8,128)(2,1)} %param.22) | copy-start | bytes 12292
  10.4 2.5 %copy-start.16 = (s32[8]{0:T(128)S(1)}, s32[8]{0:T(128)}, u32[]{:S(2)}) copy-start(s32[8]{0:T(128)} %param.17) | copy-start | bytes 100
  10.4 2.6 %copy-start.14 = (bf16[8,256]{1,0:T(8,128)(2,1)S(1)}, bf16[8,256]{1,0:T(8,128)(2,1)}, u32[]{:S(2)}) copy-start(bf16[8,256]{1,0:T(8,128)(2,1)} %param.23) | copy-start | bytes 12292
  10.4 2.6 %copy-start.17 = (s32[8]{0:T(128)S(1)}, s32[8]{0:T(128)}, u32[]{:S(2)}) copy-start(s32[8]{0:T(128)} %param.16) | copy-start | bytes 100
  10.5 2.8 %copy-start.8 = (bf16[384,256]{1,0:T(8,128)(2,1)S(1)}, bf16[384,256]{1,0:T(8,128)(2,1)}, u32[]{:S(2)}) copy-start(bf16[384,256]{1,0:T(8,128)(2,1)} %param.14) | copy-start | bytes 589828
  10.5 4.0 %copy-start.1 = (bf16[4096,256]{1,0:T(8,128)(2,1)S(1)}, bf16[4096,256]{1,0:T(8,128)(2,1)}, u32[]{:S(2)}) copy-start(bf16[4096,256]{1,0:T(8,128)(2,1)} %param.13) | copy-start | bytes 6291460
  14.4 3.7 %copy-start.3 = (bf16[384,256]{1,0:T(8,128)(2,1)S(1)}, bf16[384,256]{1,0:T(8,128)(2,1)}, u32[]{:S(2)}) copy-start(bf16[384,256]{1,0:T(8,128)(2,1)} %get-tuple-element.27.gated) | copy-start | bytes 589828
  15.5 16.5 %collective-permute-start = (bf16[16,128,256]{2,1,0:T(8,128)(2,1)}, bf16[16,128,256]{2,1,0:T(8,128)(2,1)}, u32[]{:S(2)}, u32[]{:S(2)}) collective-permute-start(bf16[16,128,256]{2,1,0:T(8,128)(2,1)} %dynamic-slice_bitcast_fusion), channel_id=1, source_target_pairs={{0,1},{1,0},{2,3},{3,2},{4,5},{5,4},{6,7},{7,6},{8,9},{9,8},{10,11... | collective-permute-start | bytes 3145736 | tf_op jit(solution)/shard_map/ppermute | solution.py:37
  18.1 13.9 %collective-permute-start.1 = (bf16[384,256]{1,0:T(8,128)(2,1)S(1)}, bf16[384,256]{1,0:T(8,128)(2,1)S(1)}, u32[]{:S(2)}, u32[]{:S(2)}) collective-permute-start(bf16[384,256]{1,0:T(8,128)(2,1)S(1)} %copy-done.3), channel_id=1, source_target_pairs={{0,1},{1,0},{2,3},{3,2},{4,5},{5,4},{6,7},{7,6},{8,9},{9,8},{10,11... | collective-permute-start | bytes 589832 | tf_op jit(solution)/shard_map/ppermute | solution.py:37
  20.0 16.8 %all-to-all-start = ((bf16[8,16,384]{2,1,0:T(8,128)(2,1)}), bf16[8,16,384]{2,1,0:T(8,128)(2,1)S(1)}, u32[]{:S(2)}, u32[]{:S(2)}) async-start(bf16[8,16,384]{2,1,0:T(8,128)(2,1)} %bitcast.10), calls=%async_computation | async-start | bytes 196608 | tf_op jit(solution)/shard_map/all_to_all | solution.py:226
  32.0 39.1 %reduce-scatter.3.cloned.1.call-start = ((), (), s32[]{:S(2)}) async-start(), calls=%async_computation.6 | async-start | bytes 1966080 | tf_op jit(solution)/shard_map/reduce_scatter | solution.py:230
  35.2 1.1 copy-start.2
  60.2 31.7 %collective-permute-start.2 = (bf16[3072,256]{1,0:T(8,128)(2,1)}, bf16[3072,256]{1,0:T(8,128)(2,1)}, u32[]{:S(2)}, u32[]{:S(2)}) collective-permute-start(bf16[3072,256]{1,0:T(8,128)(2,1)} %all-gather.4.cloned.1.call-done.mine), channel_id=1, source_target_pairs={{0,1},{1,0},{2,3},{3,2},{4,5},{5,4},{6,7},{7,6},{8,9},{9,8},{10,11... | collective-permute-start | bytes 4718600 | tf_op jit(solution)/shard_map/ppermute | solution.py:37
  66.6 25.3 %all-to-all-start.1 = ((bf16[4,512,384]{2,1,0:T(8,128)(2,1)}), bf16[4,512,384]{2,1,0:T(8,128)(2,1)}, u32[]{:S(2)}, u32[]{:S(2)}) async-start(bf16[4,512,384]{2,1,0:T(8,128)(2,1)} %bitcast.12), calls=%async_computation.1 | async-start | bytes 3145728 | tf_op jit(solution)/shard_map/all_to_all | solution.py:41
  71.0 74.4 %reduce-scatter.5.cloned.1.call-start = ((), (), s32[]{:S(2)}) async-start(), calls=%async_computation.7 | async-start | bytes 491520 | tf_op jit(solution)/shard_map/reduce_scatter | solution.py:245
  71.6 102.2 %all-gather.6.cloned.1.call-start = ((), (), s32[]{:S(2)}) async-start(), calls=%async_computation.8 | async-start | bytes 2359296 | tf_op jit(solution)/shard_map/all_gather | solution.py:242
  91.9 1.4 copy-start.4
  96.3 3.7 %collective-permute-start.3 = (bf16[256,256]{1,0:T(8,128)(2,1)S(1)}, bf16[256,256]{1,0:T(8,128)(2,1)S(1)}, u32[]{:S(2)}, u32[]{:S(2)}) collective-permute-start(bf16[256,256]{1,0:T(8,128)(2,1)S(1)} %get-tuple-element.31), channel_id=1, source_target_pairs={{0,1},{1,0},{2,3},{3,2},{4,5},{5,4},{6,7},{7,6},{8,9},{9,8},{10,11... | collective-permute-start | bytes 393224 | tf_op jit(solution)/shard_map/ppermute | solution.py:37
  138.6 6.8 %copy-start.6 = (f32[384,384]{0,1:T(8,128)S(1)}, f32[384,384]{0,1:T(8,128)}, u32[]{:S(2)}) copy-start(f32[384,384]{0,1:T(8,128)} %copy-done.5) | copy-start | bytes 1769476
  138.6 6.8 %copy-start.9 = (bf16[384,3,128]{2,0,1:T(8,128)(2,1)S(1)}, bf16[384,3,128]{2,0,1:T(8,128)(2,1)}, u32[]{:S(2)}) copy-start(bf16[384,3,128]{2,0,1:T(8,128)(2,1)} %param.12) | copy-start | bytes 884740
  138.6 25.6 %all-to-all-start.2 = ((bf16[4,512,384]{2,1,0:T(8,128)(2,1)}), bf16[4,512,384]{2,1,0:T(8,128)(2,1)}, u32[]{:S(2)}, u32[]{:S(2)}) async-start(bf16[4,512,384]{2,1,0:T(8,128)(2,1)} %bitcast.59), calls=%async_computation.2 | async-start | bytes 3145728 | tf_op jit(solution)/shard_map/all_to_all | solution.py:41
  146.5 0.9 copy-start.11
  164.2 8.8 %copy-start.7 = (f32[384,256]{1,0:T(8,128)S(1)}, f32[384,256]{1,0:T(8,128)}, u32[]{:S(2)}) copy-start(f32[384,256]{1,0:T(8,128)} %get-tuple-element.42) | copy-start | bytes 1179652
  167.0 6.0 %collective-permute-start.4 = (bf16[384,256]{1,0:T(8,128)(2,1)S(1)}, bf16[384,256]{1,0:T(8,128)(2,1)S(1)}, u32[]{:S(2)}, u32[]{:S(2)}) collective-permute-start(bf16[384,256]{1,0:T(8,128)(2,1)S(1)} %get-tuple-element.36), channel_id=1, source_target_pairs={{0,1},{1,0},{2,3},{3,2},{4,5},{5,4},{6,7},{7,6},{8,9},{9,8},{10,11... | collective-permute-start | bytes 589832 | tf_op jit(solution)/shard_map/ppermute | solution.py:37
Sparse Core Ops, SparseCore 0:
  14.6 45.5 all-gather.3
  119.9 40.1 all-gather.5
Sparse Core Ops, SparseCore 1:
  36.9 33.6 reduce-scatter.2
  74.6 36.8 reduce-scatter.4

commit v8 on v7

--- a/solution.py
+++ b/solution.py
@@ -110,30 +110,35 @@
     )(held, mine, theirs)
 
 
-def mix_body(place, weight, other, held, out_mine, out_theirs):
-    core = place[0]
-    heads = [z * NX + x for x in range(NX) for z in range(NZHI)]
+def mix_body(place, weight, other, *refs):
+    *pieces, out_mine, out_theirs = refs
+    core, x = place[0], place[1]
+    held = jnp.concatenate([piece[...] for piece in pieces])
+    heads = []
+    for i in range(NX):
+        chip = lax.rem(x + NX - i, NX)
+        heads += [z * NX + chip for z in range(NZHI)]
     theirs = jnp.concatenate([other[head] for head in heads])
-    out_theirs[...] = dot(held[...], theirs, ((0,), (0,))).astype(BF)
+    out_theirs[...] = dot(held, theirs, ((0,), (0,))).astype(BF)
     mine = jnp.concatenate([weight[head * NCORE + core] for head in heads])
-    out_mine[...] = dot(held[...], mine, ((0,), (0,)))
-
-
-def mix_part(place, weight, other, held):
-    rows, toks = held.shape
-    width = weight.shape[2]
+    out_mine[...] = dot(held, mine, ((0,), (0,)))
+
+
+def mix_part(place, weight, other, pieces):
+    toks, width = pieces[0].shape[1], weight.shape[2]
+    rows = sum(p.shape[0] for p in pieces)
     return call(
         mix_body,
         (
             jax.ShapeDtypeStruct((toks, width), F32),
             jax.ShapeDtypeStruct((toks, width), BF),
         ),
-        [SMEM] + [VMEM] * 3,
+        [SMEM] + [VMEM] * (2 + len(pieces)),
         (VMEM, VMEM),
         4 * rows * toks * width,
         2 * rows * (toks + 2 * width),
         limit=16,
-    )(place, weight, other, held)
+    )(place, weight, other, *pieces)
 
 
 def place_body(place, src, dst, taken, given, in_sems, out_sems):
@@ -191,7 +196,7 @@
     width = cotangent.shape[1]
     factor = HEAD ** (-0.5)
     core = lax.axis_index("core")
-    place = core.reshape(1).astype(jnp.int32)
+    place = jnp.stack([core, lax.axis_index("x")]).astype(jnp.int32)
     weight = out_weight.reshape(-1, HEAD, width)
 
     other = weight.reshape(-1, NCORE, HEAD, width)
@@ -232,20 +237,25 @@
     own = lax.all_gather(attended, "zhi", axis=0, tiled=True)
     own = jnp.concatenate([own] * NX)
     gated_y = after(gated_y, own)
+    natural = after(natural, own)
     own = gather_x(own)
+
+    whole = lax.all_gather(natural, "zhi", axis=0, tiled=True)
+    own, whole = lax.optimization_barrier((own, whole))
     theirs_y = shift(gated_y, "core", NCORE, 1)
 
     total, swap = weight_part(own, gated_y, theirs_y)
     total = jnp.concatenate([total, shift(swap, "core", NCORE, 1)])
     total = lax.all_gather(total, "zlo").astype(F32).sum(0).astype(BF)
-    natural, total = lax.optimization_barrier((natural, total))
+    whole = after(whole, total)
+    summed = after(summed, total)
     total = lax.all_gather(total, "y", axis=0, tiled=True)
     total = put_heads(place, total)
 
-    summed = lax.psum_scatter(summed, "zhi", scatter_dimension=0, tiled=True)
-
-    whole = lax.all_gather(natural, "zhi", axis=0, tiled=True)
-    whole = gather_x(jnp.concatenate([whole] * NX))
+    summed = lax.all_to_all(summed, "zhi", split_axis=0, concat_axis=0, tiled=True)
+    summed = summed.reshape(NZHI, HEAD, toks).astype(F32).sum(0).astype(BF)
+
+    whole = [whole] + [shift(whole, "x", NX, i) for i in (1, 2, 3)]
 
     upstream = summed.T
     grad_values = dot(rounded, upstream, ((0,), (0,))).astype(BF)
@@ -256,7 +266,7 @@
     grad_keys = (dot(grad_scores, queries, ((0,), (0,))) * factor).astype(BF)
     grad_qkv = jnp.stack([grad_queries, grad_keys, grad_values], axis=1)
 
-    whole, grad_qkv = lax.optimization_barrier((whole, grad_qkv))
+    *whole, grad_qkv = lax.optimization_barrier((*whole, grad_qkv))
     mixed, swap = mix_part(place, weight, other, whole)
     mixed = (gate * (mixed + shift(swap, "core", NCORE, 1).astype(F32))).astype(BF)
     return (mixed, grad_qkv, total)

time: 185 us -> 177 us (0.957)
  the two profiles are of different devices: /device:TPU:49 before, /device:TPU:2 now
where the time goes in v8:
time: 177 us; the launch traced here: 176 us
  blocking collectives  65.7 us (37%)
  starting transfers between devices  39.5 us (22%)
  waiting for transfers between devices  23 us (13%)
  between operations  15.8 us (9%)
  Pallas kernels  12.3 us (7%)
  matrix products  7.34 us (4%)
  local copies, waits for them, and re-layouts  6.9 us (4%)
  other arithmetic  5.9 us (3%)
    all_gather x1, blocking collectives, on_device(): own = lax.all_gather(attended, 'zhi', axis=0, tiled=True)  26.2 us
    all_gather x1, blocking collectives, on_device(): whole = lax.all_gather(natural, 'zhi', axis=0, tiled=True)  23.7 us
    ppermute x8, starting transfers between devices, shift(): lax.ppermute(value, axis, [(i, (i + step) % size) for i in range(size)])  19.9 us
    all_gather x1, blocking collectives, on_device(): total = lax.all_gather(total, 'zlo').astype(F32).sum(0).astype(BF)  15.8 us
    all_to_all x1, waiting for transfers between devices, on_device(): lax.all_to_all(summed, 'zhi', split_axis=0, concat_axis=0, tiled=True)  9.42 us
    all_to_all x1, starting transfers between devices, on_device(): lax.all_to_all(summed, 'zhi', split_axis=0, concat_axis=0, tiled=True)  7.5 us
    all_to_all x1, starting transfers between devices, on_device(): lax.all_to_all(attended, 'y', split_axis=0, concat_axis=0, tiled=True)  7.11 us
    dot_general x6, matrix products, dot(): return lax.dot_general(a, b, (dims, ((), ())), preferred_element_type=F32)  5.39 us
  transfers between devices with their start and end apart: 14, of which 7 were waited for; matrix products, arithmetic and copies ran while one was open for 6% of the time, Pallas kernels for 5%

profile of v8, /device:TPU:2, one launch (start us, length us, event | category | flops | bytes accessed | tf_op | source)
XLA Modules:
  0.0 176.4 jit_solution(12204998208632691826)
XLA Ops:
  9.0 1.2 fusion.33
  10.5 2.0 %fusion.3 = bf16[128,384]{1,0:T(8,128)(2,1)} fusion(bf16[384,3,128]{2,0,1:T(8,128)(2,1)} %param.12, f32[384,384]{0,1:T(8,128)S(1)} %get-tuple-element.52, f32[384]{0:T(512)S(1)} %fusion.8, f32[384]{0:T(512)S(1)} %get-tuple-element.51), kind=kOutput, calls=%fused_computation.8 | convolution fusion | flops 38240256 | bytes 789504 | tf_op jit(solution)/shard_map/dot_general | solution.py:33
  13.3 1.2 multiply_convert_fusion.2
  14.5 1.1 dynamic-slice_bitcast_fusion
  15.5 1.9 %collective-permute-start = (bf16[16,128,256]{2,1,0:T(8,128)(2,1)}, bf16[16,128,256]{2,1,0:T(8,128)(2,1)}, u32[]{:S(2)}, u32[]{:S(2)}) collective-permute-start(bf16[16,128,256]{2,1,0:T(8,128)(2,1)} %dynamic-slice_bitcast_fusion), channel_id=1, source_target_pairs={{0,1},{1,0},{2,3},{3,2},{4,5},{5,4},{6,7},{7,6},{8,9},{9,8},{10,11... | collective-permute-start | bytes 3145736 | tf_op jit(solution)/shard_map/ppermute | solution.py:37
  17.5 2.4 %collective-permute-start.1 = (bf16[384,256]{1,0:T(8,128)(2,1)S(1)}, bf16[384,256]{1,0:T(8,128)(2,1)S(1)}, u32[]{:S(2)}, u32[]{:S(2)}) collective-permute-start(bf16[384,256]{1,0:T(8,128)(2,1)S(1)} %copy-done.3), channel_id=1, source_target_pairs={{0,1},{1,0},{2,3},{3,2},{4,5},{5,4},{6,7},{7,6},{8,9},{9,8},{10,11... | collective-permute-start | bytes 589832 | tf_op jit(solution)/shard_map/ppermute | solution.py:37
  19.9 7.1 %all-to-all-start = ((bf16[8,16,384]{2,1,0:T(8,128)(2,1)}), bf16[8,16,384]{2,1,0:T(8,128)(2,1)S(1)}, u32[]{:S(2)}, u32[]{:S(2)}) async-start(bf16[8,16,384]{2,1,0:T(8,128)(2,1)} %bitcast.11), calls=%async_computation | async-start | bytes 196608 | tf_op jit(solution)/shard_map/all_to_all | solution.py:231
  27.1 3.2 %shard_map.139 = bf16[2048,384]{1,0:T(8,128)(2,1)S(1)} custom-call(s32[2]{0:T(128)S(1)} %pad_add_fusion.place, bf16[32,128,256]{2,1,0:T(8,128)(2,1)S(1)} %bitcast.57, bf16[16,128,256]{2,1,0:T(8,128)(2,1)} %collective-permute-done.other, bf16[384,256]{1,0:T(8,128)(2,1)S(1)} %copy-done.3, bf16[384,256]{1,0:T(8,128)(2,1)S(1)} %collective-permute-done.1.theirs), custom_call_target="tpu_custom_call" | custom-call | flops 805306368 | bytes 3145728 | tf_op jit(solution)/shard_map/pallas_call | solution.py:74
  30.3 1.1 copy-done.2
  31.5 4.3 %all-to-all-done = bf16[8,16,384]{2,1,0:T(8,128)(2,1)S(1)} async-done(((bf16[8,16,384]{2,1,0:T(8,128)(2,1)}), bf16[8,16,384]{2,1,0:T(8,128)(2,1)S(1)}, u32[]{:S(2)}, u32[]{:S(2)}) %all-to-all-start) | async-done | bytes 98336 | tf_op jit(solution)/shard_map/all_to_all | solution.py:231
  35.8 26.2 %all_gather.18 = bf16[512,384]{1,0:T(8,128)(2,1)S(1)} all-gather(bf16[128,384]{1,0:T(8,128)(2,1)S(1)} %bitcast.63), channel_id=1, replica_groups=mesh['zlo'=3,'y'=8,'zhi'=4,'x'=4,'core'=2] {'zhi'}, dimensions={0}, use_global_device_ids=true | all-gather | bytes 491520 | tf_op jit(solution)/shard_map/all_gather | solution.py:237
  65.2 1.4 all-gather.4.cloned.1.call-done.mine
  66.6 1.9 %collective-permute-start.2 = (bf16[3072,256]{1,0:T(8,128)(2,1)}, bf16[3072,256]{1,0:T(8,128)(2,1)}, u32[]{:S(2)}, u32[]{:S(2)}) collective-permute-start(bf16[3072,256]{1,0:T(8,128)(2,1)} %all-gather.4.cloned.1.call-done.mine), channel_id=1, source_target_pairs={{0,1},{1,0},{2,3},{3,2},{4,5},{5,4},{6,7},{7,6},{8,9},{9,8},{10,11... | collective-permute-start | bytes 4718600 | tf_op jit(solution)/shard_map/ppermute | solution.py:37
  68.5 4.9 %all-to-all-start.1 = ((bf16[4,512,384]{2,1,0:T(8,128)(2,1)}), bf16[4,512,384]{2,1,0:T(8,128)(2,1)}, u32[]{:S(2)}, u32[]{:S(2)}) async-start(bf16[4,512,384]{2,1,0:T(8,128)(2,1)} %bitcast.13), calls=%async_computation.1 | async-start | bytes 3145728 | tf_op jit(solution)/shard_map/all_to_all | solution.py:41
  73.4 23.7 %all_gather.19.refs_0_ = bf16[512,384]{1,0:T(8,128)(2,1)S(1)} all-gather(bf16[128,384]{1,0:T(8,128)(2,1)} %fusion.3), channel_id=1, replica_groups=mesh['zlo'=3,'y'=8,'zhi'=4,'x'=4,'core'=2] {'zhi'}, dimensions={0}, use_global_device_ids=true | all-gather | bytes 491520 | tf_op jit(solution)/shard_map/all_gather | solution.py:243
  97.1 1.4 copy-done.4
  98.5 2.9 %shard_map.140 = (bf16[256,256]{1,0:T(8,128)(2,1)S(1)}, bf16[256,256]{1,0:T(8,128)(2,1)S(1)}) custom-call(bf16[2048,384]{1,0:T(8,128)(2,1)} %bitcast.14.held, bf16[3072,256]{1,0:T(8,128)(2,1)S(1)} %copy-done.4, bf16[3072,256]{1,0:T(8,128)(2,1)} %collective-permute-done.2.theirs), custom_call_target="tpu_custom_call" | custom-call | flops 805306368 | bytes 4718592 | tf_op jit(solution)/shard_map/pallas_call | solution.py:101
  101.4 1.9 %collective-permute-start.3 = (bf16[256,256]{1,0:T(8,128)(2,1)S(1)}, bf16[256,256]{1,0:T(8,128)(2,1)S(1)}, u32[]{:S(2)}, u32[]{:S(2)}) collective-permute-start(bf16[256,256]{1,0:T(8,128)(2,1)S(1)} %get-tuple-element.40), channel_id=1, source_target_pairs={{0,1},{1,0},{2,3},{3,2},{4,5},{5,4},{6,7},{7,6},{8,9},{9,8},{10,11... | collective-permute-start | bytes 393224 | tf_op jit(solution)/shard_map/ppermute | solution.py:37
  103.3 1.3 collective-permute-done.3
  104.6 15.8 %all-gather = bf16[1536,256]{1,0:T(8,128)(2,1)} all-gather(bf16[512,256]{1,0:T(8,128)(2,1)S(1)} %pad_maximum_fusion.1), channel_id=2, replica_groups=mesh['zlo'=3,'y'=8,'zhi'=4,'x'=4,'core'=2] {'zlo'}, dimensions={0}, use_global_device_ids=true | all-gather | bytes 1048576 | tf_op jit(solution)/shard_map/all_gather | solution.py:249
  120.4 2.0 %reduce_sum.53 = bf16[512,256]{1,0:T(8,128)(2,1)} reduce(bf16[3,512,256]{2,1,0:T(8,128)(2,1)} %bitcast.59, bf16[]{:T(256)} %constant.32.clone.1), dimensions={0}, to_apply=%region_4.5 | reduce | flops 262144 | bytes 1048578 | tf_op jit(solution)/shard_map/reduce_sum | solution.py:249
  122.5 7.5 %all-to-all-start.2 = ((bf16[4,128,384]{2,1,0:T(8,128)(2,1)}), bf16[4,128,384]{2,1,0:T(8,128)(2,1)}, u32[]{:S(2)}, u32[]{:S(2)}) async-start(bf16[4,128,384]{2,1,0:T(8,128)(2,1)} %bitcast.62), calls=%async_computation.3 | async-start | bytes 786432 | tf_op jit(solution)/shard_map/all_to_all | solution.py:255
  130.0 3.4 %collective-permute-start.6 = (bf16[512,384]{1,0:T(8,128)(2,1)S(1)}, bf16[512,384]{1,0:T(8,128)(2,1)S(1)}, u32[]{:S(2)}, u32[]{:S(2)}) collective-permute-start(bf16[512,384]{1,0:T(8,128)(2,1)S(1)} %all_gather.19.refs_0_), channel_id=1, source_target_pairs={{0,6},{2,0},{4,2},{6,4},{1,7},{3,1},{5,3},{7,5},{8,14},{10,8},{12,... | collective-permute-start | bytes 1179656 | tf_op jit(solution)/shard_map/ppermute | solution.py:37
  133.3 2.7 %collective-permute-start.5 = (bf16[512,384]{1,0:T(8,128)(2,1)S(1)}, bf16[512,384]{1,0:T(8,128)(2,1)}, u32[]{:S(2)}, u32[]{:S(2)}) collective-permute-start(bf16[512,384]{1,0:T(8,128)(2,1)S(1)} %all_gather.19.refs_0_), channel_id=1, source_target_pairs={{0,4},{2,6},{4,0},{6,2},{1,5},{3,7},{5,1},{7,3},{8,12},{10,14},{12... | collective-permute-start | bytes 1179656 | tf_op jit(solution)/shard_map/ppermute | solution.py:37
  136.1 3.7 %collective-permute-start.4 = (bf16[512,384]{1,0:T(8,128)(2,1)S(1)}, bf16[512,384]{1,0:T(8,128)(2,1)}, u32[]{:S(2)}, u32[]{:S(2)}) collective-permute-start(bf16[512,384]{1,0:T(8,128)(2,1)S(1)} %all_gather.19.refs_0_), channel_id=1, source_target_pairs={{0,2},{2,4},{4,6},{6,0},{1,3},{3,5},{5,7},{7,1},{8,10},{10,12},{12... | collective-permute-start | bytes 1179656 | tf_op jit(solution)/shard_map/ppermute | solution.py:37
  139.8 9.4 %all-to-all-done.2 = bf16[4,128,384]{2,1,0:T(8,128)(2,1)} async-done(((bf16[4,128,384]{2,1,0:T(8,128)(2,1)}), bf16[4,128,384]{2,1,0:T(8,128)(2,1)}, u32[]{:S(2)}, u32[]{:S(2)}) %all-to-all-start.2) | async-done | bytes 393248 | tf_op jit(solution)/shard_map/all_to_all | solution.py:255
  150.3 1.4 multiply_reduce_fusion
  153.8 2.5 %shard_map.141 = (f32[384,256]{1,0:T(8,128)S(1)}, bf16[384,256]{1,0:T(8,128)(2,1)S(1)}) custom-call(s32[2]{0:T(128)S(1)} %pad_add_fusion.place, bf16[32,128,256]{2,1,0:T(8,128)(2,1)S(1)} %bitcast.58, bf16[16,128,256]{2,1,0:T(8,128)(2,1)} %collective-permute-done.other, bf16[512,384]{1,0:T(8,128)(2,1)S(1)} %all_gather.19.refs_0_, ...), custom_call_target="tpu_custom_call" | custom-call | flops 805306368 | bytes 3670016 | tf_op jit(solution)/shard_map/pallas_call | solution.py:130
  156.3 1.9 %collective-permute-start.7 = (bf16[384,256]{1,0:T(8,128)(2,1)S(1)}, bf16[384,256]{1,0:T(8,128)(2,1)S(1)}, u32[]{:S(2)}, u32[]{:S(2)}) collective-permute-start(bf16[384,256]{1,0:T(8,128)(2,1)S(1)} %get-tuple-element.49), channel_id=1, source_target_pairs={{0,1},{1,0},{2,3},{3,2},{4,5},{5,4},{6,7},{7,6},{8,9},{9,8},{10,11... | collective-permute-start | bytes 589832 | tf_op jit(solution)/shard_map/ppermute | solution.py:37
  158.2 1.4 collective-permute-done.7
  160.4 4.8 %all-gather.6.cloned.1.call-done = bf16[4096,256]{1,0:T(8,128)(2,1)} async-done(((bf16[512,256]{1,0:T(8,128)(2,1)}), bf16[4096,256]{1,0:T(8,128)(2,1)}) %all-gather.6.cloned.1.call-update) | async-done | bytes 2097168 | tf_op jit(solution)/shard_map/all_gather | solution.py:252
  165.2 3.8 %shard_map.142 = bf16[32,128,256]{2,1,0:T(8,128)(2,1)} custom-call(s32[2]{0:T(128)} %copy-done.5, bf16[8,512,256]{2,1,0:T(8,128)(2,1)} %bitcast.60), custom_call_target="tpu_custom_call" | custom-call | bytes 4194304 | tf_op jit(solution)/shard_map/pallas_call | solution.py:165
  (68 shorter events, 9.2 us)
Async XLA Ops:
  8.0 4.4 %copy-start = (bf16[1000,256]{1,0:T(8,128)(2,1)S(1)}, bf16[1000,256]{1,0:T(8,128)(2,1)}, u32[]{:S(2)}) copy-start(bf16[1000,256]{1,0:T(8,128)(2,1)} %param.20) | copy-start | bytes 1536004
  8.0 58.5 %all-gather.4.cloned.1.call-start = ((), (), s32[]{:S(2)}) async-start(), calls=%async_computation.4 | async-start | bytes 1769472 | tf_op jit(solution)/shard_map/all_gather | solution.py:229
  10.2 2.4 %copy-start.6 = (f32[384,384]{0,1:T(8,128)}, f32[384,384]{0,1:T(8,128)S(1)}, u32[]{:S(2)}) copy-start(f32[384,384]{0,1:T(8,128)S(1)} %get-tuple-element.52) | copy-start | bytes 1769476
  10.3 2.2 %copy-start.11 = (s32[8]{0:T(128)S(1)}, s32[8]{0:T(128)}, u32[]{:S(2)}) copy-start(s32[8]{0:T(128)} %param.19) | copy-start | bytes 100
  10.4 2.3 %copy-start.12 = (bf16[16,256]{1,0:T(8,128)(2,1)S(1)}, bf16[16,256]{1,0:T(8,128)(2,1)}, u32[]{:S(2)}) copy-start(bf16[16,256]{1,0:T(8,128)(2,1)} %param.21) | copy-start | bytes 24580
  10.4 2.3 %copy-start.15 = (s32[8]{0:T(128)S(1)}, s32[8]{0:T(128)}, u32[]{:S(2)}) copy-start(s32[8]{0:T(128)} %param.18) | copy-start | bytes 100
  10.4 2.5 %copy-start.13 = (bf16[8,256]{1,0:T(8,128)(2,1)S(1)}, bf16[8,256]{1,0:T(8,128)(2,1)}, u32[]{:S(2)}) copy-start(bf16[8,256]{1,0:T(8,128)(2,1)} %param.22) | copy-start | bytes 12292
  10.4 2.5 %copy-start.16 = (s32[8]{0:T(128)S(1)}, s32[8]{0:T(128)}, u32[]{:S(2)}) copy-start(s32[8]{0:T(128)} %param.17) | copy-start | bytes 100
  10.4 2.6 %copy-start.14 = (bf16[8,256]{1,0:T(8,128)(2,1)S(1)}, bf16[8,256]{1,0:T(8,128)(2,1)}, u32[]{:S(2)}) copy-start(bf16[8,256]{1,0:T(8,128)(2,1)} %param.23) | copy-start | bytes 12292
  10.4 2.6 %copy-start.17 = (s32[8]{0:T(128)S(1)}, s32[8]{0:T(128)}, u32[]{:S(2)}) copy-start(s32[8]{0:T(128)} %param.16) | copy-start | bytes 100
  10.5 2.8 %copy-start.9 = (bf16[384,256]{1,0:T(8,128)(2,1)S(1)}, bf16[384,256]{1,0:T(8,128)(2,1)}, u32[]{:S(2)}) copy-start(bf16[384,256]{1,0:T(8,128)(2,1)} %param.14) | copy-start | bytes 589828
  10.5 4.0 %copy-start.1 = (bf16[4096,256]{1,0:T(8,128)(2,1)S(1)}, bf16[4096,256]{1,0:T(8,128)(2,1)}, u32[]{:S(2)}) copy-start(bf16[4096,256]{1,0:T(8,128)(2,1)} %param.13) | copy-start | bytes 6291460
  14.4 3.0 %copy-start.3 = (bf16[384,256]{1,0:T(8,128)(2,1)S(1)}, bf16[384,256]{1,0:T(8,128)(2,1)}, u32[]{:S(2)}) copy-start(bf16[384,256]{1,0:T(8,128)(2,1)} %get-tuple-element.33.gated) | copy-start | bytes 589828
  15.5 11.6 %collective-permute-start = (bf16[16,128,256]{2,1,0:T(8,128)(2,1)}, bf16[16,128,256]{2,1,0:T(8,128)(2,1)}, u32[]{:S(2)}, u32[]{:S(2)}) collective-permute-start(bf16[16,128,256]{2,1,0:T(8,128)(2,1)} %dynamic-slice_bitcast_fusion), channel_id=1, source_target_pairs={{0,1},{1,0},{2,3},{3,2},{4,5},{5,4},{6,7},{7,6},{8,9},{9,8},{10,11... | collective-permute-start | bytes 3145736 | tf_op jit(solution)/shard_map/ppermute | solution.py:37
  17.5 9.7 %collective-permute-start.1 = (bf16[384,256]{1,0:T(8,128)(2,1)S(1)}, bf16[384,256]{1,0:T(8,128)(2,1)S(1)}, u32[]{:S(2)}, u32[]{:S(2)}) collective-permute-start(bf16[384,256]{1,0:T(8,128)(2,1)S(1)} %copy-done.3), channel_id=1, source_target_pairs={{0,1},{1,0},{2,3},{3,2},{4,5},{5,4},{6,7},{7,6},{8,9},{9,8},{10,11... | collective-permute-start | bytes 589832 | tf_op jit(solution)/shard_map/ppermute | solution.py:37
  19.9 15.8 %all-to-all-start = ((bf16[8,16,384]{2,1,0:T(8,128)(2,1)}), bf16[8,16,384]{2,1,0:T(8,128)(2,1)S(1)}, u32[]{:S(2)}, u32[]{:S(2)}) async-start(bf16[8,16,384]{2,1,0:T(8,128)(2,1)} %bitcast.11), calls=%async_computation | async-start | bytes 196608 | tf_op jit(solution)/shard_map/all_to_all | solution.py:231
  27.0 95.4 %reduce-scatter.2.cloned.1.call-start = ((), (), s32[]{:S(2)}) async-start(), calls=%async_computation.5 | async-start | bytes 1966080 | tf_op jit(solution)/shard_map/reduce_scatter | solution.py:235
  27.1 126.7 %copy-start.5 = (s32[2]{0:T(128)}, s32[2]{0:T(128)S(1)}, u32[]{:S(2)}) copy-start(s32[2]{0:T(128)S(1)} %pad_add_fusion.place) | copy-start | bytes 28
  30.3 1.1 copy-start.2
  66.6 30.5 %collective-permute-start.2 = (bf16[3072,256]{1,0:T(8,128)(2,1)}, bf16[3072,256]{1,0:T(8,128)(2,1)}, u32[]{:S(2)}, u32[]{:S(2)}) collective-permute-start(bf16[3072,256]{1,0:T(8,128)(2,1)} %all-gather.4.cloned.1.call-done.mine), channel_id=1, source_target_pairs={{0,1},{1,0},{2,3},{3,2},{4,5},{5,4},{6,7},{7,6},{8,9},{9,8},{10,11... | collective-permute-start | bytes 4718600 | tf_op jit(solution)/shard_map/ppermute | solution.py:37
  68.5 28.6 %all-to-all-start.1 = ((bf16[4,512,384]{2,1,0:T(8,128)(2,1)}), bf16[4,512,384]{2,1,0:T(8,128)(2,1)}, u32[]{:S(2)}, u32[]{:S(2)}) async-start(bf16[4,512,384]{2,1,0:T(8,128)(2,1)} %bitcast.13), calls=%async_computation.1 | async-start | bytes 3145728 | tf_op jit(solution)/shard_map/all_to_all | solution.py:41
  73.4 91.8 %all-gather.6.cloned.1.call-start = ((), (), s32[]{:S(2)}) async-start(), calls=%async_computation.6 | async-start | bytes 2359296 | tf_op jit(solution)/shard_map/all_gather | solution.py:252
  97.0 1.4 copy-start.4
  101.4 3.2 %collective-permute-start.3 = (bf16[256,256]{1,0:T(8,128)(2,1)S(1)}, bf16[256,256]{1,0:T(8,128)(2,1)S(1)}, u32[]{:S(2)}, u32[]{:S(2)}) collective-permute-start(bf16[256,256]{1,0:T(8,128)(2,1)S(1)} %get-tuple-element.40), channel_id=1, source_target_pairs={{0,1},{1,0},{2,3},{3,2},{4,5},{5,4},{6,7},{7,6},{8,9},{9,8},{10,11... | collective-permute-start | bytes 393224 | tf_op jit(solution)/shard_map/ppermute | solution.py:37
  122.5 26.8 %all-to-all-start.2 = ((bf16[4,128,384]{2,1,0:T(8,128)(2,1)}), bf16[4,128,384]{2,1,0:T(8,128)(2,1)}, u32[]{:S(2)}, u32[]{:S(2)}) async-start(bf16[4,128,384]{2,1,0:T(8,128)(2,1)} %bitcast.62), calls=%async_computation.3 | async-start | bytes 786432 | tf_op jit(solution)/shard_map/all_to_all | solution.py:255
  130.0 23.5 %collective-permute-start.6 = (bf16[512,384]{1,0:T(8,128)(2,1)S(1)}, bf16[512,384]{1,0:T(8,128)(2,1)S(1)}, u32[]{:S(2)}, u32[]{:S(2)}) collective-permute-start(bf16[512,384]{1,0:T(8,128)(2,1)S(1)} %all_gather.19.refs_0_), channel_id=1, source_target_pairs={{0,6},{2,0},{4,2},{6,4},{1,7},{3,1},{5,3},{7,5},{8,14},{10,8},{12,... | collective-permute-start | bytes 1179656 | tf_op jit(solution)/shard_map/ppermute | solution.py:37
  133.3 20.1 %collective-permute-start.5 = (bf16[512,384]{1,0:T(8,128)(2,1)S(1)}, bf16[512,384]{1,0:T(8,128)(2,1)}, u32[]{:S(2)}, u32[]{:S(2)}) collective-permute-start(bf16[512,384]{1,0:T(8,128)(2,1)S(1)} %all_gather.19.refs_0_), channel_id=1, source_target_pairs={{0,4},{2,6},{4,0},{6,2},{1,5},{3,7},{5,1},{7,3},{8,12},{10,14},{12... | collective-permute-start | bytes 1179656 | tf_op jit(solution)/shard_map/ppermute | solution.py:37
  136.1 17.8 %collective-permute-start.4 = (bf16[512,384]{1,0:T(8,128)(2,1)S(1)}, bf16[512,384]{1,0:T(8,128)(2,1)}, u32[]{:S(2)}, u32[]{:S(2)}) collective-permute-start(bf16[512,384]{1,0:T(8,128)(2,1)S(1)} %all_gather.19.refs_0_), channel_id=1, source_target_pairs={{0,2},{2,4},{4,6},{6,0},{1,3},{3,5},{5,7},{7,1},{8,10},{10,12},{12... | collective-permute-start | bytes 1179656 | tf_op jit(solution)/shard_map/ppermute | solution.py:37
  150.3 1.5 copy-start.7
  150.3 1.6 copy-start.10
  153.5 6.2 %copy-start.8 = (f32[384,256]{1,0:T(8,128)S(1)}, f32[384,256]{1,0:T(8,128)}, u32[]{:S(2)}) copy-start(f32[384,256]{1,0:T(8,128)} %get-tuple-element.54) | copy-start | bytes 1179652
  156.3 3.3 %collective-permute-start.7 = (bf16[384,256]{1,0:T(8,128)(2,1)S(1)}, bf16[384,256]{1,0:T(8,128)(2,1)S(1)}, u32[]{:S(2)}, u32[]{:S(2)}) collective-permute-start(bf16[384,256]{1,0:T(8,128)(2,1)S(1)} %get-tuple-element.49), channel_id=1, source_target_pairs={{0,1},{1,0},{2,3},{3,2},{4,5},{5,4},{6,7},{7,6},{8,9},{9,8},{10,11... | collective-permute-start | bytes 589832 | tf_op jit(solution)/shard_map/ppermute | solution.py:37
Sparse Core Ops, SparseCore 0:
  14.6 51.9 all-gather.3
  122.5 42.5 all-gather.5
Sparse Core Ops, SparseCore 1:
  35.8 35.4 reduce-scatter.1

commit v9 on v8

--- a/solution.py
+++ b/solution.py
@@ -87,27 +87,28 @@
     return jnp.concatenate([held[start : start + SLAB, :] for start in starts])
 
 
-def part_body(held, mine, theirs, out_mine, out_theirs, rows):
+def part_body(held, gated, out_mine, out_theirs, rows):
     toks = held.shape[1]
     for y in range(NY):
         rows[:, y * toks : (y + 1) * toks] = slabs(held, y)
-    out_theirs[...] = dot(rows[...], theirs[...], ((1,), (0,))).astype(BF)
-    out_mine[...] = dot(rows[...], mine[...], ((1,), (0,))).astype(BF)
-
-
-def weight_part(held, mine, theirs):
+    width = out_mine.shape[1]
+    out_theirs[...] = dot(rows[...], gated[:, width:], ((1,), (0,))).astype(BF)
+    out_mine[...] = dot(rows[...], gated[:, :width], ((1,), (0,))).astype(BF)
+
+
+def weight_part(held, gated):
     rows = held.shape[0] // NY
-    toks, width = mine.shape
+    toks, width = gated.shape
     return call(
         part_body,
-        (jax.ShapeDtypeStruct((rows, width), BF),) * 2,
-        [VMEM] * 3,
+        (jax.ShapeDtypeStruct((rows, width // NCORE), BF),) * 2,
+        [VMEM] * 2,
         (VMEM, VMEM),
-        4 * rows * toks * width,
-        2 * rows * toks + 4 * toks * width,
+        2 * rows * toks * width,
+        2 * rows * toks + 2 * toks * width,
         [pltpu.VMEM((rows, toks), BF)],
         limit=16,
-    )(held, mine, theirs)
+    )(held, gated)
 
 
 def mix_body(place, weight, other, *refs):
@@ -226,25 +227,24 @@
     gated = (gate * cotangent.astype(F32)).astype(BF)
 
     attended, gated = lax.optimization_barrier((attended, gated))
-    gated_y = lax.all_gather(gated, "y", axis=0, tiled=True)
+    theirs = shift(gated, "core", NCORE, 1)
+    both = jnp.concatenate([gated, theirs], axis=1)
+    gated_y = lax.all_gather(both, "y", axis=0, tiled=True)
     natural = attended
     attended = lax.all_to_all(attended, "y", split_axis=0, concat_axis=0, tiled=True)
 
-    summed = upstream_part(place, weight, other, gated, shift(gated, "core", NCORE, 1))
+    summed = upstream_part(place, weight, other, gated, theirs)
     attended, summed = lax.optimization_barrier((attended, summed))
     summed = lax.psum_scatter(summed, "x", scatter_dimension=0, tiled=True)
 
     own = lax.all_gather(attended, "zhi", axis=0, tiled=True)
-    own = jnp.concatenate([own] * NX)
-    gated_y = after(gated_y, own)
     natural = after(natural, own)
-    own = gather_x(own)
+    own = gather_x(jnp.concatenate([own] * NX))
 
     whole = lax.all_gather(natural, "zhi", axis=0, tiled=True)
     own, whole = lax.optimization_barrier((own, whole))
-    theirs_y = shift(gated_y, "core", NCORE, 1)
-
-    total, swap = weight_part(own, gated_y, theirs_y)
+
+    total, swap = weight_part(own, gated_y)
     total = jnp.concatenate([total, shift(swap, "core", NCORE, 1)])
     total = lax.all_gather(total, "zlo").astype(F32).sum(0).astype(BF)
     whole = after(whole, total)

time: 177 us -> 174 us (0.983)
  blocking collectives: 65.7 us -> 61.6 us
  local copies, waits for them, and re-layouts: 6.9 us -> 4.18 us
  other arithmetic: 5.9 us -> 8.06 us
  waiting for transfers between devices: 23 us -> 24.8 us
    all_gather x1, blocking collectives: 23.7 us -> 19.2 us  [on_device(): whole = lax.all_gather(natural, 'zhi', axis=0, tiled=True)]
    all_to_all x1, starting transfers between devices: 7.5 us -> 10 us  [on_device(): lax.all_to_all(summed, 'zhi', split_axis=0, concat_axis=0, tiled=True)]
    ppermute x8 -> x7, starting transfers between devices: 19.9 us -> 17.7 us  [shift(): lax.ppermute(value, axis, [(i, (i + step) % size) for i in range(size)])]
    concatenate x0 -> x2, other arithmetic: none -> 2.16 us  [the longest x1 1.34 us: on_device(): own = gather_x(jnp.concatenate([own] * NX))]
    unnamed x39 -> x34, local copies, waits for them, and re-layouts: 5.03 us -> 3.1 us
    ppermute x8 -> x7, waiting for transfers between devices: 3.1 us -> 4.79 us  [shift(): lax.ppermute(value, axis, [(i, (i + step) % size) for i in range(size)])]
  transfers between devices with their start and end apart: 14 -> 13, of which waited for: 7 -> 7; matrix products, arithmetic and copies ran while one was open for 6% -> 5% of each run, Pallas kernels for 5% -> 5%
where the time goes in v9:
time: 174 us; the launch traced here: 173 us
  blocking collectives  61.6 us (35%)
  starting transfers between devices  39.8 us (23%)
  waiting for transfers between devices  24.8 us (14%)
  between operations  15.8 us (9%)
  Pallas kernels  11.9 us (7%)
  other arithmetic  8.06 us (5%)
  matrix products  7.44 us (4%)
  local copies, waits for them, and re-layouts  4.18 us (2%)
    all_gather x1, blocking collectives, on_device(): own = lax.all_gather(attended, 'zhi', axis=0, tiled=True)  26.1 us
    all_gather x1, blocking collectives, on_device(): whole = lax.all_gather(natural, 'zhi', axis=0, tiled=True)  19.2 us
    ppermute x7, starting transfers between devices, shift(): lax.ppermute(value, axis, [(i, (i + step) % size) for i in range(size)])  17.7 us
    all_gather x1, blocking collectives, on_device(): total = lax.all_gather(total, 'zlo').astype(F32).sum(0).astype(BF)  16.2 us
    all_to_all x1, starting transfers between devices, on_device(): lax.all_to_all(summed, 'zhi', split_axis=0, concat_axis=0, tiled=True)  10 us
    all_to_all x1, waiting for transfers between devices, on_device(): lax.all_to_all(summed, 'zhi', split_axis=0, concat_axis=0, tiled=True)  9.37 us
    all_to_all x1, starting transfers between devices, on_device(): lax.all_to_all(attended, 'y', split_axis=0, concat_axis=0, tiled=True)  7.13 us
    all_gather x1, waiting for transfers between devices, on_device(): total = lax.all_gather(total, 'y', axis=0, tiled=True)  6.11 us
  transfers between devices with their start and end apart: 13, of which 7 were waited for; matrix products, arithmetic and copies ran while one was open for 5% of the time, Pallas kernels for 5%

profile of v9, /device:TPU:2, one launch (start us, length us, event | category | flops | bytes accessed | tf_op | source)
XLA Modules:
  0.0 173.5 jit_solution(10314833465695949353)
XLA Ops:
  9.1 1.3 fusion.33
  10.5 2.0 %fusion.3 = bf16[128,384]{1,0:T(8,128)(2,1)} fusion(bf16[384,3,128]{2,0,1:T(8,128)(2,1)} %param.12, f32[384,384]{0,1:T(8,128)S(1)} %get-tuple-element.50, f32[384]{0:T(512)S(1)} %fusion.8, f32[384]{0:T(512)S(1)} %get-tuple-element.49), kind=kOutput, calls=%fused_computation.9 | convolution fusion | flops 38240256 | bytes 789504 | tf_op jit(solution)/shard_map/dot_general | solution.py:33
  13.3 1.2 multiply_convert_fusion.2
  14.5 1.9 %collective-permute-start.1 = (bf16[384,256]{1,0:T(8,128)(2,1)S(1)}, bf16[384,256]{1,0:T(8,128)(2,1)S(1)}, u32[]{:S(2)}, u32[]{:S(2)}) collective-permute-start(bf16[384,256]{1,0:T(8,128)(2,1)S(1)} %get-tuple-element.32.gated), channel_id=1, source_target_pairs={{0,1},{1,0},{2,3},{3,2},{4,5},{5,4},{6,7},{7,6},{8,9},{9,8},{10,11... | collective-permute-start | bytes 589832 | tf_op jit(solution)/shard_map/ppermute | solution.py:37
  16.4 1.4 collective-permute-done.1.theirs
  18.7 1.1 dynamic-slice_bitcast_fusion
  19.7 2.0 %collective-permute-start = (bf16[16,128,256]{2,1,0:T(8,128)(2,1)}, bf16[16,128,256]{2,1,0:T(8,128)(2,1)}, u32[]{:S(2)}, u32[]{:S(2)}) collective-permute-start(bf16[16,128,256]{2,1,0:T(8,128)(2,1)} %dynamic-slice_bitcast_fusion), channel_id=1, source_target_pairs={{0,1},{1,0},{2,3},{3,2},{4,5},{5,4},{6,7},{7,6},{8,9},{9,8},{10,11... | collective-permute-start | bytes 3145736 | tf_op jit(solution)/shard_map/ppermute | solution.py:37
  21.8 7.1 %all-to-all-start = ((bf16[8,16,384]{2,1,0:T(8,128)(2,1)}), bf16[8,16,384]{2,1,0:T(8,128)(2,1)S(1)}, u32[]{:S(2)}, u32[]{:S(2)}) async-start(bf16[8,16,384]{2,1,0:T(8,128)(2,1)} %bitcast.11), calls=%async_computation | async-start | bytes 196608 | tf_op jit(solution)/shard_map/all_to_all | solution.py:234
  29.0 3.2 %shard_map.139 = bf16[2048,384]{1,0:T(8,128)(2,1)S(1)} custom-call(s32[2]{0:T(128)S(1)} %pad_add_fusion.place, bf16[32,128,256]{2,1,0:T(8,128)(2,1)S(1)} %bitcast.57, bf16[16,128,256]{2,1,0:T(8,128)(2,1)} %collective-permute-done.other, bf16[384,256]{1,0:T(8,128)(2,1)S(1)} %get-tuple-element.32.gated, bf16[384,256]{1,0:T(8,128)(2,1)S(1)} %collective-permute-done.1.theirs), custom_call_target="tpu_custom_call" | custom-call | flops 805306368 | bytes 3145728 | tf_op jit(solution)/shard_map/pallas_call | solution.py:74
  32.2 1.1 copy-done.2
  33.4 4.4 %all-to-all-done = bf16[8,16,384]{2,1,0:T(8,128)(2,1)S(1)} async-done(((bf16[8,16,384]{2,1,0:T(8,128)(2,1)}), bf16[8,16,384]{2,1,0:T(8,128)(2,1)S(1)}, u32[]{:S(2)}, u32[]{:S(2)}) %all-to-all-start) | async-done | bytes 98336 | tf_op jit(solution)/shard_map/all_to_all | solution.py:234
  37.8 26.1 %all_gather.18 = bf16[512,384]{1,0:T(8,128)(2,1)S(1)} all-gather(bf16[128,384]{1,0:T(8,128)(2,1)S(1)} %bitcast.64), channel_id=1, replica_groups=mesh['zlo'=3,'y'=8,'zhi'=4,'x'=4,'core'=2] {'zhi'}, dimensions={0}, use_global_device_ids=true | all-gather | bytes 491520 | tf_op jit(solution)/shard_map/all_gather | solution.py:240
  63.9 1.3 pad_maximum_fusion
  65.3 4.9 %all-to-all-start.1 = ((bf16[4,512,384]{2,1,0:T(8,128)(2,1)}), bf16[4,512,384]{2,1,0:T(8,128)(2,1)}, u32[]{:S(2)}, u32[]{:S(2)}) async-start(bf16[4,512,384]{2,1,0:T(8,128)(2,1)} %bitcast.59), calls=%async_computation.1 | async-start | bytes 3145728 | tf_op jit(solution)/shard_map/all_to_all | solution.py:41
  70.2 19.2 %all_gather.19.refs_0_ = bf16[512,384]{1,0:T(8,128)(2,1)S(1)} all-gather(bf16[128,384]{1,0:T(8,128)(2,1)} %fusion.3), channel_id=1, replica_groups=mesh['zlo'=3,'y'=8,'zhi'=4,'x'=4,'core'=2] {'zhi'}, dimensions={0}, use_global_device_ids=true | all-gather | bytes 491520 | tf_op jit(solution)/shard_map/all_gather | solution.py:244
  89.4 1.9 %copy-done.3 = bf16[3072,512]{1,0:T(8,128)(2,1)S(1)} copy-done((bf16[3072,512]{1,0:T(8,128)(2,1)S(1)}, bf16[3072,512]{1,0:T(8,128)(2,1)}, u32[]{:S(2)}) %copy-start.3) | copy-done | bytes 3145752
  91.3 2.4 %shard_map.140 = (bf16[256,256]{1,0:T(8,128)(2,1)S(1)}, bf16[256,256]{1,0:T(8,128)(2,1)S(1)}) custom-call(bf16[2048,384]{1,0:T(8,128)(2,1)} %bitcast.14.held, bf16[3072,512]{1,0:T(8,128)(2,1)S(1)} %copy-done.3), custom_call_target="tpu_custom_call" | custom-call | flops 805306368 | bytes 4718592 | tf_op jit(solution)/shard_map/pallas_call | solution.py:102
  93.7 1.9 %collective-permute-start.2 = (bf16[256,256]{1,0:T(8,128)(2,1)S(1)}, bf16[256,256]{1,0:T(8,128)(2,1)S(1)}, u32[]{:S(2)}, u32[]{:S(2)}) collective-permute-start(bf16[256,256]{1,0:T(8,128)(2,1)S(1)} %get-tuple-element.38), channel_id=1, source_target_pairs={{0,1},{1,0},{2,3},{3,2},{4,5},{5,4},{6,7},{7,6},{8,9},{9,8},{10,11... | collective-permute-start | bytes 393224 | tf_op jit(solution)/shard_map/ppermute | solution.py:37
  95.7 1.3 collective-permute-done.2
  97.0 16.2 %all-gather = bf16[1536,256]{1,0:T(8,128)(2,1)} all-gather(bf16[512,256]{1,0:T(8,128)(2,1)S(1)} %pad_maximum_fusion.3), channel_id=2, replica_groups=mesh['zlo'=3,'y'=8,'zhi'=4,'x'=4,'core'=2] {'zlo'}, dimensions={0}, use_global_device_ids=true | all-gather | bytes 1048576 | tf_op jit(solution)/shard_map/all_gather | solution.py:249
  113.2 2.0 %reduce_sum.53 = bf16[512,256]{1,0:T(8,128)(2,1)} reduce(bf16[3,512,256]{2,1,0:T(8,128)(2,1)} %bitcast.60, bf16[]{:T(256)} %constant.32.clone.1), dimensions={0}, to_apply=%region_4.5 | reduce | flops 262144 | bytes 1048578 | tf_op jit(solution)/shard_map/reduce_sum | solution.py:249
  115.3 10.0 %all-to-all-start.2 = ((bf16[4,128,384]{2,1,0:T(8,128)(2,1)}), bf16[4,128,384]{2,1,0:T(8,128)(2,1)}, u32[]{:S(2)}, u32[]{:S(2)}) async-start(bf16[4,128,384]{2,1,0:T(8,128)(2,1)} %bitcast.63), calls=%async_computation.3 | async-start | bytes 786432 | tf_op jit(solution)/shard_map/all_to_all | solution.py:255
  125.4 2.8 %collective-permute-start.3 = (bf16[512,384]{1,0:T(8,128)(2,1)S(1)}, bf16[512,384]{1,0:T(8,128)(2,1)S(1)}, u32[]{:S(2)}, u32[]{:S(2)}) collective-permute-start(bf16[512,384]{1,0:T(8,128)(2,1)S(1)} %all_gather.19.refs_0_), channel_id=1, source_target_pairs={{0,2},{2,4},{4,6},{6,0},{1,3},{3,5},{5,7},{7,1},{8,10},{10,12},{12... | collective-permute-start | bytes 1179656 | tf_op jit(solution)/shard_map/ppermute | solution.py:37
  128.2 4.5 %collective-permute-start.4 = (bf16[512,384]{1,0:T(8,128)(2,1)S(1)}, bf16[512,384]{1,0:T(8,128)(2,1)}, u32[]{:S(2)}, u32[]{:S(2)}) collective-permute-start(bf16[512,384]{1,0:T(8,128)(2,1)S(1)} %all_gather.19.refs_0_), channel_id=1, source_target_pairs={{0,4},{2,6},{4,0},{6,2},{1,5},{3,7},{5,1},{7,3},{8,12},{10,14},{12... | collective-permute-start | bytes 1179656 | tf_op jit(solution)/shard_map/ppermute | solution.py:37
  132.7 2.5 %collective-permute-start.5 = (bf16[512,384]{1,0:T(8,128)(2,1)S(1)}, bf16[512,384]{1,0:T(8,128)(2,1)}, u32[]{:S(2)}, u32[]{:S(2)}) collective-permute-start(bf16[512,384]{1,0:T(8,128)(2,1)S(1)} %all_gather.19.refs_0_), channel_id=1, source_target_pairs={{0,6},{2,0},{4,2},{6,4},{1,7},{3,1},{5,3},{7,5},{8,14},{10,8},{12,... | collective-permute-start | bytes 1179656 | tf_op jit(solution)/shard_map/ppermute | solution.py:37
  135.3 9.4 %all-to-all-done.2 = bf16[4,128,384]{2,1,0:T(8,128)(2,1)} async-done(((bf16[4,128,384]{2,1,0:T(8,128)(2,1)}), bf16[4,128,384]{2,1,0:T(8,128)(2,1)}, u32[]{:S(2)}, u32[]{:S(2)}) %all-to-all-start.2) | async-done | bytes 393248 | tf_op jit(solution)/shard_map/all_to_all | solution.py:255
  145.7 1.4 multiply_reduce_fusion
  149.5 2.5 %shard_map.141 = (f32[384,256]{1,0:T(8,128)S(1)}, bf16[384,256]{1,0:T(8,128)(2,1)S(1)}) custom-call(s32[2]{0:T(128)S(1)} %pad_add_fusion.place, bf16[32,128,256]{2,1,0:T(8,128)(2,1)S(1)} %bitcast.58, bf16[16,128,256]{2,1,0:T(8,128)(2,1)} %collective-permute-done.other, bf16[512,384]{1,0:T(8,128)(2,1)S(1)} %all_gather.19.refs_0_, ...), custom_call_target="tpu_custom_call" | custom-call | flops 805306368 | bytes 3670016 | tf_op jit(solution)/shard_map/pallas_call | solution.py:131
  152.0 1.9 %collective-permute-start.6 = (bf16[384,256]{1,0:T(8,128)(2,1)S(1)}, bf16[384,256]{1,0:T(8,128)(2,1)S(1)}, u32[]{:S(2)}, u32[]{:S(2)}) collective-permute-start(bf16[384,256]{1,0:T(8,128)(2,1)S(1)} %get-tuple-element.47), channel_id=1, source_target_pairs={{0,1},{1,0},{2,3},{3,2},{4,5},{5,4},{6,7},{7,6},{8,9},{9,8},{10,11... | collective-permute-start | bytes 589832 | tf_op jit(solution)/shard_map/ppermute | solution.py:37
  153.9 1.4 collective-permute-done.6
  156.1 6.1 %all-gather.6.cloned.1.call-done = bf16[4096,256]{1,0:T(8,128)(2,1)} async-done(((bf16[512,256]{1,0:T(8,128)(2,1)}), bf16[4096,256]{1,0:T(8,128)(2,1)}) %all-gather.6.cloned.1.call-update) | async-done | bytes 2097168 | tf_op jit(solution)/shard_map/all_gather | solution.py:252
  162.2 3.8 %shard_map.142 = bf16[32,128,256]{2,1,0:T(8,128)(2,1)} custom-call(s32[2]{0:T(128)} %copy-done.4, bf16[8,512,256]{2,1,0:T(8,128)(2,1)} %bitcast.61), custom_call_target="tpu_custom_call" | custom-call | bytes 4194304 | tf_op jit(solution)/shard_map/pallas_call | solution.py:166
  (62 shorter events, 7.2 us)
Async XLA Ops:
  8.0 4.5 %copy-start = (bf16[1000,256]{1,0:T(8,128)(2,1)S(1)}, bf16[1000,256]{1,0:T(8,128)(2,1)}, u32[]{:S(2)}) copy-start(bf16[1000,256]{1,0:T(8,128)(2,1)} %param.20) | copy-start | bytes 1536004
  8.0 4.5 %copy-start.10 = (s32[8]{0:T(128)S(1)}, s32[8]{0:T(128)}, u32[]{:S(2)}) copy-start(s32[8]{0:T(128)} %param.19) | copy-start | bytes 100
  8.0 81.4 %all-gather.4.cloned.1.call-start = ((), (), s32[]{:S(2)}) async-start(), calls=%async_computation.4 | async-start | bytes 3538944 | tf_op jit(solution)/shard_map/all_gather | solution.py:232
  9.0 3.7 %copy-start.11 = (bf16[16,256]{1,0:T(8,128)(2,1)S(1)}, bf16[16,256]{1,0:T(8,128)(2,1)}, u32[]{:S(2)}) copy-start(bf16[16,256]{1,0:T(8,128)(2,1)} %param.21) | copy-start | bytes 24580
  9.0 3.7 %copy-start.14 = (s32[8]{0:T(128)S(1)}, s32[8]{0:T(128)}, u32[]{:S(2)}) copy-start(s32[8]{0:T(128)} %param.18) | copy-start | bytes 100
  9.0 3.9 %copy-start.12 = (bf16[8,256]{1,0:T(8,128)(2,1)S(1)}, bf16[8,256]{1,0:T(8,128)(2,1)}, u32[]{:S(2)}) copy-start(bf16[8,256]{1,0:T(8,128)(2,1)} %param.22) | copy-start | bytes 12292
  9.0 3.9 %copy-start.15 = (s32[8]{0:T(128)S(1)}, s32[8]{0:T(128)}, u32[]{:S(2)}) copy-start(s32[8]{0:T(128)} %param.17) | copy-start | bytes 100
  10.3 4.2 %copy-start.5 = (f32[384,384]{0,1:T(8,128)}, f32[384,384]{0,1:T(8,128)S(1)}, u32[]{:S(2)}) copy-start(f32[384,384]{0,1:T(8,128)S(1)} %get-tuple-element.50) | copy-start | bytes 1769476
  10.3 2.8 %copy-start.13 = (bf16[8,256]{1,0:T(8,128)(2,1)S(1)}, bf16[8,256]{1,0:T(8,128)(2,1)}, u32[]{:S(2)}) copy-start(bf16[8,256]{1,0:T(8,128)(2,1)} %param.23) | copy-start | bytes 12292
  10.3 2.8 %copy-start.16 = (s32[8]{0:T(128)S(1)}, s32[8]{0:T(128)}, u32[]{:S(2)}) copy-start(s32[8]{0:T(128)} %param.16) | copy-start | bytes 100
  10.3 2.9 %copy-start.8 = (bf16[384,256]{1,0:T(8,128)(2,1)S(1)}, bf16[384,256]{1,0:T(8,128)(2,1)}, u32[]{:S(2)}) copy-start(bf16[384,256]{1,0:T(8,128)(2,1)} %param.14) | copy-start | bytes 589828
  10.5 8.2 %copy-start.1 = (bf16[4096,256]{1,0:T(8,128)(2,1)S(1)}, bf16[4096,256]{1,0:T(8,128)(2,1)}, u32[]{:S(2)}) copy-start(bf16[4096,256]{1,0:T(8,128)(2,1)} %param.13) | copy-start | bytes 6291460
  14.5 3.3 %collective-permute-start.1 = (bf16[384,256]{1,0:T(8,128)(2,1)S(1)}, bf16[384,256]{1,0:T(8,128)(2,1)S(1)}, u32[]{:S(2)}, u32[]{:S(2)}) collective-permute-start(bf16[384,256]{1,0:T(8,128)(2,1)S(1)} %get-tuple-element.32.gated), channel_id=1, source_target_pairs={{0,1},{1,0},{2,3},{3,2},{4,5},{5,4},{6,7},{7,6},{8,9},{9,8},{10,11... | collective-permute-start | bytes 589832 | tf_op jit(solution)/shard_map/ppermute | solution.py:37
  19.7 9.3 %collective-permute-start = (bf16[16,128,256]{2,1,0:T(8,128)(2,1)}, bf16[16,128,256]{2,1,0:T(8,128)(2,1)}, u32[]{:S(2)}, u32[]{:S(2)}) collective-permute-start(bf16[16,128,256]{2,1,0:T(8,128)(2,1)} %dynamic-slice_bitcast_fusion), channel_id=1, source_target_pairs={{0,1},{1,0},{2,3},{3,2},{4,5},{5,4},{6,7},{7,6},{8,9},{9,8},{10,11... | collective-permute-start | bytes 3145736 | tf_op jit(solution)/shard_map/ppermute | solution.py:37
  21.8 16.0 %all-to-all-start = ((bf16[8,16,384]{2,1,0:T(8,128)(2,1)}), bf16[8,16,384]{2,1,0:T(8,128)(2,1)S(1)}, u32[]{:S(2)}, u32[]{:S(2)}) async-start(bf16[8,16,384]{2,1,0:T(8,128)(2,1)} %bitcast.11), calls=%async_computation | async-start | bytes 196608 | tf_op jit(solution)/shard_map/all_to_all | solution.py:234
  28.9 86.4 %reduce-scatter.2.cloned.1.call-start = ((), (), s32[]{:S(2)}) async-start(), calls=%async_computation.5 | async-start | bytes 1966080 | tf_op jit(solution)/shard_map/reduce_scatter | solution.py:238
  29.0 120.5 %copy-start.4 = (s32[2]{0:T(128)}, s32[2]{0:T(128)S(1)}, u32[]{:S(2)}) copy-start(s32[2]{0:T(128)S(1)} %pad_add_fusion.place) | copy-start | bytes 28
  32.2 1.1 copy-start.2
  65.3 24.1 %all-to-all-start.1 = ((bf16[4,512,384]{2,1,0:T(8,128)(2,1)}), bf16[4,512,384]{2,1,0:T(8,128)(2,1)}, u32[]{:S(2)}, u32[]{:S(2)}) async-start(bf16[4,512,384]{2,1,0:T(8,128)(2,1)} %bitcast.59), calls=%async_computation.1 | async-start | bytes 3145728 | tf_op jit(solution)/shard_map/all_to_all | solution.py:41
  70.2 92.1 %all-gather.6.cloned.1.call-start = ((), (), s32[]{:S(2)}) async-start(), calls=%async_computation.6 | async-start | bytes 2359296 | tf_op jit(solution)/shard_map/all_gather | solution.py:252
  89.4 1.9 %copy-start.3 = (bf16[3072,512]{1,0:T(8,128)(2,1)S(1)}, bf16[3072,512]{1,0:T(8,128)(2,1)}, u32[]{:S(2)}) copy-start(bf16[3072,512]{1,0:T(8,128)(2,1)} %all-gather.4.cloned.1.call-done.gated) | copy-start | bytes 9437188
  93.7 3.2 %collective-permute-start.2 = (bf16[256,256]{1,0:T(8,128)(2,1)S(1)}, bf16[256,256]{1,0:T(8,128)(2,1)S(1)}, u32[]{:S(2)}, u32[]{:S(2)}) collective-permute-start(bf16[256,256]{1,0:T(8,128)(2,1)S(1)} %get-tuple-element.38), channel_id=1, source_target_pairs={{0,1},{1,0},{2,3},{3,2},{4,5},{5,4},{6,7},{7,6},{8,9},{9,8},{10,11... | collective-permute-start | bytes 393224 | tf_op jit(solution)/shard_map/ppermute | solution.py:37
  115.3 29.3 %all-to-all-start.2 = ((bf16[4,128,384]{2,1,0:T(8,128)(2,1)}), bf16[4,128,384]{2,1,0:T(8,128)(2,1)}, u32[]{:S(2)}, u32[]{:S(2)}) async-start(bf16[4,128,384]{2,1,0:T(8,128)(2,1)} %bitcast.63), calls=%async_computation.3 | async-start | bytes 786432 | tf_op jit(solution)/shard_map/all_to_all | solution.py:255
  125.4 23.5 %collective-permute-start.3 = (bf16[512,384]{1,0:T(8,128)(2,1)S(1)}, bf16[512,384]{1,0:T(8,128)(2,1)S(1)}, u32[]{:S(2)}, u32[]{:S(2)}) collective-permute-start(bf16[512,384]{1,0:T(8,128)(2,1)S(1)} %all_gather.19.refs_0_), channel_id=1, source_target_pairs={{0,2},{2,4},{4,6},{6,0},{1,3},{3,5},{5,7},{7,1},{8,10},{10,12},{12... | collective-permute-start | bytes 1179656 | tf_op jit(solution)/shard_map/ppermute | solution.py:37
  128.2 20.7 %collective-permute-start.4 = (bf16[512,384]{1,0:T(8,128)(2,1)S(1)}, bf16[512,384]{1,0:T(8,128)(2,1)}, u32[]{:S(2)}, u32[]{:S(2)}) collective-permute-start(bf16[512,384]{1,0:T(8,128)(2,1)S(1)} %all_gather.19.refs_0_), channel_id=1, source_target_pairs={{0,4},{2,6},{4,0},{6,2},{1,5},{3,7},{5,1},{7,3},{8,12},{10,14},{12... | collective-permute-start | bytes 1179656 | tf_op jit(solution)/shard_map/ppermute | solution.py:37
  132.7 16.8 %collective-permute-start.5 = (bf16[512,384]{1,0:T(8,128)(2,1)S(1)}, bf16[512,384]{1,0:T(8,128)(2,1)}, u32[]{:S(2)}, u32[]{:S(2)}) collective-permute-start(bf16[512,384]{1,0:T(8,128)(2,1)S(1)} %all_gather.19.refs_0_), channel_id=1, source_target_pairs={{0,6},{2,0},{4,2},{6,4},{1,7},{3,1},{5,3},{7,5},{8,14},{10,8},{12,... | collective-permute-start | bytes 1179656 | tf_op jit(solution)/shard_map/ppermute | solution.py:37
  145.7 1.5 copy-start.6
  145.7 1.6 copy-start.9
  148.9 6.5 %copy-start.7 = (f32[384,256]{1,0:T(8,128)S(1)}, f32[384,256]{1,0:T(8,128)}, u32[]{:S(2)}) copy-start(f32[384,256]{1,0:T(8,128)} %get-tuple-element.52) | copy-start | bytes 1179652
  152.0 3.3 %collective-permute-start.6 = (bf16[384,256]{1,0:T(8,128)(2,1)S(1)}, bf16[384,256]{1,0:T(8,128)(2,1)S(1)}, u32[]{:S(2)}, u32[]{:S(2)}) collective-permute-start(bf16[384,256]{1,0:T(8,128)(2,1)S(1)} %get-tuple-element.47), channel_id=1, source_target_pairs={{0,1},{1,0},{2,3},{3,2},{4,5},{5,4},{6,7},{7,6},{8,9},{9,8},{10,11... | collective-permute-start | bytes 589832 | tf_op jit(solution)/shard_map/ppermute | solution.py:37
Sparse Core Ops, SparseCore 0:
  18.8 56.8 all-gather.3
  115.4 46.7 all-gather.5
Sparse Core Ops, SparseCore 1:
  37.9 36.6 reduce-scatter.1

commit v10 on v9

--- a/solution.py
+++ b/solution.py
@@ -147,14 +147,14 @@
     loads = [pltpu.make_async_copy(src.at[y], taken.at[y], in_sems.at[y]) for y in range(NY)]
     for load in loads:
         load.start()
-    for load in loads:
-        load.wait()
+    for y in range(NY):
+        loads[y].wait()
+        for i in range(NX * NCORE * NZHI):
+            given[i, y * SLAB : (y + 1) * SLAB, :] = taken[y, i * SLAB : (i + 1) * SLAB, :]
     stores = []
     for i in range(NX * NCORE * NZHI):
         c, x, z = i // (NX * NZHI), i // NZHI % NX, i % NZHI
         head = (z * NX + x) * NCORE + (core if c == 0 else 1 - core)
-        for y in range(NY):
-            given[i, y * SLAB : (y + 1) * SLAB, :] = taken[y, i * SLAB : (i + 1) * SLAB, :]
         stores.append(pltpu.make_async_copy(given.at[i], dst.at[head], out_sems.at[i]))
         stores[-1].start()
     for store in stores:
@@ -246,7 +246,10 @@
 
     total, swap = weight_part(own, gated_y)
     total = jnp.concatenate([total, shift(swap, "core", NCORE, 1)])
-    total = lax.all_gather(total, "zlo").astype(F32).sum(0).astype(BF)
+    rows = total.shape[0]
+    total = lax.all_gather(total, "zlo", axis=0, tiled=True)
+    terms = [total[i * rows : (i + 1) * rows].astype(F32) for i in range(NZLO)]
+    total = (terms[0] + terms[1] + terms[2]).astype(BF)
     whole = after(whole, total)
     summed = after(summed, total)
     total = lax.all_gather(total, "y", axis=0, tiled=True)

time: 174 us -> 173 us (level)
    reduce_sum x1 -> x0, other arithmetic: 2.03 us -> none  [on_device(): total = lax.all_gather(total, 'zlo').astype(F32).sum(0).astype(BF)]
where the time goes in v10:
time: 173 us; the launch traced here: 172 us
  blocking collectives  61.5 us (36%)
  starting transfers between devices  39.8 us (23%)
  waiting for transfers between devices  24.8 us (14%)
  between operations  15.8 us (9%)
  Pallas kernels  11.9 us (7%)
  matrix products  7.4 us (4%)
  other arithmetic  6.79 us (4%)
  local copies, waits for them, and re-layouts  4.18 us (2%)
    all_gather x1, blocking collectives, on_device(): own = lax.all_gather(attended, 'zhi', axis=0, tiled=True)  26.1 us
    all_gather x1, blocking collectives, on_device(): whole = lax.all_gather(natural, 'zhi', axis=0, tiled=True)  19.3 us
    ppermute x7, starting transfers between devices, shift(): lax.ppermute(value, axis, [(i, (i + step) % size) for i in range(size)])  17.7 us
    all_gather x1, blocking collectives, on_device(): total = lax.all_gather(total, 'zlo', axis=0, tiled=True)  16.1 us
    all_to_all x1, starting transfers between devices, on_device(): lax.all_to_all(summed, 'zhi', split_axis=0, concat_axis=0, tiled=True)  10.1 us
    all_to_all x1, waiting for transfers between devices, on_device(): lax.all_to_all(summed, 'zhi', split_axis=0, concat_axis=0, tiled=True)  9.37 us
    all_to_all x1, starting transfers between devices, on_device(): lax.all_to_all(attended, 'y', split_axis=0, concat_axis=0, tiled=True)  7.13 us
    all_gather x1, waiting for transfers between devices, on_device(): total = lax.all_gather(total, 'y', axis=0, tiled=True)  6.11 us
  transfers between devices with their start and end apart: 13, of which 7 were waited for; matrix products, arithmetic and copies ran while one was open for 5% of the time, Pallas kernels for 5%

profile of v10, /device:TPU:2, one launch (start us, length us, event | category | flops | bytes accessed | tf_op | source)
XLA Modules:
  0.0 172.1 jit_solution(12253363447185904794)
XLA Ops:
  9.1 1.3 fusion.33
  10.5 2.0 %fusion.3 = bf16[128,384]{1,0:T(8,128)(2,1)} fusion(bf16[384,3,128]{2,0,1:T(8,128)(2,1)} %param.12, f32[384,384]{0,1:T(8,128)S(1)} %get-tuple-element.50, f32[384]{0:T(512)S(1)} %fusion.8, f32[384]{0:T(512)S(1)} %get-tuple-element.49), kind=kOutput, calls=%fused_computation.9 | convolution fusion | flops 38240256 | bytes 789504 | tf_op jit(solution)/shard_map/dot_general | solution.py:33
  13.3 1.2 multiply_convert_fusion.2
  14.4 1.9 %collective-permute-start.1 = (bf16[384,256]{1,0:T(8,128)(2,1)S(1)}, bf16[384,256]{1,0:T(8,128)(2,1)S(1)}, u32[]{:S(2)}, u32[]{:S(2)}) collective-permute-start(bf16[384,256]{1,0:T(8,128)(2,1)S(1)} %get-tuple-element.32.gated), channel_id=1, source_target_pairs={{0,1},{1,0},{2,3},{3,2},{4,5},{5,4},{6,7},{7,6},{8,9},{9,8},{10,11... | collective-permute-start | bytes 589832 | tf_op jit(solution)/shard_map/ppermute | solution.py:37
  16.4 1.4 collective-permute-done.1.theirs
  18.6 1.1 dynamic-slice_bitcast_fusion
  19.7 2.0 %collective-permute-start = (bf16[16,128,256]{2,1,0:T(8,128)(2,1)}, bf16[16,128,256]{2,1,0:T(8,128)(2,1)}, u32[]{:S(2)}, u32[]{:S(2)}) collective-permute-start(bf16[16,128,256]{2,1,0:T(8,128)(2,1)} %dynamic-slice_bitcast_fusion), channel_id=1, source_target_pairs={{0,1},{1,0},{2,3},{3,2},{4,5},{5,4},{6,7},{7,6},{8,9},{9,8},{10,11... | collective-permute-start | bytes 3145736 | tf_op jit(solution)/shard_map/ppermute | solution.py:37
  21.7 7.1 %all-to-all-start = ((bf16[8,16,384]{2,1,0:T(8,128)(2,1)}), bf16[8,16,384]{2,1,0:T(8,128)(2,1)S(1)}, u32[]{:S(2)}, u32[]{:S(2)}) async-start(bf16[8,16,384]{2,1,0:T(8,128)(2,1)} %bitcast.11), calls=%async_computation | async-start | bytes 196608 | tf_op jit(solution)/shard_map/all_to_all | solution.py:234
  29.0 3.2 %shard_map.139 = bf16[2048,384]{1,0:T(8,128)(2,1)S(1)} custom-call(s32[2]{0:T(128)S(1)} %pad_add_fusion.place, bf16[32,128,256]{2,1,0:T(8,128)(2,1)S(1)} %bitcast.56, bf16[16,128,256]{2,1,0:T(8,128)(2,1)} %collective-permute-done.other, bf16[384,256]{1,0:T(8,128)(2,1)S(1)} %get-tuple-element.32.gated, bf16[384,256]{1,0:T(8,128)(2,1)S(1)} %collective-permute-done.1.theirs), custom_call_target="tpu_custom_call" | custom-call | flops 805306368 | bytes 3145728 | tf_op jit(solution)/shard_map/pallas_call | solution.py:74
  32.2 1.1 copy-done.2
  33.3 4.4 %all-to-all-done = bf16[8,16,384]{2,1,0:T(8,128)(2,1)S(1)} async-done(((bf16[8,16,384]{2,1,0:T(8,128)(2,1)}), bf16[8,16,384]{2,1,0:T(8,128)(2,1)S(1)}, u32[]{:S(2)}, u32[]{:S(2)}) %all-to-all-start) | async-done | bytes 98336 | tf_op jit(solution)/shard_map/all_to_all | solution.py:234
  37.8 26.1 %all_gather.15 = bf16[512,384]{1,0:T(8,128)(2,1)S(1)} all-gather(bf16[128,384]{1,0:T(8,128)(2,1)S(1)} %bitcast.62), channel_id=1, replica_groups=mesh['zlo'=3,'y'=8,'zhi'=4,'x'=4,'core'=2] {'zhi'}, dimensions={0}, use_global_device_ids=true | all-gather | bytes 491520 | tf_op jit(solution)/shard_map/all_gather | solution.py:240
  63.9 1.3 pad_maximum_fusion
  65.2 4.9 %all-to-all-start.1 = ((bf16[4,512,384]{2,1,0:T(8,128)(2,1)}), bf16[4,512,384]{2,1,0:T(8,128)(2,1)}, u32[]{:S(2)}, u32[]{:S(2)}) async-start(bf16[4,512,384]{2,1,0:T(8,128)(2,1)} %bitcast.58), calls=%async_computation.1 | async-start | bytes 3145728 | tf_op jit(solution)/shard_map/all_to_all | solution.py:41
  70.1 19.3 %all_gather.16.refs_0_ = bf16[512,384]{1,0:T(8,128)(2,1)S(1)} all-gather(bf16[128,384]{1,0:T(8,128)(2,1)} %fusion.3), channel_id=1, replica_groups=mesh['zlo'=3,'y'=8,'zhi'=4,'x'=4,'core'=2] {'zhi'}, dimensions={0}, use_global_device_ids=true | all-gather | bytes 491520 | tf_op jit(solution)/shard_map/all_gather | solution.py:244
  89.3 1.9 %copy-done.3 = bf16[3072,512]{1,0:T(8,128)(2,1)S(1)} copy-done((bf16[3072,512]{1,0:T(8,128)(2,1)S(1)}, bf16[3072,512]{1,0:T(8,128)(2,1)}, u32[]{:S(2)}) %copy-start.3) | copy-done | bytes 3145752
  91.2 2.4 %shard_map.140 = (bf16[256,256]{1,0:T(8,128)(2,1)S(1)}, bf16[256,256]{1,0:T(8,128)(2,1)S(1)}) custom-call(bf16[2048,384]{1,0:T(8,128)(2,1)} %bitcast.14.held, bf16[3072,512]{1,0:T(8,128)(2,1)S(1)} %copy-done.3), custom_call_target="tpu_custom_call" | custom-call | flops 805306368 | bytes 4718592 | tf_op jit(solution)/shard_map/pallas_call | solution.py:102
  93.6 1.9 %collective-permute-start.2 = (bf16[256,256]{1,0:T(8,128)(2,1)S(1)}, bf16[256,256]{1,0:T(8,128)(2,1)S(1)}, u32[]{:S(2)}, u32[]{:S(2)}) collective-permute-start(bf16[256,256]{1,0:T(8,128)(2,1)S(1)} %get-tuple-element.38), channel_id=1, source_target_pairs={{0,1},{1,0},{2,3},{3,2},{4,5},{5,4},{6,7},{7,6},{8,9},{9,8},{10,11... | collective-permute-start | bytes 393224 | tf_op jit(solution)/shard_map/ppermute | solution.py:37
  95.6 1.3 collective-permute-done.2
  96.9 16.1 %all_gather.18 = bf16[1536,256]{1,0:T(8,128)(2,1)S(1)} all-gather(bf16[512,256]{1,0:T(8,128)(2,1)S(1)} %pad_maximum_fusion.3), channel_id=1, replica_groups=mesh['zlo'=3,'y'=8,'zhi'=4,'x'=4,'core'=2] {'zlo'}, dimensions={0}, use_global_device_ids=true | all-gather | bytes 1048576 | tf_op jit(solution)/shard_map/all_gather | solution.py:250
  113.9 10.1 %all-to-all-start.2 = ((bf16[4,128,384]{2,1,0:T(8,128)(2,1)}), bf16[4,128,384]{2,1,0:T(8,128)(2,1)}, u32[]{:S(2)}, u32[]{:S(2)}) async-start(bf16[4,128,384]{2,1,0:T(8,128)(2,1)} %bitcast.61), calls=%async_computation.3 | async-start | bytes 786432 | tf_op jit(solution)/shard_map/all_to_all | solution.py:258
  124.0 2.8 %collective-permute-start.3 = (bf16[512,384]{1,0:T(8,128)(2,1)S(1)}, bf16[512,384]{1,0:T(8,128)(2,1)S(1)}, u32[]{:S(2)}, u32[]{:S(2)}) collective-permute-start(bf16[512,384]{1,0:T(8,128)(2,1)S(1)} %all_gather.16.refs_0_), channel_id=1, source_target_pairs={{0,2},{2,4},{4,6},{6,0},{1,3},{3,5},{5,7},{7,1},{8,10},{10,12},{12... | collective-permute-start | bytes 1179656 | tf_op jit(solution)/shard_map/ppermute | solution.py:37
  126.8 4.5 %collective-permute-start.4 = (bf16[512,384]{1,0:T(8,128)(2,1)S(1)}, bf16[512,384]{1,0:T(8,128)(2,1)}, u32[]{:S(2)}, u32[]{:S(2)}) collective-permute-start(bf16[512,384]{1,0:T(8,128)(2,1)S(1)} %all_gather.16.refs_0_), channel_id=1, source_target_pairs={{0,4},{2,6},{4,0},{6,2},{1,5},{3,7},{5,1},{7,3},{8,12},{10,14},{12... | collective-permute-start | bytes 1179656 | tf_op jit(solution)/shard_map/ppermute | solution.py:37
  131.3 2.5 %collective-permute-start.5 = (bf16[512,384]{1,0:T(8,128)(2,1)S(1)}, bf16[512,384]{1,0:T(8,128)(2,1)}, u32[]{:S(2)}, u32[]{:S(2)}) collective-permute-start(bf16[512,384]{1,0:T(8,128)(2,1)S(1)} %all_gather.16.refs_0_), channel_id=1, source_target_pairs={{0,6},{2,0},{4,2},{6,4},{1,7},{3,1},{5,3},{7,5},{8,14},{10,8},{12,... | collective-permute-start | bytes 1179656 | tf_op jit(solution)/shard_map/ppermute | solution.py:37
  133.9 9.4 %all-to-all-done.2 = bf16[4,128,384]{2,1,0:T(8,128)(2,1)} async-done(((bf16[4,128,384]{2,1,0:T(8,128)(2,1)}), bf16[4,128,384]{2,1,0:T(8,128)(2,1)}, u32[]{:S(2)}, u32[]{:S(2)}) %all-to-all-start.2) | async-done | bytes 393248 | tf_op jit(solution)/shard_map/all_to_all | solution.py:258
  143.2 1.1 reduce_sum.41
  144.3 1.4 multiply_reduce_fusion
  148.1 2.5 %shard_map.141 = (f32[384,256]{1,0:T(8,128)S(1)}, bf16[384,256]{1,0:T(8,128)(2,1)S(1)}) custom-call(s32[2]{0:T(128)S(1)} %pad_add_fusion.place, bf16[32,128,256]{2,1,0:T(8,128)(2,1)S(1)} %bitcast.57, bf16[16,128,256]{2,1,0:T(8,128)(2,1)} %collective-permute-done.other, bf16[512,384]{1,0:T(8,128)(2,1)S(1)} %all_gather.16.refs_0_, ...), custom_call_target="tpu_custom_call" | custom-call | flops 805306368 | bytes 3670016 | tf_op jit(solution)/shard_map/pallas_call | solution.py:131
  150.6 1.9 %collective-permute-start.6 = (bf16[384,256]{1,0:T(8,128)(2,1)S(1)}, bf16[384,256]{1,0:T(8,128)(2,1)S(1)}, u32[]{:S(2)}, u32[]{:S(2)}) collective-permute-start(bf16[384,256]{1,0:T(8,128)(2,1)S(1)} %get-tuple-element.47), channel_id=1, source_target_pairs={{0,1},{1,0},{2,3},{3,2},{4,5},{5,4},{6,7},{7,6},{8,9},{9,8},{10,11... | collective-permute-start | bytes 589832 | tf_op jit(solution)/shard_map/ppermute | solution.py:37
  152.5 1.4 collective-permute-done.6
  154.7 6.1 %all-gather.5.cloned.1.call-done = bf16[4096,256]{1,0:T(8,128)(2,1)} async-done(((bf16[512,256]{1,0:T(8,128)(2,1)}), bf16[4096,256]{1,0:T(8,128)(2,1)}) %all-gather.5.cloned.1.call-update) | async-done | bytes 2097168 | tf_op jit(solution)/shard_map/all_gather | solution.py:255
  160.8 3.8 %shard_map.142 = bf16[32,128,256]{2,1,0:T(8,128)(2,1)} custom-call(s32[2]{0:T(128)} %copy-done.4, bf16[8,512,256]{2,1,0:T(8,128)(2,1)} %bitcast.59), custom_call_target="tpu_custom_call" | custom-call | bytes 4194304 | tf_op jit(solution)/shard_map/pallas_call | solution.py:166
  (62 shorter events, 6.9 us)
Async XLA Ops:
  8.0 4.5 %copy-start = (bf16[1000,256]{1,0:T(8,128)(2,1)S(1)}, bf16[1000,256]{1,0:T(8,128)(2,1)}, u32[]{:S(2)}) copy-start(bf16[1000,256]{1,0:T(8,128)(2,1)} %param.20) | copy-start | bytes 1536004
  8.0 4.5 %copy-start.10 = (s32[8]{0:T(128)S(1)}, s32[8]{0:T(128)}, u32[]{:S(2)}) copy-start(s32[8]{0:T(128)} %param.19) | copy-start | bytes 100
  8.0 81.3 %all-gather.3.cloned.1.call-start = ((), (), s32[]{:S(2)}) async-start(), calls=%async_computation.4 | async-start | bytes 3538944 | tf_op jit(solution)/shard_map/all_gather | solution.py:232
  9.0 3.7 %copy-start.11 = (bf16[16,256]{1,0:T(8,128)(2,1)S(1)}, bf16[16,256]{1,0:T(8,128)(2,1)}, u32[]{:S(2)}) copy-start(bf16[16,256]{1,0:T(8,128)(2,1)} %param.21) | copy-start | bytes 24580
  9.0 3.7 %copy-start.14 = (s32[8]{0:T(128)S(1)}, s32[8]{0:T(128)}, u32[]{:S(2)}) copy-start(s32[8]{0:T(128)} %param.18) | copy-start | bytes 100
  9.0 3.9 %copy-start.12 = (bf16[8,256]{1,0:T(8,128)(2,1)S(1)}, bf16[8,256]{1,0:T(8,128)(2,1)}, u32[]{:S(2)}) copy-start(bf16[8,256]{1,0:T(8,128)(2,1)} %param.22) | copy-start | bytes 12292
  9.0 3.9 %copy-start.15 = (s32[8]{0:T(128)S(1)}, s32[8]{0:T(128)}, u32[]{:S(2)}) copy-start(s32[8]{0:T(128)} %param.17) | copy-start | bytes 100
  10.3 4.1 %copy-start.5 = (f32[384,384]{0,1:T(8,128)}, f32[384,384]{0,1:T(8,128)S(1)}, u32[]{:S(2)}) copy-start(f32[384,384]{0,1:T(8,128)S(1)} %get-tuple-element.50) | copy-start | bytes 1769476
  10.3 2.8 %copy-start.13 = (bf16[8,256]{1,0:T(8,128)(2,1)S(1)}, bf16[8,256]{1,0:T(8,128)(2,1)}, u32[]{:S(2)}) copy-start(bf16[8,256]{1,0:T(8,128)(2,1)} %param.23) | copy-start | bytes 12292
  10.3 2.8 %copy-start.16 = (s32[8]{0:T(128)S(1)}, s32[8]{0:T(128)}, u32[]{:S(2)}) copy-start(s32[8]{0:T(128)} %param.16) | copy-start | bytes 100
  10.3 2.9 %copy-start.8 = (bf16[384,256]{1,0:T(8,128)(2,1)S(1)}, bf16[384,256]{1,0:T(8,128)(2,1)}, u32[]{:S(2)}) copy-start(bf16[384,256]{1,0:T(8,128)(2,1)} %param.14) | copy-start | bytes 589828
  10.5 8.1 %copy-start.1 = (bf16[4096,256]{1,0:T(8,128)(2,1)S(1)}, bf16[4096,256]{1,0:T(8,128)(2,1)}, u32[]{:S(2)}) copy-start(bf16[4096,256]{1,0:T(8,128)(2,1)} %param.13) | copy-start | bytes 6291460
  14.4 3.3 %collective-permute-start.1 = (bf16[384,256]{1,0:T(8,128)(2,1)S(1)}, bf16[384,256]{1,0:T(8,128)(2,1)S(1)}, u32[]{:S(2)}, u32[]{:S(2)}) collective-permute-start(bf16[384,256]{1,0:T(8,128)(2,1)S(1)} %get-tuple-element.32.gated), channel_id=1, source_target_pairs={{0,1},{1,0},{2,3},{3,2},{4,5},{5,4},{6,7},{7,6},{8,9},{9,8},{10,11... | collective-permute-start | bytes 589832 | tf_op jit(solution)/shard_map/ppermute | solution.py:37
  19.7 9.3 %collective-permute-start = (bf16[16,128,256]{2,1,0:T(8,128)(2,1)}, bf16[16,128,256]{2,1,0:T(8,128)(2,1)}, u32[]{:S(2)}, u32[]{:S(2)}) collective-permute-start(bf16[16,128,256]{2,1,0:T(8,128)(2,1)} %dynamic-slice_bitcast_fusion), channel_id=1, source_target_pairs={{0,1},{1,0},{2,3},{3,2},{4,5},{5,4},{6,7},{7,6},{8,9},{9,8},{10,11... | collective-permute-start | bytes 3145736 | tf_op jit(solution)/shard_map/ppermute | solution.py:37
  21.7 16.0 %all-to-all-start = ((bf16[8,16,384]{2,1,0:T(8,128)(2,1)}), bf16[8,16,384]{2,1,0:T(8,128)(2,1)S(1)}, u32[]{:S(2)}, u32[]{:S(2)}) async-start(bf16[8,16,384]{2,1,0:T(8,128)(2,1)} %bitcast.11), calls=%async_computation | async-start | bytes 196608 | tf_op jit(solution)/shard_map/all_to_all | solution.py:234
  28.9 85.0 %reduce-scatter.2.cloned.1.call-start = ((), (), s32[]{:S(2)}) async-start(), calls=%async_computation.5 | async-start | bytes 1966080 | tf_op jit(solution)/shard_map/reduce_scatter | solution.py:238
  29.0 119.2 %copy-start.4 = (s32[2]{0:T(128)}, s32[2]{0:T(128)S(1)}, u32[]{:S(2)}) copy-start(s32[2]{0:T(128)S(1)} %pad_add_fusion.place) | copy-start | bytes 28
  32.2 1.1 copy-start.2
  65.2 24.1 %all-to-all-start.1 = ((bf16[4,512,384]{2,1,0:T(8,128)(2,1)}), bf16[4,512,384]{2,1,0:T(8,128)(2,1)}, u32[]{:S(2)}, u32[]{:S(2)}) async-start(bf16[4,512,384]{2,1,0:T(8,128)(2,1)} %bitcast.58), calls=%async_computation.1 | async-start | bytes 3145728 | tf_op jit(solution)/shard_map/all_to_all | solution.py:41
  70.0 90.8 %all-gather.5.cloned.1.call-start = ((), (), s32[]{:S(2)}) async-start(), calls=%async_computation.6 | async-start | bytes 2359296 | tf_op jit(solution)/shard_map/all_gather | solution.py:255
  89.3 1.9 %copy-start.3 = (bf16[3072,512]{1,0:T(8,128)(2,1)S(1)}, bf16[3072,512]{1,0:T(8,128)(2,1)}, u32[]{:S(2)}) copy-start(bf16[3072,512]{1,0:T(8,128)(2,1)} %all-gather.3.cloned.1.call-done.gated) | copy-start | bytes 9437188
  93.6 3.2 %collective-permute-start.2 = (bf16[256,256]{1,0:T(8,128)(2,1)S(1)}, bf16[256,256]{1,0:T(8,128)(2,1)S(1)}, u32[]{:S(2)}, u32[]{:S(2)}) collective-permute-start(bf16[256,256]{1,0:T(8,128)(2,1)S(1)} %get-tuple-element.38), channel_id=1, source_target_pairs={{0,1},{1,0},{2,3},{3,2},{4,5},{5,4},{6,7},{7,6},{8,9},{9,8},{10,11... | collective-permute-start | bytes 393224 | tf_op jit(solution)/shard_map/ppermute | solution.py:37
  113.9 29.3 %all-to-all-start.2 = ((bf16[4,128,384]{2,1,0:T(8,128)(2,1)}), bf16[4,128,384]{2,1,0:T(8,128)(2,1)}, u32[]{:S(2)}, u32[]{:S(2)}) async-start(bf16[4,128,384]{2,1,0:T(8,128)(2,1)} %bitcast.61), calls=%async_computation.3 | async-start | bytes 786432 | tf_op jit(solution)/shard_map/all_to_all | solution.py:258
  124.0 23.5 %collective-permute-start.3 = (bf16[512,384]{1,0:T(8,128)(2,1)S(1)}, bf16[512,384]{1,0:T(8,128)(2,1)S(1)}, u32[]{:S(2)}, u32[]{:S(2)}) collective-permute-start(bf16[512,384]{1,0:T(8,128)(2,1)S(1)} %all_gather.16.refs_0_), channel_id=1, source_target_pairs={{0,2},{2,4},{4,6},{6,0},{1,3},{3,5},{5,7},{7,1},{8,10},{10,12},{12... | collective-permute-start | bytes 1179656 | tf_op jit(solution)/shard_map/ppermute | solution.py:37
  126.8 20.7 %collective-permute-start.4 = (bf16[512,384]{1,0:T(8,128)(2,1)S(1)}, bf16[512,384]{1,0:T(8,128)(2,1)}, u32[]{:S(2)}, u32[]{:S(2)}) collective-permute-start(bf16[512,384]{1,0:T(8,128)(2,1)S(1)} %all_gather.16.refs_0_), channel_id=1, source_target_pairs={{0,4},{2,6},{4,0},{6,2},{1,5},{3,7},{5,1},{7,3},{8,12},{10,14},{12... | collective-permute-start | bytes 1179656 | tf_op jit(solution)/shard_map/ppermute | solution.py:37
  131.3 16.8 %collective-permute-start.5 = (bf16[512,384]{1,0:T(8,128)(2,1)S(1)}, bf16[512,384]{1,0:T(8,128)(2,1)}, u32[]{:S(2)}, u32[]{:S(2)}) collective-permute-start(bf16[512,384]{1,0:T(8,128)(2,1)S(1)} %all_gather.16.refs_0_), channel_id=1, source_target_pairs={{0,6},{2,0},{4,2},{6,4},{1,7},{3,1},{5,3},{7,5},{8,14},{10,8},{12,... | collective-permute-start | bytes 1179656 | tf_op jit(solution)/shard_map/ppermute | solution.py:37
  144.3 1.5 copy-start.6
  144.3 1.6 copy-start.9
  147.5 6.5 %copy-start.7 = (f32[384,256]{1,0:T(8,128)S(1)}, f32[384,256]{1,0:T(8,128)}, u32[]{:S(2)}) copy-start(f32[384,256]{1,0:T(8,128)} %get-tuple-element.52) | copy-start | bytes 1179652
  150.6 3.3 %collective-permute-start.6 = (bf16[384,256]{1,0:T(8,128)(2,1)S(1)}, bf16[384,256]{1,0:T(8,128)(2,1)S(1)}, u32[]{:S(2)}, u32[]{:S(2)}) collective-permute-start(bf16[384,256]{1,0:T(8,128)(2,1)S(1)} %get-tuple-element.47), channel_id=1, source_target_pairs={{0,1},{1,0},{2,3},{3,2},{4,5},{5,4},{6,7},{7,6},{8,9},{9,8},{10,11... | collective-permute-start | bytes 589832 | tf_op jit(solution)/shard_map/ppermute | solution.py:37
Sparse Core Ops, SparseCore 0:
  18.7 56.8 all-gather.2
  114.0 46.7 all-gather.4
Sparse Core Ops, SparseCore 1:
  37.9 36.8 reduce-scatter.1

commit v11 on v10

--- a/solution.py
+++ b/solution.py
@@ -229,12 +229,12 @@
     attended, gated = lax.optimization_barrier((attended, gated))
     theirs = shift(gated, "core", NCORE, 1)
     both = jnp.concatenate([gated, theirs], axis=1)
-    gated_y = lax.all_gather(both, "y", axis=0, tiled=True)
     natural = attended
     attended = lax.all_to_all(attended, "y", split_axis=0, concat_axis=0, tiled=True)
 
     summed = upstream_part(place, weight, other, gated, theirs)
-    attended, summed = lax.optimization_barrier((attended, summed))
+    attended, summed, both = lax.optimization_barrier((attended, summed, both))
+    gated_y = lax.all_gather(both, "y", axis=0, tiled=True)
     summed = lax.psum_scatter(summed, "x", scatter_dimension=0, tiled=True)
 
     own = lax.all_gather(attended, "zhi", axis=0, tiled=True)

time: 173 us -> 175 us (1.012)
  waiting for transfers between devices: 24.8 us -> 27.5 us
  matrix products: 7.4 us -> 5.35 us
    all_to_all x1, waiting for transfers between devices: 0.01 us -> 4.54 us  [gather_x(): return lax.all_to_all(value, 'x', split_axis=0, concat_axis=0, tiled=True)]
    dot_general x6, matrix products: 5.47 us -> 3.41 us  [dot(): return lax.dot_general(a, b, (dims, ((), ())), preferred_element_type=F32)]
    ppermute x7, waiting for transfers between devices: 4.79 us -> 2.79 us  [shift(): lax.ppermute(value, axis, [(i, (i + step) % size) for i in range(size)])]
  transfers between devices with their start and end apart: 13 -> 13, of which waited for: 7 -> 7; matrix products, arithmetic and copies ran while one was open for 5% -> 7% of each run, Pallas kernels for 5% -> 5%
where the time goes in v11:
time: 175 us; the launch traced here: 174 us
  blocking collectives  60.7 us (35%)
  starting transfers between devices  40.9 us (23%)
  waiting for transfers between devices  27.5 us (16%)
  between operations  15.8 us (9%)
  Pallas kernels  11.9 us (7%)
  other arithmetic  6.11 us (3%)
  local copies, waits for them, and re-layouts  5.48 us (3%)
  matrix products  5.35 us (3%)
    all_gather x1, blocking collectives, on_device(): own = lax.all_gather(attended, 'zhi', axis=0, tiled=True)  26.4 us
    all_gather x1, blocking collectives, on_device(): whole = lax.all_gather(natural, 'zhi', axis=0, tiled=True)  18.6 us
    ppermute x7, starting transfers between devices, shift(): lax.ppermute(value, axis, [(i, (i + step) % size) for i in range(size)])  18.1 us
    all_gather x1, blocking collectives, on_device(): total = lax.all_gather(total, 'zlo', axis=0, tiled=True)  15.7 us
    all_to_all x1, starting transfers between devices, on_device(): lax.all_to_all(summed, 'zhi', split_axis=0, concat_axis=0, tiled=True)  10.8 us
    all_to_all x1, waiting for transfers between devices, on_device(): lax.all_to_all(summed, 'zhi', split_axis=0, concat_axis=0, tiled=True)  9.43 us
    all_to_all x1, starting transfers between devices, on_device(): lax.all_to_all(attended, 'y', split_axis=0, concat_axis=0, tiled=True)  7.12 us
    all_gather x1, waiting for transfers between devices, on_device(): total = lax.all_gather(total, 'y', axis=0, tiled=True)  6.67 us
  transfers between devices with their start and end apart: 13, of which 7 were waited for; matrix products, arithmetic and copies ran while one was open for 7% of the time, Pallas kernels for 5%

profile of v11, /device:TPU:2, one launch (start us, length us, event | category | flops | bytes accessed | tf_op | source)
XLA Modules:
  0.0 173.7 jit_solution(13774428161576660098)
XLA Ops:
  8.0 2.4 %dynamic-slice_bitcast_fusion = bf16[16,128,256]{2,1,0:T(8,128)(2,1)} fusion(bf16[16,2,128,256]{3,2,1,0:T(8,128)(2,1)} %bitcast.55, s32[]{:T(128)S(6)} %select_n.9), kind=kLoop, calls=%fused_computation.16 | loop fusion | bytes 2097156 | tf_op jit(solution)/shard_map/jit(dynamic_index_in_dim)/squeeze | solution.py:204
  10.4 2.0 %collective-permute-start = (bf16[16,128,256]{2,1,0:T(8,128)(2,1)}, bf16[16,128,256]{2,1,0:T(8,128)(2,1)}, u32[]{:S(2)}, u32[]{:S(2)}) collective-permute-start(bf16[16,128,256]{2,1,0:T(8,128)(2,1)} %dynamic-slice_bitcast_fusion), channel_id=1, source_target_pairs={{0,1},{1,0},{2,3},{3,2},{4,5},{5,4},{6,7},{7,6},{8,9},{9,8},{10,11... | collective-permute-start | bytes 3145736 | tf_op jit(solution)/shard_map/ppermute | solution.py:37
  13.2 0.9 fusion.3
  15.0 1.2 multiply_convert_fusion.2
  16.1 2.4 %collective-permute-start.1 = (bf16[384,256]{1,0:T(8,128)(2,1)S(1)}, bf16[384,256]{1,0:T(8,128)(2,1)S(1)}, u32[]{:S(2)}, u32[]{:S(2)}) collective-permute-start(bf16[384,256]{1,0:T(8,128)(2,1)S(1)} %get-tuple-element.33.gated), channel_id=1, source_target_pairs={{0,1},{1,0},{2,3},{3,2},{4,5},{5,4},{6,7},{7,6},{8,9},{9,8},{10,11... | collective-permute-start | bytes 589832 | tf_op jit(solution)/shard_map/ppermute | solution.py:37
  18.5 7.1 %all-to-all-start = ((bf16[8,16,384]{2,1,0:T(8,128)(2,1)}), bf16[8,16,384]{2,1,0:T(8,128)(2,1)S(1)}, u32[]{:S(2)}, u32[]{:S(2)}) async-start(bf16[8,16,384]{2,1,0:T(8,128)(2,1)} %bitcast.11), calls=%async_computation | async-start | bytes 196608 | tf_op jit(solution)/shard_map/all_to_all | solution.py:233
  25.8 0.8 pad_maximum_fusion.1
  26.6 3.2 %shard_map.139 = bf16[2048,384]{1,0:T(8,128)(2,1)S(1)} custom-call(s32[2]{0:T(128)S(1)} %pad_add_fusion.place, bf16[32,128,256]{2,1,0:T(8,128)(2,1)S(1)} %bitcast.56, bf16[16,128,256]{2,1,0:T(8,128)(2,1)} %collective-permute-done.other, bf16[384,256]{1,0:T(8,128)(2,1)S(1)} %get-tuple-element.33.gated, bf16[384,256]{1,0:T(8,128)(2,1)S(1)} %collective-permute-done.1.theirs), custom_call_target="tpu_custom_call" | custom-call | flops 805306368 | bytes 3145728 | tf_op jit(solution)/shard_map/pallas_call | solution.py:74
  29.8 1.1 copy-done.2
  30.9 3.5 %all-to-all-done = bf16[8,16,384]{2,1,0:T(8,128)(2,1)S(1)} async-done(((bf16[8,16,384]{2,1,0:T(8,128)(2,1)}), bf16[8,16,384]{2,1,0:T(8,128)(2,1)S(1)}, u32[]{:S(2)}, u32[]{:S(2)}) %all-to-all-start) | async-done | bytes 98336 | tf_op jit(solution)/shard_map/all_to_all | solution.py:233
  35.0 26.4 %all_gather.15 = bf16[512,384]{1,0:T(8,128)(2,1)S(1)} all-gather(bf16[128,384]{1,0:T(8,128)(2,1)S(1)} %bitcast.62), channel_id=1, replica_groups=mesh['zlo'=3,'y'=8,'zhi'=4,'x'=4,'core'=2] {'zhi'}, dimensions={0}, use_global_device_ids=true | all-gather | bytes 491520 | tf_op jit(solution)/shard_map/all_gather | solution.py:240
  61.4 1.3 pad_maximum_fusion
  62.7 4.8 %all-to-all-start.1 = ((bf16[4,512,384]{2,1,0:T(8,128)(2,1)}), bf16[4,512,384]{2,1,0:T(8,128)(2,1)}, u32[]{:S(2)}, u32[]{:S(2)}) async-start(bf16[4,512,384]{2,1,0:T(8,128)(2,1)} %bitcast.58), calls=%async_computation.1 | async-start | bytes 3145728 | tf_op jit(solution)/shard_map/all_to_all | solution.py:41
  67.5 18.6 %all_gather.16.refs_0_ = bf16[512,384]{1,0:T(8,128)(2,1)S(1)} all-gather(bf16[128,384]{1,0:T(8,128)(2,1)} %fusion.3), channel_id=1, replica_groups=mesh['zlo'=3,'y'=8,'zhi'=4,'x'=4,'core'=2] {'zhi'}, dimensions={0}, use_global_device_ids=true | all-gather | bytes 491520 | tf_op jit(solution)/shard_map/all_gather | solution.py:244
  86.1 4.5 %all-to-all-done.1 = bf16[4,512,384]{2,1,0:T(8,128)(2,1)} async-done(((bf16[4,512,384]{2,1,0:T(8,128)(2,1)}), bf16[4,512,384]{2,1,0:T(8,128)(2,1)}, u32[]{:S(2)}, u32[]{:S(2)}) %all-to-all-start.1) | async-done | bytes 1572896 | tf_op jit(solution)/shard_map/all_to_all | solution.py:41
  90.7 1.9 %copy-done.3 = bf16[3072,512]{1,0:T(8,128)(2,1)S(1)} copy-done((bf16[3072,512]{1,0:T(8,128)(2,1)S(1)}, bf16[3072,512]{1,0:T(8,128)(2,1)}, u32[]{:S(2)}) %copy-start.3) | copy-done | bytes 3145752
  92.6 2.4 %shard_map.140 = (bf16[256,256]{1,0:T(8,128)(2,1)S(1)}, bf16[256,256]{1,0:T(8,128)(2,1)S(1)}) custom-call(bf16[2048,384]{1,0:T(8,128)(2,1)} %bitcast.14.held, bf16[3072,512]{1,0:T(8,128)(2,1)S(1)} %copy-done.3), custom_call_target="tpu_custom_call" | custom-call | flops 805306368 | bytes 4718592 | tf_op jit(solution)/shard_map/pallas_call | solution.py:102
  95.0 1.9 %collective-permute-start.2 = (bf16[256,256]{1,0:T(8,128)(2,1)S(1)}, bf16[256,256]{1,0:T(8,128)(2,1)S(1)}, u32[]{:S(2)}, u32[]{:S(2)}) collective-permute-start(bf16[256,256]{1,0:T(8,128)(2,1)S(1)} %get-tuple-element.40), channel_id=1, source_target_pairs={{0,1},{1,0},{2,3},{3,2},{4,5},{5,4},{6,7},{7,6},{8,9},{9,8},{10,11... | collective-permute-start | bytes 393224 | tf_op jit(solution)/shard_map/ppermute | solution.py:37
  96.9 1.3 collective-permute-done.2
  98.2 15.7 %all_gather.18 = bf16[1536,256]{1,0:T(8,128)(2,1)S(1)} all-gather(bf16[512,256]{1,0:T(8,128)(2,1)S(1)} %pad_maximum_fusion.3), channel_id=1, replica_groups=mesh['zlo'=3,'y'=8,'zhi'=4,'x'=4,'core'=2] {'zlo'}, dimensions={0}, use_global_device_ids=true | all-gather | bytes 1048576 | tf_op jit(solution)/shard_map/all_gather | solution.py:250
  114.8 10.8 %all-to-all-start.2 = ((bf16[4,128,384]{2,1,0:T(8,128)(2,1)}), bf16[4,128,384]{2,1,0:T(8,128)(2,1)}, u32[]{:S(2)}, u32[]{:S(2)}) async-start(bf16[4,128,384]{2,1,0:T(8,128)(2,1)} %bitcast.61), calls=%async_computation.3 | async-start | bytes 786432 | tf_op jit(solution)/shard_map/all_to_all | solution.py:258
  125.6 1.9 %collective-permute-start.3 = (bf16[512,384]{1,0:T(8,128)(2,1)S(1)}, bf16[512,384]{1,0:T(8,128)(2,1)S(1)}, u32[]{:S(2)}, u32[]{:S(2)}) collective-permute-start(bf16[512,384]{1,0:T(8,128)(2,1)S(1)} %all_gather.16.refs_0_), channel_id=1, source_target_pairs={{0,2},{2,4},{4,6},{6,0},{1,3},{3,5},{5,7},{7,1},{8,10},{10,12},{12... | collective-permute-start | bytes 1179656 | tf_op jit(solution)/shard_map/ppermute | solution.py:37
  127.5 5.4 %collective-permute-start.4 = (bf16[512,384]{1,0:T(8,128)(2,1)S(1)}, bf16[512,384]{1,0:T(8,128)(2,1)}, u32[]{:S(2)}, u32[]{:S(2)}) collective-permute-start(bf16[512,384]{1,0:T(8,128)(2,1)S(1)} %all_gather.16.refs_0_), channel_id=1, source_target_pairs={{0,4},{2,6},{4,0},{6,2},{1,5},{3,7},{5,1},{7,3},{8,12},{10,14},{12... | collective-permute-start | bytes 1179656 | tf_op jit(solution)/shard_map/ppermute | solution.py:37
  132.9 2.5 %collective-permute-start.5 = (bf16[512,384]{1,0:T(8,128)(2,1)S(1)}, bf16[512,384]{1,0:T(8,128)(2,1)}, u32[]{:S(2)}, u32[]{:S(2)}) collective-permute-start(bf16[512,384]{1,0:T(8,128)(2,1)S(1)} %all_gather.16.refs_0_), channel_id=1, source_target_pairs={{0,6},{2,0},{4,2},{6,4},{1,7},{3,1},{5,3},{7,5},{8,14},{10,8},{12,... | collective-permute-start | bytes 1179656 | tf_op jit(solution)/shard_map/ppermute | solution.py:37
  135.4 9.4 %all-to-all-done.2 = bf16[4,128,384]{2,1,0:T(8,128)(2,1)} async-done(((bf16[4,128,384]{2,1,0:T(8,128)(2,1)}), bf16[4,128,384]{2,1,0:T(8,128)(2,1)}, u32[]{:S(2)}, u32[]{:S(2)}) %all-to-all-start.2) | async-done | bytes 393248 | tf_op jit(solution)/shard_map/all_to_all | solution.py:258
  144.9 1.1 reduce_sum.41
  145.9 1.4 multiply_reduce_fusion
  149.2 2.5 %shard_map.141 = (f32[384,256]{1,0:T(8,128)S(1)}, bf16[384,256]{1,0:T(8,128)(2,1)S(1)}) custom-call(s32[2]{0:T(128)S(1)} %pad_add_fusion.place, bf16[32,128,256]{2,1,0:T(8,128)(2,1)S(1)} %bitcast.57, bf16[16,128,256]{2,1,0:T(8,128)(2,1)} %collective-permute-done.other, bf16[512,384]{1,0:T(8,128)(2,1)S(1)} %all_gather.16.refs_0_, ...), custom_call_target="tpu_custom_call" | custom-call | flops 805306368 | bytes 3670016 | tf_op jit(solution)/shard_map/pallas_call | solution.py:131
  151.7 1.9 %collective-permute-start.6 = (bf16[384,256]{1,0:T(8,128)(2,1)S(1)}, bf16[384,256]{1,0:T(8,128)(2,1)S(1)}, u32[]{:S(2)}, u32[]{:S(2)}) collective-permute-start(bf16[384,256]{1,0:T(8,128)(2,1)S(1)} %get-tuple-element.49), channel_id=1, source_target_pairs={{0,1},{1,0},{2,3},{3,2},{4,5},{5,4},{6,7},{7,6},{8,9},{9,8},{10,11... | collective-permute-start | bytes 589832 | tf_op jit(solution)/shard_map/ppermute | solution.py:37
  153.6 1.4 collective-permute-done.6
  155.8 6.7 %all-gather.5.cloned.1.call-done = bf16[4096,256]{1,0:T(8,128)(2,1)} async-done(((bf16[512,256]{1,0:T(8,128)(2,1)}), bf16[4096,256]{1,0:T(8,128)(2,1)}) %all-gather.5.cloned.1.call-update) | async-done | bytes 2097168 | tf_op jit(solution)/shard_map/all_gather | solution.py:255
  162.4 3.8 %shard_map.142 = bf16[32,128,256]{2,1,0:T(8,128)(2,1)} custom-call(s32[2]{0:T(128)} %copy-done.4, bf16[8,512,256]{2,1,0:T(8,128)(2,1)} %bitcast.59), custom_call_target="tpu_custom_call" | custom-call | bytes 4194304 | tf_op jit(solution)/shard_map/pallas_call | solution.py:166
  (66 shorter events, 5.6 us)
Async XLA Ops:
  8.0 6.2 %copy-start = (bf16[1000,256]{1,0:T(8,128)(2,1)S(1)}, bf16[1000,256]{1,0:T(8,128)(2,1)}, u32[]{:S(2)}) copy-start(bf16[1000,256]{1,0:T(8,128)(2,1)} %param.20) | copy-start | bytes 1536004
  8.0 4.4 %copy-start.15 = (s32[8]{0:T(128)S(1)}, s32[8]{0:T(128)}, u32[]{:S(2)}) copy-start(s32[8]{0:T(128)} %param.15) | copy-start | bytes 100
  8.0 4.7 %copy-start.9 = (bf16[384,3,128]{2,0,1:T(8,128)(2,1)S(1)}, bf16[384,3,128]{2,0,1:T(8,128)(2,1)}, u32[]{:S(2)}) copy-start(bf16[384,3,128]{2,0,1:T(8,128)(2,1)} %param.12) | copy-start | bytes 884740
  10.4 3.8 %copy-start.11 = (s32[8]{0:T(128)S(1)}, s32[8]{0:T(128)}, u32[]{:S(2)}) copy-start(s32[8]{0:T(128)} %param.19) | copy-start | bytes 100
  10.4 16.2 %collective-permute-start = (bf16[16,128,256]{2,1,0:T(8,128)(2,1)}, bf16[16,128,256]{2,1,0:T(8,128)(2,1)}, u32[]{:S(2)}, u32[]{:S(2)}) collective-permute-start(bf16[16,128,256]{2,1,0:T(8,128)(2,1)} %dynamic-slice_bitcast_fusion), channel_id=1, source_target_pairs={{0,1},{1,0},{2,3},{3,2},{4,5},{5,4},{6,7},{7,6},{8,9},{9,8},{10,11... | collective-permute-start | bytes 3145736 | tf_op jit(solution)/shard_map/ppermute | solution.py:37
  12.7 1.6 copy-start.12
  12.7 1.6 copy-start.16
  12.8 1.8 %copy-start.13 = (bf16[8,256]{1,0:T(8,128)(2,1)S(1)}, bf16[8,256]{1,0:T(8,128)(2,1)}, u32[]{:S(2)}) copy-start(bf16[8,256]{1,0:T(8,128)(2,1)} %param.22) | copy-start | bytes 12292
  12.8 1.8 %copy-start.17 = (s32[8]{0:T(128)S(1)}, s32[8]{0:T(128)}, u32[]{:S(2)}) copy-start(s32[8]{0:T(128)} %param.17) | copy-start | bytes 100
  13.1 3.1 %copy-start.5 = (f32[384,384]{0,1:T(8,128)}, f32[384,384]{0,1:T(8,128)S(1)}, u32[]{:S(2)}) copy-start(f32[384,384]{0,1:T(8,128)S(1)} %get-tuple-element.52) | copy-start | bytes 1769476
  13.1 1.7 copy-start.14
  13.1 1.7 copy-start.18
  13.1 1.9 %copy-start.8 = (bf16[384,256]{1,0:T(8,128)(2,1)S(1)}, bf16[384,256]{1,0:T(8,128)(2,1)}, u32[]{:S(2)}) copy-start(bf16[384,256]{1,0:T(8,128)(2,1)} %param.14) | copy-start | bytes 589828
  13.2 13.3 %copy-start.1 = (bf16[4096,256]{1,0:T(8,128)(2,1)S(1)}, bf16[4096,256]{1,0:T(8,128)(2,1)}, u32[]{:S(2)}) copy-start(bf16[4096,256]{1,0:T(8,128)(2,1)} %param.13) | copy-start | bytes 6291460
  16.1 9.6 %collective-permute-start.1 = (bf16[384,256]{1,0:T(8,128)(2,1)S(1)}, bf16[384,256]{1,0:T(8,128)(2,1)S(1)}, u32[]{:S(2)}, u32[]{:S(2)}) collective-permute-start(bf16[384,256]{1,0:T(8,128)(2,1)S(1)} %get-tuple-element.33.gated), channel_id=1, source_target_pairs={{0,1},{1,0},{2,3},{3,2},{4,5},{5,4},{6,7},{7,6},{8,9},{9,8},{10,11... | collective-permute-start | bytes 589832 | tf_op jit(solution)/shard_map/ppermute | solution.py:37
  18.5 15.8 %all-to-all-start = ((bf16[8,16,384]{2,1,0:T(8,128)(2,1)}), bf16[8,16,384]{2,1,0:T(8,128)(2,1)S(1)}, u32[]{:S(2)}, u32[]{:S(2)}) async-start(bf16[8,16,384]{2,1,0:T(8,128)(2,1)} %bitcast.11), calls=%async_computation | async-start | bytes 196608 | tf_op jit(solution)/shard_map/all_to_all | solution.py:233
  25.6 65.0 %all-gather.3.cloned.1.call-start = ((), (), s32[]{:S(2)}) async-start(), calls=%async_computation.4 | async-start | bytes 3538944 | tf_op jit(solution)/shard_map/all_gather | solution.py:237
  25.8 123.4 %copy-start.4 = (s32[2]{0:T(128)}, s32[2]{0:T(128)S(1)}, u32[]{:S(2)}) copy-start(s32[2]{0:T(128)S(1)} %pad_add_fusion.place) | copy-start | bytes 28
  29.7 1.1 copy-start.2
  34.4 80.4 %reduce-scatter.2.cloned.1.call-start = ((), (), s32[]{:S(2)}) async-start(), calls=%async_computation.5 | async-start | bytes 1966080 | tf_op jit(solution)/shard_map/reduce_scatter | solution.py:238
  62.7 28.0 %all-to-all-start.1 = ((bf16[4,512,384]{2,1,0:T(8,128)(2,1)}), bf16[4,512,384]{2,1,0:T(8,128)(2,1)}, u32[]{:S(2)}, u32[]{:S(2)}) async-start(bf16[4,512,384]{2,1,0:T(8,128)(2,1)} %bitcast.58), calls=%async_computation.1 | async-start | bytes 3145728 | tf_op jit(solution)/shard_map/all_to_all | solution.py:41
  67.5 94.9 %all-gather.5.cloned.1.call-start = ((), (), s32[]{:S(2)}) async-start(), calls=%async_computation.6 | async-start | bytes 2359296 | tf_op jit(solution)/shard_map/all_gather | solution.py:255
  90.7 1.9 %copy-start.3 = (bf16[3072,512]{1,0:T(8,128)(2,1)S(1)}, bf16[3072,512]{1,0:T(8,128)(2,1)}, u32[]{:S(2)}) copy-start(bf16[3072,512]{1,0:T(8,128)(2,1)} %all-gather.3.cloned.1.call-done.gated) | copy-start | bytes 9437188
  95.0 3.2 %collective-permute-start.2 = (bf16[256,256]{1,0:T(8,128)(2,1)S(1)}, bf16[256,256]{1,0:T(8,128)(2,1)S(1)}, u32[]{:S(2)}, u32[]{:S(2)}) collective-permute-start(bf16[256,256]{1,0:T(8,128)(2,1)S(1)} %get-tuple-element.40), channel_id=1, source_target_pairs={{0,1},{1,0},{2,3},{3,2},{4,5},{5,4},{6,7},{7,6},{8,9},{9,8},{10,11... | collective-permute-start | bytes 393224 | tf_op jit(solution)/shard_map/ppermute | solution.py:37
  114.8 30.1 %all-to-all-start.2 = ((bf16[4,128,384]{2,1,0:T(8,128)(2,1)}), bf16[4,128,384]{2,1,0:T(8,128)(2,1)}, u32[]{:S(2)}, u32[]{:S(2)}) async-start(bf16[4,128,384]{2,1,0:T(8,128)(2,1)} %bitcast.61), calls=%async_computation.3 | async-start | bytes 786432 | tf_op jit(solution)/shard_map/all_to_all | solution.py:258
  125.6 23.5 %collective-permute-start.3 = (bf16[512,384]{1,0:T(8,128)(2,1)S(1)}, bf16[512,384]{1,0:T(8,128)(2,1)S(1)}, u32[]{:S(2)}, u32[]{:S(2)}) collective-permute-start(bf16[512,384]{1,0:T(8,128)(2,1)S(1)} %all_gather.16.refs_0_), channel_id=1, source_target_pairs={{0,2},{2,4},{4,6},{6,0},{1,3},{3,5},{5,7},{7,1},{8,10},{10,12},{12... | collective-permute-start | bytes 1179656 | tf_op jit(solution)/shard_map/ppermute | solution.py:37
  127.5 21.6 %collective-permute-start.4 = (bf16[512,384]{1,0:T(8,128)(2,1)S(1)}, bf16[512,384]{1,0:T(8,128)(2,1)}, u32[]{:S(2)}, u32[]{:S(2)}) collective-permute-start(bf16[512,384]{1,0:T(8,128)(2,1)S(1)} %all_gather.16.refs_0_), channel_id=1, source_target_pairs={{0,4},{2,6},{4,0},{6,2},{1,5},{3,7},{5,1},{7,3},{8,12},{10,14},{12... | collective-permute-start | bytes 1179656 | tf_op jit(solution)/shard_map/ppermute | solution.py:37
  132.9 16.2 %collective-permute-start.5 = (bf16[512,384]{1,0:T(8,128)(2,1)S(1)}, bf16[512,384]{1,0:T(8,128)(2,1)}, u32[]{:S(2)}, u32[]{:S(2)}) collective-permute-start(bf16[512,384]{1,0:T(8,128)(2,1)S(1)} %all_gather.16.refs_0_), channel_id=1, source_target_pairs={{0,6},{2,0},{4,2},{6,4},{1,7},{3,1},{5,3},{7,5},{8,14},{10,8},{12,... | collective-permute-start | bytes 1179656 | tf_op jit(solution)/shard_map/ppermute | solution.py:37
  145.9 1.5 copy-start.6
  145.9 1.6 copy-start.10
  149.1 5.9 %copy-start.7 = (f32[384,256]{1,0:T(8,128)S(1)}, f32[384,256]{1,0:T(8,128)}, u32[]{:S(2)}) copy-start(f32[384,256]{1,0:T(8,128)} %get-tuple-element.54) | copy-start | bytes 1179652
  151.7 3.3 %collective-permute-start.6 = (bf16[384,256]{1,0:T(8,128)(2,1)S(1)}, bf16[384,256]{1,0:T(8,128)(2,1)S(1)}, u32[]{:S(2)}, u32[]{:S(2)}) collective-permute-start(bf16[384,256]{1,0:T(8,128)(2,1)S(1)} %get-tuple-element.49), channel_id=1, source_target_pairs={{0,1},{1,0},{2,3},{3,2},{4,5},{5,4},{6,7},{7,6},{8,9},{9,8},{10,11... | collective-permute-start | bytes 589832 | tf_op jit(solution)/shard_map/ppermute | solution.py:37
Sparse Core Ops, SparseCore 0:
  34.5 53.4 all-gather.2
  114.9 47.5 all-gather.4
Sparse Core Ops, SparseCore 1:
  38.6 42.5 reduce-scatter.1
